TPU v7x, 32 devices: a whole 2x2x4 slice. The times are simulated.
32 devices in a mesh: dp: 32 (over z, y, x, core).
Axes of the slice: x: 2, y: 2, z: 4, core: 2. Of those that a mesh axis runs over, the one named last changes fastest.
Arguments:
- x_in: bfloat16 [131072, 512], P('dp'), may hold values from -6 to 6
- grad_out: bfloat16 [131072, 512], P('dp'), may hold values from -6 to 6
- seq_lengths: int32 [32, 4], P('dp'), may hold values from 0 to 4096, as said below
- partners: int32 [32, 128], P('dp'), may hold values from 0 to 127, as said below
- w_qkv: float32 [512, 1536], P('dp'), may hold values from -0.25 to 0.25
- w_attn_out: float32 [512, 512], P('dp'), may hold values from -1 to 1
- w_sort: float32 [512, 128], P('dp'), may hold values from -0.25 to 0.25
- w_ffn_in: float32 [512, 2048], P('dp'), may hold values from -0.25 to 0.25
- w_ffn_out: float32 [2048, 512], P('dp'), may hold values from -0.125 to 0.125
- norm_params: float32 [512, 4], P('dp')
- moment_qkv: float32 [512, 1536], P('dp'), may hold values from -112 to 112
- moment_attn_out: float32 [512, 512], P('dp'), may hold values from -80 to 80
- moment_sort: float32 [512, 128], P('dp'), may hold values from -40 to 40
- moment_ffn_in: float32 [512, 2048], P('dp'), may hold values from -64 to 64
- moment_ffn_out: float32 [2048, 512], P('dp'), may hold values from -112 to 112
- moment_norms: float32 [512, 4], P('dp'), may hold values from -224 to 224
- square_qkv: float32 [512, 1536], P('dp'), may hold values from 32.768 to 131.072
- square_attn_out: float32 [512, 512], P('dp'), may hold values from 15.72864 to 62.91456
- square_sort: float32 [512, 128], P('dp'), may hold values from 5.24288 to 20.97152
- square_ffn_in: float32 [512, 2048], P('dp'), may hold values from 11.79648 to 47.18592
- square_ffn_out: float32 [2048, 512], P('dp'), may hold values from 32.768 to 131.072
- square_norms: float32 [512, 4], P('dp'), may hold values from 131.072 to 524.288
Outputs:
- out_block: bfloat16 [131072, 512], P('dp')
- grad_in: float32 [131072, 512], P('dp')
- new_w_qkv: float32 [512, 1536], P('dp')
- new_moment_qkv: float32 [512, 1536], P('dp')
- new_square_qkv: float32 [512, 1536], P('dp')
- new_w_attn_out: float32 [512, 512], P('dp')
- new_moment_attn_out: float32 [512, 512], P('dp')
- new_square_attn_out: float32 [512, 512], P('dp')
- new_w_sort: float32 [512, 128], P('dp')
- new_moment_sort: float32 [512, 128], P('dp')
- new_square_sort: float32 [512, 128], P('dp')
- new_w_ffn_in: float32 [512, 2048], P('dp')
- new_moment_ffn_in: float32 [512, 2048], P('dp')
- new_square_ffn_in: float32 [512, 2048], P('dp')
- new_w_ffn_out: float32 [2048, 512], P('dp')
- new_moment_ffn_out: float32 [2048, 512], P('dp')
- new_square_ffn_out: float32 [2048, 512], P('dp')
- new_norm_params: float32 [512, 4], P('dp')
- new_moment_norms: float32 [512, 4], P('dp')
- new_square_norms: float32 [512, 4], P('dp')
Inputs may be any that keep to these rules, and one draw needn't show every extreme that they name: `seq_lengths`: row r either holds one sequence of more than 1024 tokens from the row's start, its other three entries being 0, or four sequences, the k-th starting at position k * 1024 and holding 4096 // 8 to 1024 tokens. Some row holds one sequence of exactly 4096 tokens. `partners`: entry (r, b) names a block of row r: for a live block, a live block of the same sequence; for any other block, b itself.
All inputs are finite; a program needn't handle non-finite values.
Results may differ from a plain program's by a relative error of at most 0.013.
The roundings to bfloat16 on the way count: a program that leaves them out, or rounds other values in their place, can miss the bound.
Values may be sent and summed in bfloat16 or wider, within the bound.
No kernel may reach another device: no remote copies, remote signals or barrier semaphores. Data moves between devices by JAX's collectives and lax.ppermute only.
A program may use at most 448 MiB of HBM per device.

v0:
```python
import math

import jax
import jax.numpy as jnp
from jax import lax
from jax.sharding import PartitionSpec as P

HEADS = 8
HEAD = 64
SORT = 64
BLOCK = 32
SINK = 8
STEP = 10


highest = lax.Precision.HIGHEST
blockwise = lax.Precision.HIGH
masked = -1000000000.0
norm_eps = 1e-05
beta_one = 0.9
beta_two = 0.999
adam_eps = 1e-08
decay = 0.01
rates = (0.05, 0.15, 0.05, 0.05, 0.025, 0.5)


def matmul(left, right):
    return jnp.dot(left, right, precision=highest, preferred_element_type=jnp.float32)


def inner_left(left, right):
    return lax.dot_general(
        left, right, (((0,), (0,)), ((), ())), preferred_element_type=jnp.float32
    )


def inner_right(left, right):
    return lax.dot_general(
        left, right, (((1,), (1,)), ((), ())), preferred_element_type=jnp.float32
    )


def layer_norm(value, gain, shift):
    center = value - jnp.mean(value, axis=-1, keepdims=True)
    spread = jnp.mean(center * center, axis=-1, keepdims=True)
    return center * lax.rsqrt(spread + norm_eps) * gain + shift


def slot_layout(lengths, slot):
    quarter = slot // 4
    places = jnp.arange(slot, dtype=jnp.int32)
    is_long = lengths[0] > quarter
    member = jnp.where(is_long, 0, places // quarter)
    offset = jnp.where(is_long, places, places % quarter)
    choose = (member[:, None] == jnp.arange(4, dtype=jnp.int32)[None, :]).astype(jnp.int32)
    limit = jnp.sum(choose * lengths[None, :], axis=1)
    live = offset < limit
    blocks = slot // BLOCK
    group = jnp.where(live[::BLOCK], member[::BLOCK], 4 + jnp.arange(blocks, dtype=jnp.int32))
    return (live.astype(jnp.float32), group)


def sorted_attention(query, key, value, normed, sort_w, live, group, partner):
    slot, width = query.shape
    blocks = slot // BLOCK
    counts = jnp.sum(live.reshape(blocks, BLOCK), axis=1)
    summary = jnp.sum((normed * live[:, None]).reshape(blocks, BLOCK, width), axis=1)
    summary = summary * lax.rsqrt(jnp.maximum(counts, 1.0))[:, None]
    sort_q = matmul(summary, sort_w[:, :SORT])
    sort_k = matmul(summary, sort_w[:, SORT:])
    same = group[:, None] == group[None, :]
    raw = lax.dot_general(
        sort_q,
        sort_k,
        (((1,), (1,)), ((), ())),
        precision=highest,
        preferred_element_type=jnp.float32,
    )
    logits = jnp.where(same, raw / math.sqrt(SORT), masked)
    for turn in range(SINK):
        logits = logits - jax.nn.logsumexp(logits, axis=1, keepdims=True)
        logits = logits - jax.nn.logsumexp(logits, axis=0, keepdims=True)
    members = jnp.sum(same.astype(jnp.float32), axis=1)
    pick = partner[:, None] == jnp.arange(blocks, dtype=jnp.int32)[None, :]
    bias = jnp.sum(jnp.where(pick, logits, 0.0), axis=1) + jnp.log(members)
    shaped = (blocks, BLOCK, HEADS, HEAD)
    q_blocks = query.reshape(shaped)
    k_blocks = key.reshape(shaped)
    v_blocks = value.reshape(shaped)
    k_far = jnp.take(k_blocks, partner, axis=0)
    v_far = jnp.take(v_blocks, partner, axis=0)
    live_own = live.reshape(blocks, BLOCK)
    live_far = jnp.take(live_own, partner, axis=0)
    scale = 1.0 / math.sqrt(HEAD)
    own = jnp.einsum("bqhd,bkhd->bhqk", q_blocks, k_blocks, precision=blockwise) * scale
    far = (
        jnp.einsum("bqhd,bkhd->bhqk", q_blocks, k_far, precision=blockwise) * scale
        + bias[:, None, None, None]
    )
    diagonal = jnp.eye(BLOCK, dtype=bool)
    own = jnp.where((live_own[:, None, None, :] > 0.5) | diagonal[None, None], own, masked)
    far = jnp.where(live_far[:, None, None, :] > 0.5, far, masked)
    scores = jnp.concatenate([own, far], axis=3)
    top = jnp.max(scores, axis=3, keepdims=True)
    expo = jnp.exp(scores - top)
    probs = expo / jnp.sum(expo, axis=3, keepdims=True)
    mixed = jnp.einsum("bhqk,bkhd->bqhd", probs[..., :BLOCK], v_blocks, precision=blockwise)
    mixed = mixed + jnp.einsum("bhqk,bkhd->bqhd", probs[..., BLOCK:], v_far, precision=blockwise)
    return mixed.reshape(slot, width)


def adamw(weight, grad, moment, square, rate):
    moment = beta_one * moment + (1.0 - beta_one) * grad
    square = beta_two * square + (1.0 - beta_two) * grad * grad
    m_hat = moment / (1.0 - beta_one**STEP)
    s_hat = square / (1.0 - beta_two**STEP)
    weight = weight - rate * (m_hat / (jnp.sqrt(s_hat) + adam_eps) + decay * weight)
    return (weight, moment, square)


def body(
    x_in,
    grad_out,
    seq_lengths,
    partners,
    w_qkv,
    w_attn_out,
    w_sort,
    w_ffn_in,
    w_ffn_out,
    norm_params,
    moment_qkv,
    moment_attn_out,
    moment_sort,
    moment_ffn_in,
    moment_ffn_out,
    moment_norms,
    square_qkv,
    square_attn_out,
    square_sort,
    square_ffn_in,
    square_ffn_out,
    square_norms,
):
    masters = (w_qkv, w_attn_out, w_sort, w_ffn_in, w_ffn_out, norm_params)
    shards = tuple((p.astype(jnp.bfloat16) for p in masters))
    full_qkv, full_attn, full_sort, full_in, full_out, full_norms = (
        lax.all_gather(shards[0], "dp", axis=0, tiled=True),
        lax.all_gather(shards[1], "dp", axis=0, tiled=True),
        lax.all_gather(shards[2], "dp", axis=0, tiled=True),
        lax.all_gather(shards[3], "dp", axis=0, tiled=True),
        lax.all_gather(shards[4], "dp", axis=0, tiled=True),
        lax.all_gather(shards[5], "dp", axis=0, tiled=True),
    )
    width = x_in.shape[1]
    live, group = slot_layout(seq_lengths[0], x_in.shape[0])
    partner = partners[0]
    norms_f = full_norms.astype(jnp.float32)
    x_f = x_in.astype(jnp.float32)
    h_one_f, norm_one_pull = jax.vjp(
        lambda value, params: layer_norm(value, params[:, 0], params[:, 1]), x_f, norms_f
    )
    h_one = h_one_f.astype(jnp.bfloat16)
    qkv = jnp.dot(h_one, full_qkv, preferred_element_type=jnp.float32).astype(jnp.bfloat16)
    qkv_f = qkv.astype(jnp.float32)

    def attend(query, key, value, normed, sort_w):
        return sorted_attention(query, key, value, normed, sort_w, live, group, partner)

    attended_f, attend_pull = jax.vjp(
        attend,
        qkv_f[:, :width],
        qkv_f[:, width : 2 * width],
        qkv_f[:, 2 * width :],
        h_one.astype(jnp.float32),
        full_sort.astype(jnp.float32),
    )
    attended = attended_f.astype(jnp.bfloat16)
    x_one = x_f + jnp.dot(attended, full_attn, preferred_element_type=jnp.float32)
    h_two_f, norm_two_pull = jax.vjp(
        lambda value, params: layer_norm(value, params[:, 2], params[:, 3]), x_one, norms_f
    )
    h_two = h_two_f.astype(jnp.bfloat16)
    act = jnp.dot(h_two, full_in, preferred_element_type=jnp.float32)
    hidden_f, gelu_pull = jax.vjp(lambda a: jax.nn.gelu(a, approximate=True), act)
    hidden = hidden_f.astype(jnp.bfloat16)
    out_block = (x_one + jnp.dot(hidden, full_out, preferred_element_type=jnp.float32)).astype(
        jnp.bfloat16
    )
    back_qkv, back_attn, back_sort, back_in, back_out, back_norms = (
        lax.all_gather(shards[0], "dp", axis=0, tiled=True),
        lax.all_gather(shards[1], "dp", axis=0, tiled=True),
        lax.all_gather(shards[2], "dp", axis=0, tiled=True),
        lax.all_gather(shards[3], "dp", axis=0, tiled=True),
        lax.all_gather(shards[4], "dp", axis=0, tiled=True),
        lax.all_gather(shards[5], "dp", axis=0, tiled=True),
    )
    grad_ffn_out = inner_left(hidden, grad_out)
    d_hidden = inner_right(grad_out, back_out)
    (d_act,) = gelu_pull(d_hidden)
    d_act = d_act.astype(jnp.bfloat16)
    grad_ffn_in = inner_left(h_two, d_act)
    d_h_two = inner_right(d_act, back_in)
    d_x_norm, grad_norm_two = norm_two_pull(d_h_two)
    d_x_one = grad_out.astype(jnp.float32) + d_x_norm
    d_z = d_x_one.astype(jnp.bfloat16)
    grad_attn_out = inner_left(attended, d_z)
    d_attended = inner_right(d_z, back_attn)
    d_query, d_key, d_value, d_normed, grad_sort = attend_pull(d_attended)
    d_qkv = jnp.concatenate([d_query, d_key, d_value], axis=1).astype(jnp.bfloat16)
    grad_qkv = inner_left(h_one, d_qkv)
    d_h_one = inner_right(d_qkv, back_qkv) + d_normed
    d_x_first, grad_norm_one = norm_one_pull(d_h_one)
    grad_in = d_x_one + d_x_first
    grad_norms = grad_norm_one + grad_norm_two
    summed_qkv, summed_attn, summed_sort, summed_in, summed_out, summed_norms = (
        lax.psum_scatter(grad_qkv, "dp", scatter_dimension=0, tiled=True),
        lax.psum_scatter(grad_attn_out, "dp", scatter_dimension=0, tiled=True),
        lax.psum_scatter(grad_sort, "dp", scatter_dimension=0, tiled=True),
        lax.psum_scatter(grad_ffn_in, "dp", scatter_dimension=0, tiled=True),
        lax.psum_scatter(grad_ffn_out, "dp", scatter_dimension=0, tiled=True),
        lax.psum_scatter(grad_norms, "dp", scatter_dimension=0, tiled=True),
    )
    grads = (summed_qkv, summed_attn, summed_sort, summed_in, summed_out, summed_norms)
    moments = (
        moment_qkv,
        moment_attn_out,
        moment_sort,
        moment_ffn_in,
        moment_ffn_out,
        moment_norms,
    )
    squares = (
        square_qkv,
        square_attn_out,
        square_sort,
        square_ffn_in,
        square_ffn_out,
        square_norms,
    )
    new = [adamw(masters[i], grads[i], moments[i], squares[i], rates[i]) for i in range(6)]
    return (
        out_block,
        grad_in,
        new[0][0],
        new[0][1],
        new[0][2],
        new[1][0],
        new[1][1],
        new[1][2],
        new[2][0],
        new[2][1],
        new[2][2],
        new[3][0],
        new[3][1],
        new[3][2],
        new[4][0],
        new[4][1],
        new[4][2],
        new[5][0],
        new[5][1],
        new[5][2],
    )


def solution(mesh):
    in_specs = (
        P("dp", None),
        P("dp", None),
        P("dp", None),
        P("dp", None),
        P("dp", None),
        P("dp", None),
        P("dp", None),
        P("dp", None),
        P("dp", None),
        P("dp", None),
        P("dp", None),
        P("dp", None),
        P("dp", None),
        P("dp", None),
        P("dp", None),
        P("dp", None),
        P("dp", None),
        P("dp", None),
        P("dp", None),
        P("dp", None),
        P("dp", None),
        P("dp", None),
    )
    out_specs = (
        P("dp", None),
        P("dp", None),
        P("dp", None),
        P("dp", None),
        P("dp", None),
        P("dp", None),
        P("dp", None),
        P("dp", None),
        P("dp", None),
        P("dp", None),
        P("dp", None),
        P("dp", None),
        P("dp", None),
        P("dp", None),
        P("dp", None),
        P("dp", None),
        P("dp", None),
        P("dp", None),
        P("dp", None),
        P("dp", None),
    )
    return jax.shard_map(body, mesh=mesh, in_specs=in_specs, out_specs=out_specs, check_vma=False)
```

profile of v0, /device:TPU:0, one launch (start us, length us, event | category | flops | bytes accessed | tf_op | source)
XLA Modules:
  0.0 2019.6 jit_solution(15278126699458489443)
XLA Ops:
  15.6 43.2 %all-gather = bf16[32,16,4]{1,2,0:T(4,128)(2,1)S(1)} all-gather(bf16[1,16,4]{1,2,0:T(4,128)(2,1)S(1)} %convert_bitcast_fusion), channel_id=1, replica_groups=mesh['dp'=32] {'dp'}, dimensions={0}, use_global_device_ids=true | all-gather | bytes 4224 | tf_op jit(solution)/shard_map/all_gather | solution.py:153
  59.9 37.0 %all_gather.24 = bf16[512,128]{1,0:T(8,128)(2,1)S(1)} all-gather(bf16[16,128]{1,0:T(8,128)(2,1)S(1)} %convert_element_type.97), channel_id=1, replica_groups=mesh['dp'=32] {'dp'}, dimensions={0}, use_global_device_ids=true | all-gather | bytes 135168 | tf_op jit(solution)/shard_map/all_gather | solution.py:150
  130.7 42.3 %all_gather.25 = bf16[512,512]{1,0:T(8,128)(2,1)} all-gather(bf16[16,512]{1,0:T(8,128)(2,1)S(1)} %convert_element_type.102), channel_id=1, replica_groups=mesh['dp'=32] {'dp'}, dimensions={0}, use_global_device_ids=true | all-gather | bytes 540672 | tf_op jit(solution)/shard_map/all_gather | solution.py:149
  306.3 21.7 %broadcast_select_fusion = (f32[128,32,8,64]{3,2,1,0:T(8,128)}, f32[128,32,8,64]{3,2,1,0:T(8,128)}) fusion(f32[128,32,8,64]{3,2,1,0:T(8,128)} %gather_fusion.2, pred[128]{0:T(512)(128)(4,1)S(1)} %compare_and_fusion, f32[128,32,8,64]{3,2,1,0:T(8,128)} %gather_fusion.1), kind=kLoop, calls=%fused_computation.81 | loop fusion | flops 4194304 | bytes 33554560 | tf_op jit(solution)/shard_map/jvp(jit(_take))/select_n | solution.py:91
  339.6 21.6 %fusion.245 = (f32[128,8,32]{2,1,0:T(8,128)S(1)}, f32[128,8,32,32]{3,2,1,0:T(8,128)}) fusion(f32[128]{0:T(128)S(1)} %log_add_fusion, f32[128,32,8,64]{3,2,1,0:T(8,128)} %get-tuple-element.192, bf16[128,32,8,64]{3,2,1,0:T(8,128)(2,1)} %reshape.734, pred[128,32]{1,0:T(8,128)(4,1)S(1)} %select_compare_fusion), kind=kOutput, calls=%fused_computation.422 | convolution fusion | flops 406814720 | bytes 16912896 | tf_op jit(solution)/shard_map/jvp(bqhd,bkhd->bhqk)/dot_general | solution.py:97
  361.3 37.1 %convert_reduce_fusion = (f32[128,8,32]{2,1,0:T(8,128)}, pred[128,8,32,64]{3,2,1,0:T(8,128)(4,1)}, f32[128,8,32,64]{3,2,1,0:T(8,128)S(1)}) fusion(f32[128,8,32]{2,1,0:T(8,128)S(1)} %reduce_max.182, f32[128,8,32,32]{3,2,1,0:T(8,128)} %get-tuple-element.198, f32[128,8,32,32]{3,2,1,0:T(8,128)} %get-tuple-element.194), kind=kLoop, calls=%fused_computation.21 | loop fusion | flops 8355840 | bytes 19136512 | tf_op jit(solution)/shard_map/jvp()/reduce_sum | solution.py:104
  419.2 23.4 %fusion.10 = f32[128,8,64,32]{2,3,1,0:T(8,128)} fusion(f32[128,8,32,64]{3,2,1,0:T(8,128)} %fusion.40, f32[128,32,8,64]{3,2,1,0:T(8,128)} %get-tuple-element.191), kind=kOutput, calls=%fused_computation.31 | convolution fusion | flops 402653184 | bytes 25165824 | tf_op jit(solution)/shard_map/jvp(bhqk,bkhd->bqhd)/dot_general | solution.py:108
  499.5 26.4 %multiply_convert_fusion = (bf16[4096,2048]{1,0:T(8,128)(2,1)}, f32[4096,2048]{1,0:T(8,128)}) fusion(bf16[512,2048]{1,0:T(8,128)(2,1)} %all-gather.7.cloned.1.call-done, f32[4096,512]{0,1:T(8,128)} %copy-done.3, f32[512]{0:T(512)S(1)} %bitcast.109, f32[512]{0:T(512)S(1)} %bitcast.94, f32[4096]{0:T(1024)S(1)} %fusion.165, f32[4096]{0:T(1024)S(1)} %broadcast_multiply_fusion), kind=kOutput, calls=%fused_computation.14 | convolution fusion | flops 8675917824 | bytes 60854272 | tf_op jit(solution)/shard_map/dot_general | solution.py:184
  539.8 137.5 %reduce-scatter.17.cloned.1.call-done = f32[64,512]{1,0:T(8,128)} async-done(((f32[2048,512]{1,0:T(8,128)}), f32[64,512]{1,0:T(8,128)}) %reduce-scatter.17.cloned.1.call-update) | async-done | bytes 131088 | tf_op jit(solution)/shard_map/reduce_scatter | solution.py:221
  686.7 46.2 %all-gather.9.cloned.1.call-done = bf16[2048,512]{1,0:T(8,128)(2,1)} async-done(((bf16[64,512]{1,0:T(8,128)(2,1)}), bf16[2048,512]{1,0:T(8,128)(2,1)}) %all-gather.9.cloned.1.call-update) | async-done | bytes 2097168 | tf_op jit(solution)/shard_map/all_gather | solution.py:152
  732.9 32.0 %fusion.6 = bf16[4096,2048]{1,0:T(8,128)(2,1)} fusion(f32[4096,2048]{1,0:T(8,128)} %get-tuple-element.202, bf16[4096,512]{1,0:T(8,128)(2,1)} %param.25, bf16[2048,512]{1,0:T(8,128)(2,1)} %all-gather.9.cloned.1.call-done), kind=kOutput, calls=%fused_computation.13 | convolution fusion | flops 8757706752 | bytes 56623104 | tf_op jit(solution)/shard_map/dot_general | solution.py:38
  827.5 29.2 %fusion.16 = f32[128,8,32,32]{3,2,1,0:T(8,128)} fusion(f32[128,32,8,64]{3,2,1,0:T(8,128)} %get-tuple-element.191, f32[128,8,64,32]{2,1,3,0:T(8,128)} %bitcast.81), kind=kOutput, calls=%fused_computation.37 | convolution fusion | flops 402653184 | bytes 20971520 | tf_op jit(solution)/shard_map/transpose(jvp(bhqk,bkhd->bqhd))/dot_general | solution.py:108
  899.1 27.0 %fusion.232 = (f32[128,8,32]{2,1,0:T(8,128)S(1)}, f32[128,8,32,64]{3,2,1,0:T(8,128)S(1)}) fusion(f32[128,8,32,64]{3,2,1,0:T(8,128)} %copy-done, f32[128,8,32]{2,1,0:T(8,128)S(1)} %copy-done.10, f32[128,8,32]{2,1,0:T(8,128)S(1)} %neg.160, f32[128,8,32]{2,1,0:T(8,128)S(1)} %copy-done.24, f32[128,8,32,32]{3,2,1,0:T(8,128)} %fusion.32, ...), kind=kLoop, calls=%fused_computation.411 | loop fusion | flops 12550144 | bytes 25690112 | tf_op jit(solution)/shard_map/transpose(jvp())/reduce_sum | solution.py:105
  933.7 23.9 %fusion.19 = f32[128,8,32,64]{3,2,1,0:T(8,128)} fusion(f32[128,32,8,64]{3,2,1,0:T(8,128)} %get-tuple-element.192, f32[128,8,32,64]{3,2,1,0:T(8,128)} %select_add_fusion, pred[128,32]{1,0:T(8,128)(4,1)S(1)} %copy-done.35), kind=kOutput, calls=%fused_computation.40 | convolution fusion | flops 404750336 | bytes 25169920 | tf_op jit(solution)/shard_map/transpose(jvp(bqhd,bkhd->bhqk))/dot_general | solution.py:97
  1005.8 21.5 %fusion.47 = f32[128,32,8,64]{3,1,2,0:T(8,128)} fusion(f32[128,8,32,64]{3,2,1,0:T(8,128)} %select_add_fusion, pred[128,32]{1,0:T(8,128)(4,1)S(1)} %copy-done.35, bf16[128,32,8,64]{3,2,1,0:T(8,128)(2,1)} %reshape.734), kind=kOutput, calls=%fused_computation.70 | convolution fusion | flops 404750336 | bytes 20975616 | tf_op jit(solution)/shard_map/transpose(jvp(bqhd,bkhd->bhqk))/dot_general | solution.py:97
  1027.3 22.5 %fusion.50 = f32[128,32,8,64]{3,1,2,0:T(8,128)} fusion(f32[128,8,32,64]{3,2,1,0:T(8,128)} %fusion.40, f32[128,8,64,32]{2,1,3,0:T(8,128)} %bitcast.83), kind=kOutput, calls=%fused_computation.71 | convolution fusion | flops 402653184 | bytes 25165824 | tf_op jit(solution)/shard_map/transpose(jvp(bhqk,bkhd->bqhd))/dot_general | solution.py:107
  1049.8 25.1 %fusion.55 = f32[128,32,8,64]{3,1,2,0:T(8,128)} fusion(f32[128,8,32,64]{3,2,1,0:T(8,128)} %fusion.40, f32[128,8,64,32]{2,1,3,0:T(8,128)} %bitcast.84), kind=kOutput, calls=%fused_computation.72 | convolution fusion | flops 402653184 | bytes 25165824 | tf_op jit(solution)/shard_map/transpose(jvp(bhqk,bkhd->bqhd))/dot_general | solution.py:108
  1180.8 37.9 %scatter_fusion = f32[128,32,8,64]{3,2,1,0:T(8,128)} fusion(f32[128,32,8,64]{3,2,1,0:T(8,128)} %copy.244, s32[128]{0:T(128)S(1)} %copy-done.128, f32[128,32,8,64]{3,2,1,0:T(8,128)} %copy.245), kind=kCustom, calls=%fused_computation.3 | custom fusion | flops 2097152 | bytes 25166336 | tf_op jit(solution)/shard_map/transpose(jvp(jit(_take)))/scatter-add | solution.py:90
  1281.8 37.9 %scatter_fusion.1 = f32[128,32,8,64]{3,2,1,0:T(8,128)} fusion(f32[128,32,8,64]{3,2,1,0:T(8,128)} %copy.250, s32[128]{0:T(128)S(1)} %copy-done.128, f32[128,32,8,64]{3,2,1,0:T(8,128)} %copy.251), kind=kCustom, calls=%fused_computation.4 | custom fusion | flops 2097152 | bytes 25166336 | tf_op jit(solution)/shard_map/transpose(jvp(jit(_take)))/scatter-add | solution.py:91
  1448.7 51.8 %reduce-scatter.21.cloned.1.call-done = f32[16,4]{1,0:T(8,128)} async-done(((f32[512,4]{1,0:T(8,128)}), f32[16,4]{1,0:T(8,128)}) %reduce-scatter.21.cloned.1.call-update) | async-done | bytes 272
  1501.9 130.2 %reduce-scatter.19.cloned.1.call-done = f32[16,128]{1,0:T(8,128)} async-done(((f32[512,128]{1,0:T(8,128)}), f32[16,128]{1,0:T(8,128)}) %reduce-scatter.19.cloned.1.call-update) | async-done | bytes 8208 | tf_op jit(solution)/shard_map/reduce_scatter | solution.py:219
  1633.4 131.7 %reduce-scatter.13.cloned.1.call-done = f32[16,512]{1,0:T(8,128)} async-done(((f32[512,512]{1,0:T(8,128)}), f32[16,512]{1,0:T(8,128)}) %reduce-scatter.13.cloned.1.call-update) | async-done | bytes 32784 | tf_op jit(solution)/shard_map/reduce_scatter | solution.py:218
  1766.4 102.4 %reduce-scatter.11.cloned.1.call-done = f32[16,1536]{1,0:T(8,128)} async-done(((f32[512,1536]{1,0:T(8,128)}), f32[16,1536]{1,0:T(8,128)}) %reduce-scatter.11.cloned.1.call-update) | async-done | bytes 98320 | tf_op jit(solution)/shard_map/reduce_scatter | solution.py:217
  1870.5 140.7 %reduce-scatter.15.cloned.1.call-done = f32[16,2048]{1,0:T(8,128)} async-done(((f32[512,2048]{1,0:T(8,128)}), f32[16,2048]{1,0:T(8,128)}) %reduce-scatter.15.cloned.1.call-update) | async-done | bytes 131088 | tf_op jit(solution)/shard_map/reduce_scatter | solution.py:220
  (585 shorter events, 752.3 us)
Async XLA Ops:
  7.2 177.4 %all-gather.5.cloned.1.call-start = ((), (), s32[]{:S(2)}) async-start(), calls=%async_computation.6 | async-start | bytes 1622016 | tf_op jit(solution)/shard_map/all_gather | solution.py:148
  8.8 490.6 %all-gather.7.cloned.1.call-start = ((), (), s32[]{:S(2)}) async-start(), calls=%async_computation.7 | async-start | bytes 2162688 | tf_op jit(solution)/shard_map/all_gather | solution.py:151
  10.4 666.9 %reduce-scatter.17.cloned.1.call-start = ((), (), s32[]{:S(2)}) async-start(), calls=%async_computation.12 | async-start | bytes 4325376 | tf_op jit(solution)/shard_map/reduce_scatter | solution.py:221
  408.1 277.7 %copy-start.23 = (f32[128,8,32]{2,1,0:T(8,128)}, f32[128,8,32]{2,1,0:T(8,128)S(1)}, u32[]{:S(2)}) copy-start(f32[128,8,32]{2,1,0:T(8,128)S(1)} %fusion.41) | copy-start | bytes 393220
  495.2 302.1 %copy-start.47 = (f32[4096]{0:T(1024)}, f32[4096]{0:T(1024)S(1)}, u32[]{:S(2)}) copy-start(f32[4096]{0:T(1024)S(1)} %broadcast_multiply_fusion) | copy-start | bytes 49156
  499.4 297.9 %copy-start.55 = (f32[4096]{0:T(1024)}, f32[4096]{0:T(1024)S(1)}, u32[]{:S(2)}) copy-start(f32[4096]{0:T(1024)S(1)} %fusion.165) | copy-start | bytes 49156
  539.8 193.1 %all-gather.9.cloned.1.call-start = ((), (), s32[]{:S(2)}) async-start(), calls=%async_computation.8 | async-start | bytes 2162688 | tf_op jit(solution)/shard_map/all_gather | solution.py:152
  679.1 821.4 %reduce-scatter.21.cloned.1.call-start = ((), (), s32[]{:S(2)}) async-start(), calls=%async_computation.14 | async-start | bytes 270336
  1366.4 265.7 %reduce-scatter.19.cloned.1.call-start = ((), (), s32[]{:S(2)}) async-start(), calls=%async_computation.13 | async-start | bytes 270336 | tf_op jit(solution)/shard_map/reduce_scatter | solution.py:219
  1367.3 397.7 %reduce-scatter.13.cloned.1.call-start = ((), (), s32[]{:S(2)}) async-start(), calls=%async_computation.10 | async-start | bytes 1081344 | tf_op jit(solution)/shard_map/reduce_scatter | solution.py:218
  1374.3 494.6 %reduce-scatter.11.cloned.1.call-start = ((), (), s32[]{:S(2)}) async-start(), calls=%async_computation.9 | async-start | bytes 3244032 | tf_op jit(solution)/shard_map/reduce_scatter | solution.py:217
  1387.3 623.9 %reduce-scatter.15.cloned.1.call-start = ((), (), s32[]{:S(2)}) async-start(), calls=%async_computation.11 | async-start | bytes 4325376 | tf_op jit(solution)/shard_map/reduce_scatter | solution.py:220
  1439.4 192.6 %copy-start.82 = (f32[16,128]{1,0:T(8,128)S(1)}, f32[16,128]{1,0:T(8,128)}, u32[]{:S(2)}) copy-start(f32[16,128]{1,0:T(8,128)} %param.30) | copy-start | bytes 24580
  1439.4 192.6 %copy-start.109 = (f32[16,128]{1,0:T(8,128)S(1)}, f32[16,128]{1,0:T(8,128)}, u32[]{:S(2)}) copy-start(f32[16,128]{1,0:T(8,128)} %param.36) | copy-start | bytes 24580
  1439.5 192.6 %copy-start.110 = (f32[16,128]{1,0:T(8,128)S(1)}, f32[16,128]{1,0:T(8,128)}, u32[]{:S(2)}) copy-start(f32[16,128]{1,0:T(8,128)} %param.42) | copy-start | bytes 24580
  1439.5 325.5 %copy-start.63 = (f32[16,512]{1,0:T(8,128)S(1)}, f32[16,512]{1,0:T(8,128)}, u32[]{:S(2)}) copy-start(f32[16,512]{1,0:T(8,128)} %param.29) | copy-start | bytes 98308
  1439.5 325.5 %copy-start.80 = (f32[16,512]{1,0:T(8,128)S(1)}, f32[16,512]{1,0:T(8,128)}, u32[]{:S(2)}) copy-start(f32[16,512]{1,0:T(8,128)} %param.35) | copy-start | bytes 98308
  1439.5 325.5 %copy-start.81 = (f32[16,512]{1,0:T(8,128)S(1)}, f32[16,512]{1,0:T(8,128)}, u32[]{:S(2)}) copy-start(f32[16,512]{1,0:T(8,128)} %param.41) | copy-start | bytes 98308
  1439.5 429.3 %copy-start.40 = (f32[16,1536]{1,0:T(8,128)S(1)}, f32[16,1536]{1,0:T(8,128)}, u32[]{:S(2)}) copy-start(f32[16,1536]{1,0:T(8,128)} %param.28) | copy-start | bytes 294916
  1439.5 429.3 %copy-start.64 = (f32[16,1536]{1,0:T(8,128)S(1)}, f32[16,1536]{1,0:T(8,128)}, u32[]{:S(2)}) copy-start(f32[16,1536]{1,0:T(8,128)} %param.34) | copy-start | bytes 294916
  1439.5 429.3 %copy-start.65 = (f32[16,1536]{1,0:T(8,128)S(1)}, f32[16,1536]{1,0:T(8,128)}, u32[]{:S(2)}) copy-start(f32[16,1536]{1,0:T(8,128)} %param.40) | copy-start | bytes 294916
  1439.5 571.7 %copy-start.36 = (f32[16,2048]{1,0:T(8,128)S(1)}, f32[16,2048]{1,0:T(8,128)}, u32[]{:S(2)}) copy-start(f32[16,2048]{1,0:T(8,128)} %param.31) | copy-start | bytes 393220
  1439.6 571.6 %copy-start.60 = (f32[16,2048]{1,0:T(8,128)S(1)}, f32[16,2048]{1,0:T(8,128)}, u32[]{:S(2)}) copy-start(f32[16,2048]{1,0:T(8,128)} %param.37) | copy-start | bytes 393220
  1439.6 571.6 %copy-start.61 = (f32[16,2048]{1,0:T(8,128)S(1)}, f32[16,2048]{1,0:T(8,128)}, u32[]{:S(2)}) copy-start(f32[16,2048]{1,0:T(8,128)} %param.43) | copy-start | bytes 393220
  (157 other events, 3472.6 us)
Sparse Core Ops, SparseCore 0:
  11.5 57.8 all-gather.4
  72.7 55.1 all-gather.6
  539.9 137.3 reduce-scatter.16
  680.6 52.2 all-gather.8
  1366.5 133.9 reduce-scatter.20
  1502.7 129.3 reduce-scatter.18
  1634.3 130.7 reduce-scatter.12
  1771.3 97.4 reduce-scatter.10
  1871.2 139.9 reduce-scatter.14
where the time goes:
time: 2030 us; the launch traced here: 2020 us
  waiting for transfers between devices  741 us (37%)
  matrix products  435 us (21%)
  local copies, waits for them, and re-layouts  373 us (18%)
  other arithmetic  331 us (16%)
  blocking collectives  122 us (6%)
    reduce_scatter x1, waiting for transfers between devices, body(): lax.psum_scatter(grad_ffn_in, 'dp', scatter_dimension=0, tiled=True)  141 us
    reduce_scatter x1, waiting for transfers between devices, body(): lax.psum_scatter(grad_ffn_out, 'dp', scatter_dimension=0, tiled=True)  137 us
    reduce_scatter x1, waiting for transfers between devices, body(): lax.psum_scatter(grad_attn_out, 'dp', scatter_dimension=0, tiled=True)  132 us
    reduce_scatter x1, waiting for transfers between devices, body(): lax.psum_scatter(grad_sort, 'dp', scatter_dimension=0, tiled=True)  130 us
    reduce_scatter x1, waiting for transfers between devices, body(): lax.psum_scatter(grad_qkv, 'dp', scatter_dimension=0, tiled=True)  102 us
    dot_general x3, matrix products, sorted_attention(): jnp.einsum('bhqk,bkhd->bqhd', probs[..., BLOCK:], v_far, precision=blockw...  77.6 us
    dot_general x4, matrix products, inner_right(): lax.dot_general(left, right, (((1,), (1,)), ((), ())), preferred_element_...  67.4 us
    dot_general x3, matrix products, sorted_attention(): jnp.einsum('bqhd,bkhd->bhqk', q_blocks, k_far, precision=blockwise) * scale  67 us
  transfers between devices with their start and end apart: 9, of which 7 were waited for; matrix products, arithmetic and copies ran while one was open for 22% of the time, Pallas kernels for 0%

commit v1 on v0

v1 whole, which is shorter than its diff:
```python
import functools
import math

import jax
import jax.numpy as jnp
from jax import lax
from jax.experimental import pallas as pl
from jax.experimental.pallas import tpu as pltpu
from jax.sharding import PartitionSpec as P

HEADS = 8
HEAD = 64
SORT = 64
BLOCK = 32
SINK = 8
STEP = 10
TILE = 512
CHUNK = 512
GROUP = 128
LANES = 128

highest = lax.Precision.HIGHEST
masked = -1000000000.0
norm_eps = 1e-05
beta_one = 0.9
beta_two = 0.999
adam_eps = 1e-08
decay = 0.01
rates = (0.05, 0.15, 0.05, 0.05, 0.025, 0.5)
f32 = jnp.float32
bf16 = jnp.bfloat16


def dot(left, right, precision=None):
    return jnp.dot(left, right, precision=precision, preferred_element_type=f32)


def dot_nt(left, right, precision=None):
    return lax.dot_general(
        left, right, (((1,), (1,)), ((), ())), precision=precision, preferred_element_type=f32
    )


def dot_tn(left, right, precision=None):
    return lax.dot_general(
        left, right, (((0,), (0,)), ((), ())), precision=precision, preferred_element_type=f32
    )


def iota(shape, axis):
    return lax.broadcasted_iota(jnp.int32, shape, axis)


def ends_of(lens, slot):
    quarter = slot // 4
    is_long = lens[0, 0] > quarter
    return [jnp.where(is_long, lens[0, 0], k * quarter + lens[0, k]) for k in range(4)]


def end_at(places, ends, slot):
    quarter = slot // 4
    return jnp.where(
        places < 2 * quarter,
        jnp.where(places < quarter, ends[0], ends[1]),
        jnp.where(places < 3 * quarter, ends[2], ends[3]),
    )


def norm_stats(value):
    center = value - jnp.mean(value, axis=-1, keepdims=True)
    spread = jnp.mean(center * center, axis=-1, keepdims=True)
    rstd = lax.rsqrt(spread + norm_eps)
    return center * rstd, rstd


def norm_back(grad, hat, rstd, gain):
    d_hat = grad * gain
    mean_d = jnp.mean(d_hat, axis=-1, keepdims=True)
    mean_dh = jnp.mean(d_hat * hat, axis=-1, keepdims=True)
    return rstd * (d_hat - mean_d - hat * mean_dh)


def params(limit=56 << 20):
    return pltpu.CompilerParams(vmem_limit_bytes=limit)


def whole(shape):
    return pl.BlockSpec(shape, lambda *_: (0,) * len(shape))


def smem():
    return pl.BlockSpec(memory_space=pltpu.SMEM)


def project_kernel(lens, x_ref, wq_ref, wk_ref, wv_ref, q_ref, k_ref, v_ref, u_ref, norms_ref, *, slot):
    tile, width = x_ref.shape
    base = pl.program_id(0) * tile

    @pl.when(pl.program_id(0) == 0)
    def _():
        norms_ref[...] = wq_ref[:, width + LANES :].astype(f32).T[:8, :]

    hat, _ = norm_stats(x_ref[...].astype(f32))
    h_one = (hat * norms_ref[0:1, :] + norms_ref[1:2, :]).astype(bf16)
    q_ref[...] = dot(h_one, wq_ref[:, :width]).astype(bf16)
    k_ref[...] = dot(h_one, wk_ref[...]).astype(bf16)
    v_ref[...] = dot(h_one, wv_ref[...]).astype(bf16)
    blocks = tile // BLOCK
    at = iota((blocks, tile), 1)
    places = at + base
    live = places < end_at(places, ends_of(lens, slot), slot)
    own = (at // BLOCK) == iota((blocks, tile), 0)
    pick = jnp.where(live & own, 1.0, 0.0).astype(bf16)
    u_ref[...] = dot(pick, h_one)


def project(lens, x, w_q, w_k, w_v):
    slot, width = x.shape
    grid = slot // TILE
    row = pl.BlockSpec((TILE, width), lambda i: (i, 0))
    out = jax.ShapeDtypeStruct((slot, width), bf16)
    return pl.pallas_call(
        functools.partial(project_kernel, slot=slot),
        grid=(grid,),
        in_specs=[smem(), row, whole(w_q.shape), whole(w_k.shape), whole(w_v.shape)],
        out_specs=[
            row,
            row,
            row,
            pl.BlockSpec((TILE // BLOCK, width), lambda i: (i, 0)),
            whole((8, width)),
        ],
        out_shape=[
            out,
            out,
            out,
            jax.ShapeDtypeStruct((slot // BLOCK, width), f32),
            jax.ShapeDtypeStruct((8, width), f32),
        ],
        compiler_params=params(),
        cost_estimate=pl.CostEstimate(
            flops=2 * slot * width * 3 * width, bytes_accessed=slot * width * 8, transcendentals=0
        ),
        name="project",
    )(lens, x, w_q, w_k, w_v)


def sort_parts(lens, u_ref, ws_ref, slot):
    blocks = u_ref.shape[0]
    ends = ends_of(lens, slot)
    quarter = slot // 4
    is_long = lens[0, 0] > quarter

    def group_of(axis, shape):
        index = iota(shape, axis)
        start = index * BLOCK
        live = start < end_at(start, ends, slot)
        member = jnp.where(is_long, 0, start // quarter)
        return jnp.where(live, member, 4 + index)

    same = group_of(0, (blocks, blocks)) == group_of(1, (blocks, blocks))
    start = iota((blocks, 1), 0) * BLOCK
    count = jnp.clip(end_at(start, ends, slot) - start, 0, BLOCK).astype(f32)
    scale = lax.rsqrt(jnp.maximum(count, 1.0))
    summary = u_ref[...] * scale
    w_sort = ws_ref[...].astype(f32)
    sort_q = dot(summary, w_sort[:, :SORT], highest)
    sort_k = dot(summary, w_sort[:, SORT:], highest)
    return same, scale, summary, w_sort, sort_q, sort_k


def sort_columns(w_q):
    return pl.BlockSpec((w_q.shape[0], 2 * SORT), lambda i: (0, w_q.shape[0] // (2 * SORT)))


def column_of(row, eye):
    return jnp.sum(jnp.where(eye, row, 0.0), axis=1, keepdims=True)


def sort_kernel(lens, u_ref, ws_ref, partner_ref, bias_ref, steps_ref, *, slot):
    blocks = u_ref.shape[0]
    same, _, _, _, sort_q, sort_k = sort_parts(lens, u_ref, ws_ref, slot)
    raw = dot_nt(sort_q, sort_k, highest)
    logits = jnp.where(same, raw / math.sqrt(SORT), masked)

    def normalize(value, axis):
        top = jnp.max(value, axis=axis, keepdims=True)
        return value - (top + jnp.log(jnp.sum(jnp.exp(value - top), axis=axis, keepdims=True)))

    for turn in range(SINK):
        logits = normalize(logits, 1)
        steps_ref[2 * turn] = logits
        logits = normalize(logits, 0)
        steps_ref[2 * turn + 1] = logits
    eye = iota((blocks, blocks), 0) == iota((blocks, blocks), 1)
    members = jnp.sum(same.astype(f32), axis=1, keepdims=True)
    partner = column_of(partner_ref[...].astype(f32), eye)
    pick = partner == iota((blocks, blocks), 1).astype(f32)
    bias = jnp.sum(jnp.where(pick, logits, 0.0), axis=1, keepdims=True) + jnp.log(members)
    bias_ref[...] = jnp.sum(jnp.where(eye, bias, 0.0), axis=0, keepdims=True)


def sort_net(lens, u, w_sort, partner, slot):
    blocks = u.shape[0]
    return pl.pallas_call(
        functools.partial(sort_kernel, slot=slot),
        in_specs=[smem(), whole(u.shape), sort_columns(w_sort), whole(partner.shape)],
        out_specs=[whole((1, blocks)), whole((2 * SINK, blocks, blocks))],
        out_shape=[
            jax.ShapeDtypeStruct((1, blocks), f32),
            jax.ShapeDtypeStruct((2 * SINK, blocks, blocks), f32),
        ],
        grid=(1,),
        compiler_params=params(),
        cost_estimate=pl.CostEstimate(flops=10**8, bytes_accessed=10**7, transcendentals=10**6),
        name="sort_net",
    )(lens, u, w_sort, partner)


def sort_back_kernel(
    lens, u_ref, ws_ref, partner_ref, d_bias_ref, steps_ref, d_u_ref, grad_ref, *, slot
):
    blocks = u_ref.shape[0]
    same, scale, summary, w_sort, sort_q, sort_k = sort_parts(lens, u_ref, ws_ref, slot)
    eye = iota((blocks, blocks), 0) == iota((blocks, blocks), 1)
    partner = column_of(partner_ref[...].astype(f32), eye)
    pick = partner == iota((blocks, blocks), 1).astype(f32)
    d_bias = column_of(d_bias_ref[...], eye)
    d_logits = jnp.where(pick, d_bias, 0.0)
    for turn in reversed(range(SINK)):
        for axis, step in ((0, 2 * turn + 1), (1, 2 * turn)):
            share = jnp.exp(steps_ref[step])
            d_logits = d_logits - share * jnp.sum(d_logits, axis=axis, keepdims=True)
    d_raw = jnp.where(same, d_logits, 0.0) / math.sqrt(SORT)
    d_sort_q = dot(d_raw, sort_k, highest)
    d_sort_k = dot_tn(d_raw, sort_q, highest)
    d_sort = jnp.concatenate([d_sort_q, d_sort_k], axis=1)
    grad_ref[...] = dot_tn(summary, d_sort, highest)
    d_u_ref[...] = dot_nt(d_sort, w_sort, highest) * scale


def sort_back(lens, u, w_sort, partner, d_bias, steps, slot):
    blocks, width = u.shape
    return pl.pallas_call(
        functools.partial(sort_back_kernel, slot=slot),
        in_specs=[
            smem(),
            whole(u.shape),
            sort_columns(w_sort),
            whole(partner.shape),
            whole(d_bias.shape),
            whole(steps.shape),
        ],
        out_specs=[whole((blocks, width)), whole((width, 2 * SORT))],
        out_shape=[
            jax.ShapeDtypeStruct((blocks, width), f32),
            jax.ShapeDtypeStruct((width, 2 * SORT), f32),
        ],
        grid=(1,),
        compiler_params=params(),
        cost_estimate=pl.CostEstimate(flops=10**8, bytes_accessed=10**7, transcendentals=10**6),
        name="sort_back",
    )(lens, u, w_sort, partner, d_bias, steps)


def lane_block(rows):
    return (iota((rows, 2 * GROUP), 1) % GROUP) // BLOCK


def compact(full):
    at = lane_block(BLOCK)
    part = [full[c * BLOCK : (c + 1) * BLOCK] for c in range(GROUP // BLOCK)]
    return jnp.where(
        at < 2,
        jnp.where(at < 1, part[0], part[1]),
        jnp.where(at < 3, part[2], part[3]),
    )


def diagonal_mask():
    rows = 2 * GROUP
    return jnp.where((iota((rows, rows), 0) % GROUP) // BLOCK == lane_block(rows), 1.0, 0.0).astype(bf16)


def spread(own, far, mask):
    own, far = own.astype(bf16), far.astype(bf16)
    times = GROUP // BLOCK
    return jnp.concatenate([own] * times + [far] * times, axis=0) * mask


def head_stack(pair, lanes):
    zero = jnp.zeros_like(pair)
    return jnp.concatenate(
        [jnp.where(lanes < HEAD, pair, zero), jnp.where(lanes < HEAD, zero, pair)], axis=0
    )


def head_lanes():
    return iota((GROUP, LANES), 1)


def by_lane(values):
    at = iota((1, GROUP), 1) // BLOCK
    return jnp.where(
        at < 2,
        jnp.where(at < 1, values[0], values[1]),
        jnp.where(at < 3, values[2], values[3]),
    )


def gather_far(dst, src, partners):
    for c, p in enumerate(partners):
        dst[GROUP + c * BLOCK : GROUP + (c + 1) * BLOCK, :] = src[pl.ds(pl.multiple_of(p * BLOCK, BLOCK), BLOCK), :]


def attend_kernel(
    lens, partner, bias, q_ref, k_ref, v_ref, o_ref, p_ref, k_cat, v_cat, mask_ref, *, slot
):
    tile, width = q_ref.shape
    step = pl.program_id(0)
    pairs = width // LANES
    per = GROUP // BLOCK

    @pl.when(step == 0)
    def _():
        mask_ref[...] = diagonal_mask()

    ends = ends_of(lens, slot)
    scale = 1.0 / math.sqrt(HEAD)

    def one_group(g, carry):
        first = step * (tile // BLOCK) + g * per
        partners = [partner[0, first + c] for c in range(per)]
        rows = pl.ds(pl.multiple_of(first * BLOCK, GROUP), GROUP)
        k_cat[0:GROUP, :] = k_ref[rows, :]
        v_cat[0:GROUP, :] = v_ref[rows, :]
        gather_far(k_cat, k_ref, partners)
        gather_far(v_cat, v_ref, partners)
        key = iota((BLOCK, GROUP), 0)
        query = iota((BLOCK, GROUP), 1)
        own_place = (first + query // BLOCK) * BLOCK + key
        far_place = by_lane(partners) * BLOCK + key
        own_live = (own_place < end_at(own_place, ends, slot)) | (query % BLOCK == key)
        far_live = far_place < end_at(far_place, ends, slot)
        own_live = jnp.concatenate([own_live.astype(f32)] * 2, axis=1) > 0.5
        far_live = jnp.concatenate([far_live.astype(f32)] * 2, axis=1) > 0.5
        lane_bias = by_lane([bias[0, first + c] for c in range(per)])
        lane_bias = jnp.concatenate([lane_bias] * 2, axis=1)
        lanes = head_lanes()
        mask = mask_ref[...]
        q_rows = pl.ds(pl.multiple_of(g * GROUP, GROUP), GROUP)
        for pair in range(pairs):
            cols = slice(pair * LANES, (pair + 1) * LANES)
            q_two = head_stack(q_ref[q_rows, cols], lanes)
            scores = dot_nt(k_cat[:, cols], q_two)
            own = jnp.where(own_live, compact(scores[:GROUP]) * scale, masked)
            far = jnp.where(far_live, compact(scores[GROUP:]) * scale + lane_bias, masked)
            top = jnp.maximum(
                jnp.max(own, axis=0, keepdims=True), jnp.max(far, axis=0, keepdims=True)
            )
            own = jnp.exp(own - top)
            far = jnp.exp(far - top)
            total = jnp.sum(own, axis=0, keepdims=True) + jnp.sum(far, axis=0, keepdims=True)
            inverse = 1.0 / total
            own = own * inverse
            far = far * inverse
            at = pl.multiple_of((g * pairs + pair) * 2 * BLOCK, 2 * BLOCK)
            p_ref[pl.ds(at, BLOCK), :] = own.astype(bf16)
            p_ref[pl.ds(at + BLOCK, BLOCK), :] = far.astype(bf16)
            mixed = dot(v_cat[:, cols].T, spread(own, far, mask))
            o_ref[pair * LANES : pair * LANES + HEAD, q_rows] = mixed[:HEAD, :GROUP].astype(bf16)
            o_ref[pair * LANES + HEAD : (pair + 1) * LANES, q_rows] = mixed[HEAD:, GROUP:].astype(bf16)
        return carry

    lax.fori_loop(0, tile // GROUP, one_group, 0)


def attend(lens, partner, bias, q, k, v):
    slot, width = q.shape
    grid = slot // TILE
    per_tile = (TILE // GROUP) * (width // LANES) * 2 * BLOCK
    return pl.pallas_call(
        functools.partial(attend_kernel, slot=slot),
        grid=(grid,),
        in_specs=[
            smem(),
            smem(),
            smem(),
            pl.BlockSpec((TILE, width), lambda i: (i, 0)),
            whole(k.shape),
            whole(v.shape),
        ],
        out_specs=[
            pl.BlockSpec((width, TILE), lambda i: (0, i)),
            pl.BlockSpec((per_tile, 2 * GROUP), lambda i: (i, 0)),
        ],
        out_shape=[
            jax.ShapeDtypeStruct((width, slot), bf16),
            jax.ShapeDtypeStruct((grid * per_tile, 2 * GROUP), bf16),
        ],
        scratch_shapes=[
            pltpu.VMEM((2 * GROUP, width), bf16),
            pltpu.VMEM((2 * GROUP, width), bf16),
            pltpu.VMEM((2 * GROUP, 2 * GROUP), bf16),
        ],
        compiler_params=params(),
        cost_estimate=pl.CostEstimate(
            flops=20 * 10**9, bytes_accessed=slot * width * 10, transcendentals=slot * 512
        ),
        name="attend",
    )(lens, partner, bias, q, k, v)


def attend_back_kernel(
    partner, q_ref, do_ref, p_ref, k_ref, v_ref,
    dq_ref, dk_ref, dv_ref, db_ref,
    k_cat, v_cat, mask_ref, dk_sum, dv_sum, db_sum,
):
    tile, width = q_ref.shape
    step = pl.program_id(0)
    pairs = width // LANES
    per = GROUP // BLOCK

    @pl.when(step == 0)
    def _():
        mask_ref[...] = diagonal_mask()
        dk_sum[...] = jnp.zeros_like(dk_sum)
        dv_sum[...] = jnp.zeros_like(dv_sum)

    scale = 1.0 / math.sqrt(HEAD)

    def one_group(g, carry):
        first = step * (tile // BLOCK) + g * per
        partners = [partner[0, first + c] for c in range(per)]
        rows = pl.ds(pl.multiple_of(first * BLOCK, GROUP), GROUP)
        k_cat[0:GROUP, :] = k_ref[rows, :]
        v_cat[0:GROUP, :] = v_ref[rows, :]
        gather_far(k_cat, k_ref, partners)
        gather_far(v_cat, v_ref, partners)
        lanes = head_lanes()
        mask = mask_ref[...]
        q_rows = pl.ds(pl.multiple_of(g * GROUP, GROUP), GROUP)
        d_bias = jnp.zeros((1, 2 * GROUP), f32)
        for pair in range(pairs):
            cols = slice(pair * LANES, (pair + 1) * LANES)
            q_two = head_stack(q_ref[q_rows, cols], lanes)
            do_two = head_stack(do_ref[q_rows, cols], lanes)
            d_prob = dot_nt(v_cat[:, cols], do_two)
            at = pl.multiple_of((g * pairs + pair) * 2 * BLOCK, 2 * BLOCK)
            own_b = p_ref[pl.ds(at, BLOCK), :]
            far_b = p_ref[pl.ds(at + BLOCK, BLOCK), :]
            own, far = own_b.astype(f32), far_b.astype(f32)
            d_own, d_far = compact(d_prob[:GROUP]), compact(d_prob[GROUP:])
            delta = jnp.sum(own * d_own, axis=0, keepdims=True) + jnp.sum(
                far * d_far, axis=0, keepdims=True
            )
            d_own = own * (d_own - delta)
            d_far = far * (d_far - delta)
            d_bias = d_bias + jnp.sum(d_far, axis=0, keepdims=True)
            d_scores = spread(d_own * scale, d_far * scale, mask)
            dk = dot(d_scores, q_two)
            dv = dot(spread(own_b, far_b, mask), do_two)
            dq = dot(k_cat[:, cols].T, d_scores)
            dq = jnp.concatenate([dq[:HEAD, :GROUP], dq[HEAD:, GROUP:]], axis=0)
            dq_ref[q_rows, cols] = dq.T.astype(bf16)
            dk_sum[rows, cols] += dk[:GROUP]
            dv_sum[rows, cols] += dv[:GROUP]
            for c, p in enumerate(partners):
                there = pl.ds(pl.multiple_of(p * BLOCK, BLOCK), BLOCK)
                here = slice(GROUP + c * BLOCK, GROUP + (c + 1) * BLOCK)
                dk_sum[there, cols] += dk[here]
                dv_sum[there, cols] += dv[here]
        db_sum[pl.ds(step * (tile // GROUP) + g, 1), :] = d_bias[:, :GROUP] + d_bias[:, GROUP:]
        return carry

    lax.fori_loop(0, tile // GROUP, one_group, 0)

    @pl.when(step == pl.num_programs(0) - 1)
    def _():
        dk_ref[...] = dk_sum[...].astype(bf16)
        dv_ref[...] = dv_sum[...].astype(bf16)
        groups = db_sum.shape[0]
        blocks = groups * per
        pick = (iota((GROUP, blocks), 0) // BLOCK == iota((GROUP, blocks), 1) % per).astype(f32)
        sums = dot(db_sum[...], pick, highest)
        mine = iota((groups, blocks), 1) // per == iota((groups, blocks), 0)
        db_ref[...] = jnp.sum(jnp.where(mine, sums, 0.0), axis=0, keepdims=True)


def attend_back(partner, q, d_o, probs, k, v):
    slot, width = q.shape
    grid = slot // TILE
    per_tile = (TILE // GROUP) * (width // LANES) * 2 * BLOCK
    row = pl.BlockSpec((TILE, width), lambda i: (i, 0))
    once = pl.BlockSpec((slot, width), lambda i: (0, 0), pipeline_mode=pl.Buffered(1))
    out = jax.ShapeDtypeStruct((slot, width), bf16)
    return pl.pallas_call(
        attend_back_kernel,
        grid=(grid,),
        in_specs=[
            smem(),
            row,
            row,
            pl.BlockSpec((per_tile, 2 * GROUP), lambda i: (i, 0)),
            once,
            once,
        ],
        out_specs=[row, once, once, whole((1, slot // BLOCK))],
        out_shape=[out, out, out, jax.ShapeDtypeStruct((1, slot // BLOCK), f32)],
        scratch_shapes=[
            pltpu.VMEM((2 * GROUP, width), bf16),
            pltpu.VMEM((2 * GROUP, width), bf16),
            pltpu.VMEM((2 * GROUP, 2 * GROUP), bf16),
            pltpu.VMEM((slot, width), f32),
            pltpu.VMEM((slot, width), f32),
            pltpu.VMEM((slot // GROUP, GROUP), f32),
        ],
        compiler_params=params(),
        cost_estimate=pl.CostEstimate(
            flops=40 * 10**9, bytes_accessed=slot * width * 16, transcendentals=0
        ),
        name="attend_back",
    )(partner, q, d_o, probs, k, v)


def ffn_kernel(
    x_ref, dy_ref, o_ref, norms_ref, wo_ref, win_ref, wout_ref,
    out_ref, dx_ref, do_ref, g_attn_ref, g_in_ref, g_out_ref, g_norm_ref,
    h_scr, ht_scr, dyt_scr, y_scr, dh_scr, gt_scr,
):
    tile, width = x_ref.shape
    hidden = win_ref.shape[1]
    step = pl.program_id(0)

    @pl.when(step == 0)
    def _():
        g_attn_ref[...] = jnp.zeros_like(g_attn_ref)
        g_in_ref[...] = jnp.zeros_like(g_in_ref)
        gt_scr[...] = jnp.zeros_like(gt_scr)
        g_norm_ref[...] = jnp.zeros_like(g_norm_ref)

    o_t = o_ref[...]
    x_one = x_ref[...].astype(f32) + dot(o_t.T, wo_ref[...])
    hat, rstd = norm_stats(x_one)
    h_two = (hat * norms_ref[2:3, :] + norms_ref[3:4, :]).astype(bf16)
    h_scr[...] = h_two
    ht_scr[...] = h_two.T
    dyt_scr[...] = dy_ref[...].T
    y_scr[...] = x_one
    dh_scr[...] = jnp.zeros_like(dh_scr)
    root = math.sqrt(2.0 / math.pi)

    def one_chunk(c, carry):
        cols = pl.ds(pl.multiple_of(c * CHUNK, CHUNK), CHUNK)
        act = dot(h_scr[...], win_ref[:, cols])
        d_hid = dot_nt(dy_ref[...], wout_ref[cols, :])
        square = act * act
        curve = jnp.tanh(act * (root + (root * 0.044715) * square))
        gate = 0.5 + 0.5 * curve
        hid = act * gate
        hid_b = hid.astype(bf16)
        slope = gate + hid * (1.0 - curve) * (root + (3.0 * root * 0.044715) * square)
        d_act = (d_hid * slope).astype(bf16)
        y_scr[...] += dot(hid_b, wout_ref[cols, :])
        gt_scr[:, cols] += dot(dyt_scr[...], hid_b)
        g_in_ref[:, cols] += dot(ht_scr[...], d_act)
        dh_scr[...] += dot_nt(d_act, win_ref[:, cols])
        return carry

    lax.fori_loop(0, hidden // CHUNK, one_chunk, 0)
    out_ref[...] = y_scr[...].astype(bf16)
    d_h = dh_scr[...]
    g_norm_ref[2:3, :] += jnp.sum(d_h * hat, axis=0, keepdims=True)
    g_norm_ref[3:4, :] += jnp.sum(d_h, axis=0, keepdims=True)
    d_x = dy_ref[...].astype(f32) + norm_back(d_h, hat, rstd, norms_ref[2:3, :])
    dx_ref[...] = d_x
    d_z = d_x.astype(bf16)
    g_attn_ref[...] += dot(o_t, d_z)
    do_ref[...] = dot_nt(d_z, wo_ref[...]).astype(bf16)

    @pl.when(step == pl.num_programs(0) - 1)
    def _():
        g_out_ref[...] = gt_scr[...].T


def ffn(x, dy, o_t, norms, w_o, w_in, w_out):
    slot, width = x.shape
    hidden = w_in.shape[1]
    grid = slot // TILE
    row = pl.BlockSpec((TILE, width), lambda i: (i, 0))

    def once(shape):
        return pl.BlockSpec(shape, lambda i: (0, 0), pipeline_mode=pl.Buffered(1))

    return pl.pallas_call(
        ffn_kernel,
        grid=(grid,),
        in_specs=[
            row,
            row,
            pl.BlockSpec((width, TILE), lambda i: (0, i)),
            once(norms.shape),
            once(w_o.shape),
            once(w_in.shape),
            once(w_out.shape),
        ],
        out_specs=[
            row,
            row,
            row,
            once((width, width)),
            once((width, hidden)),
            once((hidden, width)),
            once((8, width)),
        ],
        out_shape=[
            jax.ShapeDtypeStruct((slot, width), bf16),
            jax.ShapeDtypeStruct((slot, width), f32),
            jax.ShapeDtypeStruct((slot, width), bf16),
            jax.ShapeDtypeStruct((width, width), f32),
            jax.ShapeDtypeStruct((width, hidden), f32),
            jax.ShapeDtypeStruct((hidden, width), f32),
            jax.ShapeDtypeStruct((8, width), f32),
        ],
        scratch_shapes=[
            pltpu.VMEM((TILE, width), bf16),
            pltpu.VMEM((width, TILE), bf16),
            pltpu.VMEM((width, TILE), bf16),
            pltpu.VMEM((TILE, width), f32),
            pltpu.VMEM((TILE, width), f32),
            pltpu.VMEM((width, hidden), f32),
        ],
        compiler_params=params(),
        cost_estimate=pl.CostEstimate(
            flops=2 * slot * width * (3 * width + 6 * hidden),
            bytes_accessed=slot * width * 14,
            transcendentals=slot * hidden,
        ),
        name="ffn",
    )(x, dy, o_t, norms, w_o, w_in, w_out)


def project_back_kernel(
    lens, x_ref, dx_ref, dq_ref, dk_ref, dv_ref, du_ref, norms_ref, wq_ref, wk_ref, wv_ref,
    g_sort_ref, g_two_ref, grad_ref, gq_ref, gk_ref, gv_ref, g_norm_ref, *, slot,
):
    tile, width = x_ref.shape
    step = pl.program_id(0)

    @pl.when(step == 0)
    def _():
        gq_ref[...] = jnp.zeros_like(gq_ref)
        gk_ref[...] = jnp.zeros_like(gk_ref)
        gv_ref[...] = jnp.zeros_like(gv_ref)
        g_norm_ref[...] = jnp.zeros_like(g_norm_ref)

    hat, rstd = norm_stats(x_ref[...].astype(f32))
    h_t = (hat * norms_ref[0:1, :] + norms_ref[1:2, :]).astype(bf16).T
    blocks = tile // BLOCK
    places = step * tile + iota((tile, 1), 0)
    live = places < end_at(places, ends_of(lens, slot), slot)
    d_h = jnp.broadcast_to(du_ref[...].reshape(blocks, 1, width), (blocks, BLOCK, width))
    d_h = jnp.where(live, d_h.reshape(tile, width), 0.0)
    for ref, w_ref, g_ref in (
        (dq_ref, wq_ref, gq_ref),
        (dk_ref, wk_ref, gk_ref),
        (dv_ref, wv_ref, gv_ref),
    ):
        d_part = ref[...]
        d_h = d_h + dot_nt(d_part, w_ref[:, :width])
        g_ref[:, :width] += dot(h_t, d_part)
    g_norm_ref[0:1, :] += jnp.sum(d_h * hat, axis=0, keepdims=True)
    g_norm_ref[1:2, :] += jnp.sum(d_h, axis=0, keepdims=True)
    grad_ref[...] = dx_ref[...] + norm_back(d_h, hat, rstd, norms_ref[0:1, :])

    @pl.when(step == pl.num_programs(0) - 1)
    def _():
        gq_ref[:, width : width + LANES] = g_sort_ref[...]
        small = g_norm_ref[...] + g_two_ref[...]
        rest = jnp.zeros((LANES - small.shape[0], width), f32)
        gq_ref[:, width + LANES :] = jnp.concatenate([small, rest], axis=0).T


def project_back(lens, x, d_x, d_q, d_k, d_v, d_u, norms, w_q, w_k, w_v, g_sort, g_two):
    slot, width = x.shape
    grid = slot // TILE
    row = pl.BlockSpec((TILE, width), lambda i: (i, 0))

    def once(shape):
        return pl.BlockSpec(shape, lambda i: (0, 0), pipeline_mode=pl.Buffered(1))

    return pl.pallas_call(
        functools.partial(project_back_kernel, slot=slot),
        grid=(grid,),
        in_specs=[
            smem(), row, row, row, row, row,
            pl.BlockSpec((TILE // BLOCK, width), lambda i: (i, 0)),
            once(norms.shape),
            once(w_q.shape),
            once(w_k.shape),
            once(w_v.shape),
            once(g_sort.shape),
            once(g_two.shape),
        ],
        out_specs=[row, once(w_q.shape), once(w_k.shape), once(w_v.shape)],
        out_shape=[
            jax.ShapeDtypeStruct((slot, width), f32),
            jax.ShapeDtypeStruct(w_q.shape, f32),
            jax.ShapeDtypeStruct(w_k.shape, f32),
            jax.ShapeDtypeStruct(w_v.shape, f32),
        ],
        scratch_shapes=[pltpu.VMEM((8, width), f32)],
        compiler_params=params(),
        cost_estimate=pl.CostEstimate(
            flops=2 * slot * width * 6 * width, bytes_accessed=slot * width * 18, transcendentals=0
        ),
        name="project_back",
    )(lens, x, d_x, d_q, d_k, d_v, d_u, norms, w_q, w_k, w_v, g_sort, g_two)


def orders(count):
    bits = list(range(1, count))
    third = max(len(bits) // 4, 1)
    turns = (0, third, 2 * third)
    return [[0] + bits[t:] + bits[:t] for t in turns]


def gather(block, order, size):
    count = size.bit_length() - 1
    place = lax.axis_index("dp")
    held = block.reshape((1,) * count + block.shape)
    for bit in reversed(order):
        axis = count - 1 - bit
        came = lax.ppermute(held, "dp", [(i, i ^ (1 << bit)) for i in range(size)])
        upper = ((place >> bit) & 1) == 1
        held = jnp.concatenate(
            [jnp.where(upper, came, held), jnp.where(upper, held, came)], axis=axis
        )
    return held.reshape((size * block.shape[0],) + block.shape[1:])


def scatter_sum(value, order, size):
    count = size.bit_length() - 1
    place = lax.axis_index("dp")
    rows = value.shape[0] // size
    held = value.reshape((2,) * count + (rows,) + value.shape[1:])
    for bit in order:
        axis = count - 1 - bit
        mine = (place >> bit) & 1
        sent = lax.dynamic_index_in_dim(held, 1 - mine, axis, keepdims=True).astype(bf16)
        kept = lax.dynamic_index_in_dim(held, mine, axis, keepdims=True)
        came = lax.ppermute(sent, "dp", [(i, i ^ (1 << bit)) for i in range(size)])
        held = kept + came.astype(f32)
    return held.reshape((rows,) + value.shape[1:])


def adamw(weight, grad, moment, square, rate):
    moment = beta_one * moment + (1.0 - beta_one) * grad
    square = beta_two * square + (1.0 - beta_two) * grad * grad
    m_hat = moment / (1.0 - beta_one**STEP)
    s_hat = square / (1.0 - beta_two**STEP)
    weight = weight - rate * (m_hat / (jnp.sqrt(s_hat) + adam_eps) + decay * weight)
    return (weight, moment, square)


def body(size, x, dy, lens, partner, *state):
    slot, width = x.shape
    masters, moments, squares = state[:6], state[6:12], state[12:]
    low = [m.astype(bf16) for m in masters]
    first, second, third = orders(size.bit_length() - 1)
    norm_cols = low[5].shape[1]
    ext = jnp.concatenate(
        [low[0][:, :width], low[2], jnp.pad(low[5], ((0, 0), (0, LANES - norm_cols)))], axis=1
    )
    w_q = gather(ext, first, size)
    w_k = gather(low[0][:, width : 2 * width], second, size)
    w_v = gather(low[0][:, 2 * width :], third, size)
    w_o = gather(low[1], third, size)
    w_in = gather(low[3], first, size)
    w_out = gather(low[4], second, size)

    q, k, v, u, norms = project(lens, x, w_q, w_k, w_v)
    bias, steps = sort_net(lens, u, w_q, partner, slot)
    o_t, probs = attend(lens, partner, bias, q, k, v)
    out, d_x, d_o, g_attn, g_in, g_out, g_two = ffn(x, dy, o_t, norms, w_o, w_in, w_out)
    s_out = scatter_sum(g_out, first, size)
    s_in = scatter_sum(g_in, second, size)
    s_attn = scatter_sum(g_attn, third, size)
    d_q, d_k, d_v, d_bias = attend_back(partner, q, d_o, probs, k, v)
    d_u, g_sort = sort_back(lens, u, w_q, partner, d_bias, steps, slot)
    grad_in, g_q, g_k, g_v = project_back(
        lens, x, d_x, d_q, d_k, d_v, d_u, norms, w_q, w_k, w_v, g_sort, g_two
    )
    s_q = scatter_sum(g_q, first, size)
    s_k = scatter_sum(g_k, second, size)
    s_v = scatter_sum(g_v, third, size)
    grads = (
        jnp.concatenate([s_q[:, :width], s_k, s_v], axis=1),
        s_attn,
        s_q[:, width : width + LANES],
        s_in,
        s_out,
        s_q[:, width + LANES : width + LANES + norm_cols],
    )
    result = [out, grad_in]
    for i in range(6):
        result.extend(adamw(masters[i], grads[i], moments[i], squares[i], rates[i]))
    return tuple(result)


def solution(mesh):
    spec = P("dp", None)
    return jax.shard_map(
        functools.partial(body, mesh.shape["dp"]),
        mesh=mesh,
        in_specs=(spec,) * 22,
        out_specs=(spec,) * 20,
        check_vma=False,
    )
```

time: 2030 us -> 428 us (0.21)
  waiting for transfers between devices: 741 us -> 58.6 us
  matrix products: 435 us -> 0 us
  local copies, waits for them, and re-layouts: 373 us -> 34.6 us
  other arithmetic: 331 us -> 35.8 us
  Pallas kernels: 0 us -> 240 us
  blocking collectives: 122 us -> 0 us
  starting transfers between devices: 0.37 us -> 56.2 us
    reduce_scatter x5 -> x0, waiting for transfers between devices: 642 us -> none  [the longest x1 141 us: body(): lax.psum_scatter(grad_ffn_in, 'dp', scatter_dimension=0, tiled=True)]
    dot_general x33 -> x0, matrix products: 435 us -> none  [the longest x3 77.6 us: sorted_attention(): jnp.einsum('bhqk,bkhd->bqhd', probs[..., BLOCK:], v_far, precision=blockw...]
    pallas_call x0 -> x7, Pallas kernels: none -> 240 us  [the longest x1 89.5 us: ffn(): pl.pallas_call(ffn_kernel, grid=(grid,), in_specs=[row, row, pl.BlockSpec...]
    reduce_sum x47 -> x0, other arithmetic: 146 us -> none  [the longest x1 37.1 us: sorted_attention(): top = jnp.max(scores, axis=3, keepdims=True)]
    all_gather x3 -> x0, blocking collectives: 122 us -> none  [the longest x1 43.2 us: body(): lax.all_gather(shards[5], 'dp', axis=0, tiled=True)]
    reshape x10 -> x1, local copies, waits for them, and re-layouts: 116 us -> 0.01 us  [gather(): held = block.reshape((1,) * count + block.shape)]
    transpose x4 -> x0, local copies, waits for them, and re-layouts: 82.7 us -> none  [the longest x1 21.5 us: sorted_attention(): jnp.einsum('bqhd,bkhd->bhqk', q_blocks, k_far, precision=blockwise) * scale]
    scatter-add x2 -> x0, other arithmetic: 75.8 us -> none  [the longest x1 37.9 us: sorted_attention(): k_far = jnp.take(k_blocks, partner, axis=0)]
  transfers between devices with their start and end apart: 9 -> 60, of which waited for: 7 -> 22; matrix products, arithmetic and copies ran while one was open for 22% -> 14% of each run, Pallas kernels for 0% -> 35%
where the time goes in v1:
time: 428 us; the launch traced here: 427 us
  Pallas kernels  240 us (56%)
  waiting for transfers between devices  58.6 us (14%)
  starting transfers between devices  56.2 us (13%)
  other arithmetic  35.8 us (8%)
  local copies, waits for them, and re-layouts  34.6 us (8%)
    pallas_call x1, Pallas kernels, ffn(): pl.pallas_call(ffn_kernel, grid=(grid,), in_specs=[row, row, pl.BlockSpec...  89.5 us
    pallas_call x1, Pallas kernels, attend_back(): pl.pallas_call(attend_back_kernel, grid=(grid,), in_specs=[smem(), row, r...  56.1 us
    ppermute x30, waiting for transfers between devices, scatter_sum(): came = lax.ppermute(sent, 'dp', [(i, i ^ 1 << bit) for i in range(size)])  51.3 us
    pallas_call x1, Pallas kernels, attend(): pl.pallas_call(functools.partial(attend_kernel, slot=slot), grid=(grid,),...  48.2 us
    ppermute x30, starting transfers between devices, gather(): came = lax.ppermute(held, 'dp', [(i, i ^ 1 << bit) for i in range(size)])  34.6 us
    pallas_call x1, Pallas kernels, project_back(): pl.pallas_call(functools.partial(project_back_kernel, slot=slot), grid=(g...  24.1 us
    ppermute x30, starting transfers between devices, scatter_sum(): came = lax.ppermute(sent, 'dp', [(i, i ^ 1 << bit) for i in range(size)])  21.6 us
    add x24, other arithmetic, scatter_sum(): held = kept + came.astype(f32)  15.8 us
  transfers between devices with their start and end apart: 60, of which 22 were waited for; matrix products, arithmetic and copies ran while one was open for 14% of the time, Pallas kernels for 35%

profile of v1, /device:TPU:0, one launch (start us, length us, event | category | flops | bytes accessed | tf_op | source)
XLA Modules:
  0.0 427.2 jit_solution(15602311821544044523)
XLA Ops:
  1.6 3.0 collective-permute-start.25
  5.5 2.6 collective-permute-start.20
  29.9 3.0 collective-permute-start.7
  58.6 13.2 %project.1 = (bf16[4096,512]{1,0:T(8,128)(2,1)}, bf16[4096,512]{1,0:T(8,128)(2,1)}, bf16[4096,512]{1,0:T(8,128)(2,1)}, f32[128,512]{1,0:T(8,128)}, f32[8,512]{1,0:T(8,128)}) custom-call(s32[1,4]{1,0:T(1,128)} %lens.9, bf16[4096,512]{1,0:T(8,128)(2,1)} %x_ref.5, bf16[512,768]{1,0:T(8,128)(2,1)} %bitcast.69, bf16[512,512]{1,0:T(8,128)(2,1)} %bitcast.89, ...), custom_call_target="tpu_custom_call" | custom-call | flops 6442450944 | bytes 16777216 | tf_op jit(solution)/shard_map/project/pallas_call | solution.py:122
  71.7 4.8 %sort_net.1 = (f32[1,128]{1,0:T(1,128)}, f32[16,128,128]{2,1,0:T(8,128)}) custom-call(s32[1,4]{1,0:T(1,128)} %lens.9, f32[128,512]{1,0:T(8,128)} %get-tuple-element.46.u_ref, bf16[512,768]{1,0:T(8,128)(2,1)} %bitcast.70, s32[1,128]{1,0:T(1,128)} %partner_ref.3), custom_call_target="tpu_custom_call" | custom-call | flops 100000000 | bytes 10000000 | tf_op jit(solution)/shard_map/sort_net/pallas_call | solution.py:205
  77.6 48.2 %attend.1 = (bf16[512,4096]{1,0:T(8,128)(2,1)}, bf16[8192,256]{1,0:T(8,128)(2,1)}) custom-call(s32[1,4]{1,0:T(1,128)} %lens.9, s32[1,128]{1,0:T(1,128)} %partner_ref.3, f32[1,128]{1,0:T(1,128)} %get-tuple-element.47.bias, bf16[4096,512]{1,0:T(8,128)(2,1)} %get-tuple-element.48.q_ref, bf16[4096,512]{1,0:T(8,128)(2,1)} %get-tuple-element.49.k_ref, ...), custom_call_target="tpu_custom_call" | custom-call | flops 20000000000 | bytes 20971520 | tf_op jit(solution)/shard_map/attend/pallas_call | solution.py:382
  129.1 89.5 %ffn.1 = (bf16[4096,512]{1,0:T(8,128)(2,1)}, f32[4096,512]{1,0:T(8,128)}, bf16[4096,512]{1,0:T(8,128)(2,1)}, f32[512,512]{1,0:T(8,128)}, f32[512,2048]{1,0:T(8,1...) custom-call(bf16[4096,512]{1,0:T(8,128)(2,1)} %x_ref.5, bf16[4096,512]{1,0:T(8,128)(2,1)} %dy_ref.1, ...), custom_call_target="tpu_custom_call" | custom-call | flops 57982058496 | bytes 29360128 | tf_op jit(solution)/shard_map/ffn/pallas_call | solution.py:595
  218.6 2.8 dynamic-slice_convert_fusion.1
  221.5 2.7 dynamic-slice_convert_fusion.2
  225.5 56.1 %attend_back.1 = (bf16[4096,512]{1,0:T(8,128)(2,1)}, bf16[4096,512]{1,0:T(8,128)(2,1)}, bf16[4096,512]{1,0:T(8,128)(2,1)}, f32[1,128]{1,0:T(1,128)}) custom-call(s32[1,128]{1,0:T(1,128)} %partner_ref.3, bf16[4096,512]{1,0:T(8,128)(2,1)} %get-tuple-element.48.q_ref, bf16[4096,512]{1,0:T(8,128)(2,1)} %get-tuple-element.55.do_ref, ...), custom_call_target="tpu_custom_call" | custom-call | flops 40000000000 | bytes 33554432 | tf_op jit(solution)/shard_map/attend_back/pallas_call | solution.py:497
  281.6 4.2 sort_back.1
  285.8 24.1 %project_back.1 = (f32[4096,512]{1,0:T(8,128)}, f32[512,768]{1,0:T(8,128)}, f32[512,512]{1,0:T(8,128)}, f32[512,512]{1,0:T(8,128)}) custom-call(s32[1,4]{1,0:T(1,128)} %lens.9, bf16[4096,512]{1,0:T(8,128)(2,1)} %x_ref.5, f32[4096,512]{1,0:T(8,128)} %get-tuple-element.54.dx_ref, bf16[4096,512]{1,0:T(8,128)(2,1)} %get-tuple-element.57.dq_ref, ...), custom_call_target="tpu_custom_call" | custom-call | flops 12884901888 | bytes 37748736 | tf_op jit(solution)/shard_map/project_back/pallas_call | solution.py:692
  313.4 4.0 copy.95
  327.7 3.5 copy.79
  331.1 5.3 %add.293 = f32[2,2,2,2,1,16,768]{5,6,4,3,2,1,0:T(8,128)S(1)} add(f32[2,2,2,2,1,16,768]{5,6,4,3,2,1,0:T(8,128)} %copy.95, f32[2,2,2,2,1,16,768]{5,6,4,3,2,1,0:T(8,128)} %copy.79) | non-fusion elementwise | flops 196608 | bytes 2359296 | tf_op jit(solution)/shard_map/add | solution.py:753
  336.4 2.6 copy-done
  347.3 2.7 collective-permute-done.42
  352.4 2.7 collective-permute-done.38
  366.2 3.4 collective-permute-done.32
  372.3 9.3 %collective-permute-done.33 = bf16[2,1,1,1,1,16,768]{5,6,4,3,2,1,0:T(8,128)(2,1)S(1)} collective-permute-done((bf16[2,1,1,1,1,16,768]{5,6,4,3,2,1,0:T(8,128)(2,1)S(1)}, bf16[2,1,1,1,1,16,768]{5,6,4,3,2,1,0:T(8,128)(2,1)S(1)}, u32[]{:S(2)}, u32[]{:S(2)}) %collective-permute-start.33) | collective-permute-done | bytes 49184 | tf_op jit(solution)/shard_map/ppermute | solution.py:752
  382.8 7.7 %collective-permute-done.34 = bf16[1,1,1,1,1,16,768]{5,6,4,3,2,1,0:T(8,128)(2,1)S(1)} collective-permute-done((bf16[1,1,1,1,1,16,768]{5,6,4,3,2,1,0:T(8,128)(2,1)S(1)}, bf16[1,1,1,1,1,16,768]{5,6,4,3,2,1,0:T(8,128)(2,1)S(1)}, u32[]{:S(2)}, u32[]{:S(2)}) %collective-permute-start.34) | collective-permute-done | bytes 24608 | tf_op jit(solution)/shard_map/ppermute | solution.py:752
  400.0 5.2 %collective-permute-done.56 = bf16[2,2,2,1,1,64,512]{6,5,4,3,2,1,0:T(8,128)(2,1)S(1)} collective-permute-done((bf16[2,2,2,1,1,64,512]{6,5,4,3,2,1,0:T(8,128)(2,1)S(1)}, bf16[2,2,2,1,1,64,512]{6,5,4,3,2,1,0:T(8,128)(2,1)S(1)}, u32[]{:S(2)}, u32[]{:S(2)}) %collective-permute-start.56) | collective-permute-done | bytes 524320 | tf_op jit(solution)/shard_map/ppermute | solution.py:752
  408.0 3.9 collective-permute-done.57
  417.6 4.3 %collective-permute-done.53 = bf16[1,1,1,2,1,16,2048]{6,5,4,3,2,1,0:T(8,128)(2,1)S(1)} collective-permute-done((bf16[1,1,1,2,1,16,2048]{6,5,4,3,2,1,0:T(8,128)(2,1)S(1)}, bf16[1,1,1,2,1,16,2048]{6,5,4,3,2,1,0:T(8,128)(2,1)S(1)}, u32[]{:S(2)}, u32[]{:S(2)}) %collective-permute-start.53) | collective-permute-done | bytes 131104 | tf_op jit(solution)/shard_map/ppermute | solution.py:752
  (305 shorter events, 116.5 us)
Async XLA Ops:
  1.6 28.2 %collective-permute-start.25 = (bf16[1,1,1,1,1,64,512]{6,5,4,3,2,1,0:T(8,128)(2,1)S(1)}, bf16[1,1,1,1,1,64,512]{6,5,4,3,2,1,0:T(8,128)(2,1)S(1)}, u32[]{:S(2)}, u32[]{:S(2)}) collective-permute-start(bf16[1,1,1,1,1,64,512]{6,5,4,3,2,1,0:T(8,128)(2,1)S(1)} %convert_bitcast_fusion), channel_id=1, source_target_pairs={{0,2},{1,3},{2,0},{3,1},{4,6},{5,7},{6,4},{7,5},{8,10},{9,11},{10,... | collective-permute-start | bytes 196616 | tf_op jit(solution)/shard_map/ppermute | solution.py:734
  5.5 28.3 %collective-permute-start.20 = (bf16[1,1,1,1,1,16,2048]{6,5,4,3,2,1,0:T(8,128)(2,1)S(1)}, bf16[1,1,1,1,1,16,2048]{6,5,4,3,2,1,0:T(8,128)(2,1)S(1)}, u32[]{:S(2)}, u32[]{:S(2)}) collective-permute-start(bf16[1,1,1,1,1,16,2048]{6,5,4,3,2,1,0:T(8,128)(2,1)S(1)} %convert_bitcast_fusion.1), channel_id=1, source_target_pairs={{0,16},{1,17},{2,18},{3,19},{4,20},{5,21},{6,22},{7,23},{8,24},{9,... | collective-permute-start | bytes 196616 | tf_op jit(solution)/shard_map/ppermute | solution.py:734
  9.0 10.0 %collective-permute-start.10 = (bf16[1,1,1,1,1,16,512]{6,5,4,3,2,1,0:T(8,128)(2,1)S(1)}, bf16[1,1,1,1,1,16,512]{6,5,4,3,2,1,0:T(8,128)(2,1)S(1)}, u32[]{:S(2)}, u32[]{:S(2)}) collective-permute-start(bf16[1,1,1,1,1,16,512]{6,5,4,3,2,1,0:T(8,128)(2,1)S(1)} %get-tuple-element.208), channel_id=1, source_target_pairs={{0,4},{1,5},{2,6},{3,7},{4,0},{5,1},{6,2},{7,3},{8,12},{9,13},{10,... | collective-permute-start | bytes 49160 | tf_op jit(solution)/shard_map/ppermute | solution.py:734
  11.9 9.0 %collective-permute-start.15 = (bf16[1,1,1,1,1,16,512]{6,5,4,3,2,1,0:T(8,128)(2,1)S(1)}, bf16[1,1,1,1,1,16,512]{6,5,4,3,2,1,0:T(8,128)(2,1)S(1)}, u32[]{:S(2)}, u32[]{:S(2)}) collective-permute-start(bf16[1,1,1,1,1,16,512]{6,5,4,3,2,1,0:T(8,128)(2,1)S(1)} %convert_bitcast_fusion.2), channel_id=1, source_target_pairs={{0,4},{1,5},{2,6},{3,7},{4,0},{5,1},{6,2},{7,3},{8,12},{9,13},{10,... | collective-permute-start | bytes 49160 | tf_op jit(solution)/shard_map/ppermute | solution.py:734
  25.0 9.6 %collective-permute-start.1 = (bf16[2,1,1,1,1,16,768]{6,5,4,3,2,1,0:T(8,128)(2,1)S(1)}, bf16[2,1,1,1,1,16,768]{6,5,4,3,2,1,0:T(8,128)(2,1)S(1)}, u32[]{:S(2)}, u32[]{:S(2)}) collective-permute-start(bf16[2,1,1,1,1,16,768]{6,5,4,3,2,1,0:T(8,128)(2,1)S(1)} %pad_maximum_fusion.27), channel_id=1, source_target_pairs={{0,8},{1,9},{2,10},{3,11},{4,12},{5,13},{6,14},{7,15},{8,0},{9,1},... | collective-permute-start | bytes 147464 | tf_op jit(solution)/shard_map/ppermute | solution.py:734
  38.5 9.6 %collective-permute-start.13 = (bf16[2,1,2,2,1,16,512]{6,5,4,3,2,1,0:T(8,128)(2,1)S(1)}, bf16[2,1,2,2,1,16,512]{6,5,4,3,2,1,0:T(8,128)(2,1)S(1)}, u32[]{:S(2)}, u32[]{:S(2)}) collective-permute-start(bf16[2,1,2,2,1,16,512]{6,5,4,3,2,1,0:T(8,128)(2,1)S(1)} %pad_maximum_fusion.18), channel_id=1, source_target_pairs={{0,8},{1,9},{2,10},{3,11},{4,12},{5,13},{6,14},{7,15},{8,0},{9,1},... | collective-permute-start | bytes 393224 | tf_op jit(solution)/shard_map/ppermute | solution.py:734
  51.7 24.9 %collective-permute-start.28 = (bf16[2,2,1,2,1,64,512]{6,5,4,3,2,1,0:T(8,128)(2,1)S(1)}, bf16[2,2,1,2,1,64,512]{6,5,4,3,2,1,0:T(8,128)(2,1)S(1)}, u32[]{:S(2)}, u32[]{:S(2)}) collective-permute-start(bf16[2,2,1,2,1,64,512]{6,5,4,3,2,1,0:T(8,128)(2,1)S(1)} %pad_maximum_fusion.9), channel_id=1, source_target_pairs={{0,4},{1,5},{2,6},{3,7},{4,0},{5,1},{6,2},{7,3},{8,12},{9,13},{10,... | collective-permute-start | bytes 1572872 | tf_op jit(solution)/shard_map/ppermute | solution.py:734
  53.3 23.5 %collective-permute-start.23 = (bf16[2,2,2,1,1,16,2048]{6,5,4,3,2,1,0:T(8,128)(2,1)S(1)}, bf16[2,2,2,1,1,16,2048]{6,5,4,3,2,1,0:T(8,128)(2,1)S(1)}, u32[]{:S(2)}, u32[]{:S(2)}) collective-permute-start(bf16[2,2,2,1,1,16,2048]{6,5,4,3,2,1,0:T(8,128)(2,1)S(1)} %pad_maximum_fusion.8), channel_id=1, source_target_pairs={{0,2},{1,3},{2,0},{3,1},{4,6},{5,7},{6,4},{7,5},{8,10},{9,11},{10,... | collective-permute-start | bytes 1572872 | tf_op jit(solution)/shard_map/ppermute | solution.py:734
  76.8 49.1 %collective-permute-start.29 = (bf16[2,2,2,2,1,64,512]{6,5,4,3,2,1,0:T(8,128)(2,1)S(1)}, bf16[2,2,2,2,1,64,512]{6,5,4,3,2,1,0:T(8,128)(2,1)S(1)}, u32[]{:S(2)}, u32[]{:S(2)}) collective-permute-start(bf16[2,2,2,2,1,64,512]{6,5,4,3,2,1,0:T(8,128)(2,1)S(1)} %pad_maximum_fusion.3), channel_id=1, source_target_pairs={{0,1},{1,0},{2,3},{3,2},{4,5},{5,4},{6,7},{7,6},{8,9},{9,8},{10,11... | collective-permute-start | bytes 3145736 | tf_op jit(solution)/shard_map/ppermute | solution.py:734
  77.0 50.4 %collective-permute-start.24 = (bf16[2,2,2,2,1,16,2048]{6,5,4,3,2,1,0:T(8,128)(2,1)S(1)}, bf16[2,2,2,2,1,16,2048]{6,5,4,3,2,1,0:T(8,128)(2,1)S(1)}, u32[]{:S(2)}, u32[]{:S(2)}) collective-permute-start(bf16[2,2,2,2,1,16,2048]{6,5,4,3,2,1,0:T(8,128)(2,1)S(1)} %pad_maximum_fusion.2), channel_id=1, source_target_pairs={{0,1},{1,0},{2,3},{3,2},{4,5},{5,4},{6,7},{7,6},{8,9},{9,8},{10,11... | collective-permute-start | bytes 3145736 | tf_op jit(solution)/shard_map/ppermute | solution.py:734
  221.5 172.0 %collective-permute-start.55 = (bf16[2,2,2,2,1,64,512]{6,5,4,3,2,1,0:T(8,128)(2,1)}, bf16[2,2,2,2,1,64,512]{6,5,4,3,2,1,0:T(8,128)(2,1)}, u32[]{:S(2)}, u32[]{:S(2)}) collective-permute-start(bf16[2,2,2,2,1,64,512]{6,5,4,3,2,1,0:T(8,128)(2,1)} %dynamic-slice_convert_fusion.1), channel_id=1, source_target_pairs={{0,1},{1,0},{2,3},{3,2},{4,5},{5,4},{6,7},{7,6},{8,9},{9,8},{10,11... | collective-permute-start | bytes 3145736 | tf_op jit(solution)/shard_map/ppermute | solution.py:752
  224.2 172.5 %collective-permute-start.50 = (bf16[2,2,2,2,1,16,2048]{6,5,4,3,2,1,0:T(8,128)(2,1)}, bf16[2,2,2,2,1,16,2048]{6,5,4,3,2,1,0:T(8,128)(2,1)}, u32[]{:S(2)}, u32[]{:S(2)}) collective-permute-start(bf16[2,2,2,2,1,16,2048]{6,5,4,3,2,1,0:T(8,128)(2,1)} %dynamic-slice_convert_fusion.2), channel_id=1, source_target_pairs={{0,1},{1,0},{2,3},{3,2},{4,5},{5,4},{6,7},{7,6},{8,9},{9,8},{10,11... | collective-permute-start | bytes 3145736 | tf_op jit(solution)/shard_map/ppermute | solution.py:752
  225.4 93.4 %collective-permute-start.45 = (bf16[2,2,2,2,1,16,512]{6,5,4,3,2,1,0:T(8,128)(2,1)}, bf16[2,2,2,2,1,16,512]{6,5,4,3,2,1,0:T(8,128)(2,1)S(1)}, u32[]{:S(2)}, u32[]{:S(2)}) collective-permute-start(bf16[2,2,2,2,1,16,512]{6,5,4,3,2,1,0:T(8,128)(2,1)} %dynamic-slice_convert_fusion.10), channel_id=1, source_target_pairs={{0,1},{1,0},{2,3},{3,2},{4,5},{5,4},{6,7},{7,6},{8,9},{9,8},{10,11... | collective-permute-start | bytes 786440 | tf_op jit(solution)/shard_map/ppermute | solution.py:752
  311.9 15.2 %collective-permute-start.30 = (bf16[2,2,2,2,1,16,768]{6,5,4,3,2,1,0:T(8,128)(2,1)}, bf16[2,2,2,2,1,16,768]{6,5,4,3,2,1,0:T(8,128)(2,1)S(1)}, u32[]{:S(2)}, u32[]{:S(2)}) collective-permute-start(bf16[2,2,2,2,1,16,768]{6,5,4,3,2,1,0:T(8,128)(2,1)} %dynamic-slice_convert_fusion.7), channel_id=1, source_target_pairs={{0,1},{1,0},{2,3},{3,2},{4,5},{5,4},{6,7},{7,6},{8,9},{9,8},{10,11... | collective-permute-start | bytes 1179656 | tf_op jit(solution)/shard_map/ppermute | solution.py:752
  321.5 18.4 %collective-permute-start.36 = (bf16[2,2,1,2,1,16,512]{6,5,4,3,2,1,0:T(8,128)(2,1)}, bf16[2,2,1,2,1,16,512]{6,5,4,3,2,1,0:T(8,128)(2,1)}, u32[]{:S(2)}, u32[]{:S(2)}) collective-permute-start(bf16[2,2,1,2,1,16,512]{6,5,4,3,2,1,0:T(8,128)(2,1)} %dynamic-slice_convert_fusion.18), channel_id=1, source_target_pairs={{0,4},{1,5},{2,6},{3,7},{4,0},{5,1},{6,2},{7,3},{8,12},{9,13},{10,... | collective-permute-start | bytes 393224 | tf_op jit(solution)/shard_map/ppermute | solution.py:752
  325.0 17.1 %collective-permute-start.41 = (bf16[2,1,2,2,1,16,512]{6,5,4,3,2,1,0:T(8,128)(2,1)}, bf16[2,1,2,2,1,16,512]{6,5,4,3,2,1,0:T(8,128)(2,1)}, u32[]{:S(2)}, u32[]{:S(2)}) collective-permute-start(bf16[2,1,2,2,1,16,512]{6,5,4,3,2,1,0:T(8,128)(2,1)} %dynamic-slice_convert_fusion.17), channel_id=1, source_target_pairs={{0,8},{1,9},{2,10},{3,11},{4,12},{5,13},{6,14},{7,15},{8,0},{9,1},... | collective-permute-start | bytes 393224 | tf_op jit(solution)/shard_map/ppermute | solution.py:752
  327.1 17.0 %collective-permute-start.47 = (bf16[1,1,2,2,1,16,512]{6,5,4,3,2,1,0:T(8,128)(2,1)}, bf16[1,1,2,2,1,16,512]{6,5,4,3,2,1,0:T(8,128)(2,1)S(1)}, u32[]{:S(2)}, u32[]{:S(2)}) collective-permute-start(bf16[1,1,2,2,1,16,512]{6,5,4,3,2,1,0:T(8,128)(2,1)} %dynamic-slice_convert_fusion.21), channel_id=1, source_target_pairs={{0,16},{1,17},{2,18},{3,19},{4,20},{5,21},{6,22},{7,23},{8,24},{9,... | collective-permute-start | bytes 196616 | tf_op jit(solution)/shard_map/ppermute | solution.py:752
  339.9 16.9 %collective-permute-start.31 = (bf16[2,2,2,1,1,16,768]{6,5,4,3,2,1,0:T(8,128)(2,1)S(1)}, bf16[2,2,2,1,1,16,768]{6,5,4,3,2,1,0:T(8,128)(2,1)S(1)}, u32[]{:S(2)}, u32[]{:S(2)}) collective-permute-start(bf16[2,2,2,1,1,16,768]{6,5,4,3,2,1,0:T(8,128)(2,1)S(1)} %copy.80), channel_id=1, source_target_pairs={{0,2},{1,3},{2,0},{3,1},{4,6},{5,7},{6,4},{7,5},{8,10},{9,11},{10,... | collective-permute-start | bytes 589832 | tf_op jit(solution)/shard_map/ppermute | solution.py:752
  355.1 9.9 %collective-permute-start.49 = (bf16[1,1,1,1,1,16,512]{6,5,4,3,2,1,0:T(8,128)(2,1)S(1)}, bf16[1,1,1,1,1,16,512]{6,5,4,3,2,1,0:T(8,128)(2,1)S(1)}, u32[]{:S(2)}, u32[]{:S(2)}) collective-permute-start(bf16[1,1,1,1,1,16,512]{6,5,4,3,2,1,0:T(8,128)(2,1)S(1)} %dynamic-slice_convert_fusion.27), channel_id=1, source_target_pairs={{0,4},{1,5},{2,6},{3,7},{4,0},{5,1},{6,2},{7,3},{8,12},{9,13},{10,... | collective-permute-start | bytes 49160 | tf_op jit(solution)/shard_map/ppermute | solution.py:752
  355.7 16.6 %collective-permute-start.39 = (bf16[1,1,1,1,1,16,512]{6,5,4,3,2,1,0:T(8,128)(2,1)S(1)}, bf16[1,1,1,1,1,16,512]{6,5,4,3,2,1,0:T(8,128)(2,1)S(1)}, u32[]{:S(2)}, u32[]{:S(2)}) collective-permute-start(bf16[1,1,1,1,1,16,512]{6,5,4,3,2,1,0:T(8,128)(2,1)S(1)} %dynamic-slice_convert_fusion.29), channel_id=1, source_target_pairs={{0,2},{1,3},{2,0},{3,1},{4,6},{5,7},{6,4},{7,5},{8,10},{9,11},{10,... | collective-permute-start | bytes 49160 | tf_op jit(solution)/shard_map/ppermute | solution.py:752
  357.4 25.4 %collective-permute-start.44 = (bf16[1,1,1,1,1,16,512]{6,5,4,3,2,1,0:T(8,128)(2,1)S(1)}, bf16[1,1,1,1,1,16,512]{6,5,4,3,2,1,0:T(8,128)(2,1)S(1)}, u32[]{:S(2)}, u32[]{:S(2)}) collective-permute-start(bf16[1,1,1,1,1,16,512]{6,5,4,3,2,1,0:T(8,128)(2,1)S(1)} %dynamic-slice_convert_fusion.28), channel_id=1, source_target_pairs={{0,4},{1,5},{2,6},{3,7},{4,0},{5,1},{6,2},{7,3},{8,12},{9,13},{10,... | collective-permute-start | bytes 49160 | tf_op jit(solution)/shard_map/ppermute | solution.py:752
  371.7 9.9 %collective-permute-start.33 = (bf16[2,1,1,1,1,16,768]{5,6,4,3,2,1,0:T(8,128)(2,1)S(1)}, bf16[2,1,1,1,1,16,768]{5,6,4,3,2,1,0:T(8,128)(2,1)S(1)}, u32[]{:S(2)}, u32[]{:S(2)}) collective-permute-start(bf16[2,1,1,1,1,16,768]{5,6,4,3,2,1,0:T(8,128)(2,1)S(1)} %dynamic-slice_convert_fusion.6), channel_id=1, source_target_pairs={{0,8},{1,9},{2,10},{3,11},{4,12},{5,13},{6,14},{7,15},{8,0},{9,1},... | collective-permute-start | bytes 147464 | tf_op jit(solution)/shard_map/ppermute | solution.py:752
  396.0 9.2 %collective-permute-start.56 = (bf16[2,2,2,1,1,64,512]{6,5,4,3,2,1,0:T(8,128)(2,1)S(1)}, bf16[2,2,2,1,1,64,512]{6,5,4,3,2,1,0:T(8,128)(2,1)S(1)}, u32[]{:S(2)}, u32[]{:S(2)}) collective-permute-start(bf16[2,2,2,1,1,64,512]{6,5,4,3,2,1,0:T(8,128)(2,1)S(1)} %dynamic-slice_convert_fusion.4), channel_id=1, source_target_pairs={{0,2},{1,3},{2,0},{3,1},{4,6},{5,7},{6,4},{7,5},{8,10},{9,11},{10,... | collective-permute-start | bytes 1572872 | tf_op jit(solution)/shard_map/ppermute | solution.py:752
  398.5 9.2 %collective-permute-start.51 = (bf16[2,2,1,2,1,16,2048]{6,5,4,3,2,1,0:T(8,128)(2,1)S(1)}, bf16[2,2,1,2,1,16,2048]{6,5,4,3,2,1,0:T(8,128)(2,1)S(1)}, u32[]{:S(2)}, u32[]{:S(2)}) collective-permute-start(bf16[2,2,1,2,1,16,2048]{6,5,4,3,2,1,0:T(8,128)(2,1)S(1)} %dynamic-slice_convert_fusion.5), channel_id=1, source_target_pairs={{0,4},{1,5},{2,6},{3,7},{4,0},{5,1},{6,2},{7,3},{8,12},{9,13},{10,... | collective-permute-start | bytes 1572872 | tf_op jit(solution)/shard_map/ppermute | solution.py:752
  (63 other events, 547.9 us)

commit v2 on v1

v2 whole, which is shorter than its diff:
```python
import functools
import math

import jax
import jax.numpy as jnp
from jax import lax
from jax.experimental import pallas as pl
from jax.experimental.pallas import tpu as pltpu
from jax.sharding import PartitionSpec as P

HEADS = 8
HEAD = 64
SORT = 64
BLOCK = 32
SINK = 8
STEP = 10
TILE = 512
WIDE = 1024
ROWS = 16
ABREAST = 4
SUB = 256
GROUP = 128
LANES = 128

highest = lax.Precision.HIGHEST
masked = -1000000000.0
norm_eps = 1e-05
beta_one = 0.9
beta_two = 0.999
adam_eps = 1e-08
decay = 0.01
rates = (0.05, 0.15, 0.05, 0.05, 0.025, 0.5)
f32 = jnp.float32
bf16 = jnp.bfloat16


def dot(left, right, precision=None):
    return jnp.dot(left, right, precision=precision, preferred_element_type=f32)


def dot_nt(left, right, precision=None):
    return lax.dot_general(
        left, right, (((1,), (1,)), ((), ())), precision=precision, preferred_element_type=f32
    )


def dot_tn(left, right, precision=None):
    return lax.dot_general(
        left, right, (((0,), (0,)), ((), ())), precision=precision, preferred_element_type=f32
    )


def iota(shape, axis):
    return lax.broadcasted_iota(jnp.int32, shape, axis)


def ends_of(lens, slot):
    quarter = slot // 4
    is_long = lens[0, 0] > quarter
    return [jnp.where(is_long, lens[0, 0], k * quarter + lens[0, k]) for k in range(4)]


def end_at(places, ends, slot):
    quarter = slot // 4
    return jnp.where(
        places < 2 * quarter,
        jnp.where(places < quarter, ends[0], ends[1]),
        jnp.where(places < 3 * quarter, ends[2], ends[3]),
    )


def norm_stats(value):
    center = value - jnp.mean(value, axis=-1, keepdims=True)
    spread = jnp.mean(center * center, axis=-1, keepdims=True)
    rstd = lax.rsqrt(spread + norm_eps)
    return center * rstd, rstd


def norm_back(grad, hat, rstd, gain):
    d_hat = grad * gain
    mean_d = jnp.mean(d_hat, axis=-1, keepdims=True)
    mean_dh = jnp.mean(d_hat * hat, axis=-1, keepdims=True)
    return rstd * (d_hat - mean_d - hat * mean_dh)


def params(limit=56 << 20):
    return pltpu.CompilerParams(vmem_limit_bytes=limit)


def whole(shape):
    return pl.BlockSpec(shape, lambda *_: (0,) * len(shape))


def smem():
    return pl.BlockSpec(memory_space=pltpu.SMEM)


def project_kernel(lens, x_ref, w_ref, q_ref, k_ref, v_ref, u_ref, norms_ref, *, slot):
    tile, width = x_ref.shape
    base = pl.program_id(0) * tile

    @pl.when(pl.program_id(0) == 0)
    def _():
        norms_ref[...] = w_ref[:, 3 * width + LANES :].astype(f32).T[:8, :]

    parts = []
    for r in range(0, tile, SUB):
        hat, _ = norm_stats(x_ref[r : r + SUB, :].astype(f32))
        parts.append((hat * norms_ref[0:1, :] + norms_ref[1:2, :]).astype(bf16))
        for part, ref in enumerate((q_ref, k_ref, v_ref)):
            ref[r : r + SUB, :] = dot(parts[-1], w_ref[:, part * width : (part + 1) * width]).astype(bf16)
    h_one = jnp.concatenate(parts, axis=0)
    blocks = tile // BLOCK
    at = iota((blocks, tile), 1)
    places = at + base
    live = places < end_at(places, ends_of(lens, slot), slot)
    own = (at // BLOCK) == iota((blocks, tile), 0)
    pick = jnp.where(live & own, 1.0, 0.0).astype(bf16)
    u_ref[...] = dot(pick, h_one)


def project(lens, x, w_one):
    slot, width = x.shape
    grid = slot // WIDE
    row = pl.BlockSpec((WIDE, width), lambda i: (i, 0))
    out = jax.ShapeDtypeStruct((slot, width), bf16)
    return pl.pallas_call(
        functools.partial(project_kernel, slot=slot),
        grid=(grid,),
        in_specs=[smem(), row, whole(w_one.shape)],
        out_specs=[
            row,
            row,
            row,
            pl.BlockSpec((WIDE // BLOCK, width), lambda i: (i, 0)),
            whole((8, width)),
        ],
        out_shape=[
            out,
            out,
            out,
            jax.ShapeDtypeStruct((slot // BLOCK, width), f32),
            jax.ShapeDtypeStruct((8, width), f32),
        ],
        compiler_params=params(),
        cost_estimate=pl.CostEstimate(
            flops=2 * slot * width * 3 * width, bytes_accessed=slot * width * 8, transcendentals=0
        ),
        name="project",
    )(lens, x, w_one)


def sort_parts(lens, u_ref, ws_ref, slot):
    blocks = u_ref.shape[0]
    ends = ends_of(lens, slot)
    quarter = slot // 4
    is_long = lens[0, 0] > quarter

    def group_of(axis, shape):
        index = iota(shape, axis)
        start = index * BLOCK
        live = start < end_at(start, ends, slot)
        member = jnp.where(is_long, 0, start // quarter)
        return jnp.where(live, member, 4 + index)

    same = group_of(0, (blocks, blocks)) == group_of(1, (blocks, blocks))
    start = iota((blocks, 1), 0) * BLOCK
    count = jnp.clip(end_at(start, ends, slot) - start, 0, BLOCK).astype(f32)
    scale = lax.rsqrt(jnp.maximum(count, 1.0))
    summary = u_ref[...] * scale
    w_sort = ws_ref[...].astype(f32)
    sort_q = dot(summary, w_sort[:, :SORT], highest)
    sort_k = dot(summary, w_sort[:, SORT:], highest)
    return same, scale, summary, w_sort, sort_q, sort_k


def sort_columns(w_one):
    return pl.BlockSpec((w_one.shape[0], 2 * SORT), lambda i: (0, 3 * w_one.shape[0] // (2 * SORT)))


def column_of(row, eye):
    return jnp.sum(jnp.where(eye, row, 0.0), axis=1, keepdims=True)


def sort_kernel(lens, u_ref, ws_ref, partner_ref, bias_ref, steps_ref, *, slot):
    blocks = u_ref.shape[0]
    same, _, _, _, sort_q, sort_k = sort_parts(lens, u_ref, ws_ref, slot)
    raw = dot_nt(sort_q, sort_k, highest)
    logits = jnp.where(same, raw / math.sqrt(SORT), masked)

    def normalize(value, axis):
        top = jnp.max(value, axis=axis, keepdims=True)
        return value - (top + jnp.log(jnp.sum(jnp.exp(value - top), axis=axis, keepdims=True)))

    for turn in range(SINK):
        logits = normalize(logits, 1)
        steps_ref[2 * turn] = logits
        logits = normalize(logits, 0)
        steps_ref[2 * turn + 1] = logits
    eye = iota((blocks, blocks), 0) == iota((blocks, blocks), 1)
    members = jnp.sum(same.astype(f32), axis=1, keepdims=True)
    partner = column_of(partner_ref[...].astype(f32), eye)
    pick = partner == iota((blocks, blocks), 1).astype(f32)
    bias = jnp.sum(jnp.where(pick, logits, 0.0), axis=1, keepdims=True) + jnp.log(members)
    bias_ref[...] = jnp.sum(jnp.where(eye, bias, 0.0), axis=0, keepdims=True)


def sort_net(lens, u, w_sort, partner, slot):
    blocks = u.shape[0]
    return pl.pallas_call(
        functools.partial(sort_kernel, slot=slot),
        in_specs=[smem(), whole(u.shape), sort_columns(w_sort), whole(partner.shape)],
        out_specs=[whole((1, blocks)), whole((2 * SINK, blocks, blocks))],
        out_shape=[
            jax.ShapeDtypeStruct((1, blocks), f32),
            jax.ShapeDtypeStruct((2 * SINK, blocks, blocks), f32),
        ],
        grid=(1,),
        compiler_params=params(),
        cost_estimate=pl.CostEstimate(flops=10**8, bytes_accessed=10**7, transcendentals=10**6),
        name="sort_net",
    )(lens, u, w_sort, partner)


def sort_back_kernel(
    lens, u_ref, ws_ref, partner_ref, steps_ref, *refs, slot
):
    *d_bias_refs, d_u_ref, grad_ref = refs
    blocks = u_ref.shape[0]
    same, scale, summary, w_sort, sort_q, sort_k = sort_parts(lens, u_ref, ws_ref, slot)
    eye = iota((blocks, blocks), 0) == iota((blocks, blocks), 1)
    partner = column_of(partner_ref[...].astype(f32), eye)
    pick = partner == iota((blocks, blocks), 1).astype(f32)
    d_bias = column_of(sum(ref[...] for ref in d_bias_refs), eye)
    d_logits = jnp.where(pick, d_bias, 0.0)
    for turn in reversed(range(SINK)):
        for axis, step in ((0, 2 * turn + 1), (1, 2 * turn)):
            share = jnp.exp(steps_ref[step])
            d_logits = d_logits - share * jnp.sum(d_logits, axis=axis, keepdims=True)
    d_raw = jnp.where(same, d_logits, 0.0) / math.sqrt(SORT)
    d_sort_q = dot(d_raw, sort_k, highest)
    d_sort_k = dot_tn(d_raw, sort_q, highest)
    d_sort = jnp.concatenate([d_sort_q, d_sort_k], axis=1)
    grad_ref[...] = dot_tn(summary, d_sort, highest)
    d_u_ref[...] = dot_nt(d_sort, w_sort, highest) * scale


def sort_back(lens, u, w_sort, partner, d_bias, steps, slot):
    blocks, width = u.shape
    return pl.pallas_call(
        functools.partial(sort_back_kernel, slot=slot),
        in_specs=[
            smem(),
            whole(u.shape),
            sort_columns(w_sort),
            whole(partner.shape),
            whole(steps.shape),
            *[whole(part.shape) for part in d_bias],
        ],
        out_specs=[whole((blocks, width)), whole((width, 2 * SORT))],
        out_shape=[
            jax.ShapeDtypeStruct((blocks, width), f32),
            jax.ShapeDtypeStruct((width, 2 * SORT), f32),
        ],
        grid=(1,),
        compiler_params=params(),
        cost_estimate=pl.CostEstimate(flops=10**8, bytes_accessed=10**7, transcendentals=10**6),
        name="sort_back",
    )(lens, u, w_sort, partner, steps, *d_bias)


def lane_block(rows):
    return (iota((rows, 2 * GROUP), 1) % GROUP) // BLOCK


def compact(full):
    at = lane_block(BLOCK)
    part = [full[c * BLOCK : (c + 1) * BLOCK] for c in range(GROUP // BLOCK)]
    return jnp.where(
        at < 2,
        jnp.where(at < 1, part[0], part[1]),
        jnp.where(at < 3, part[2], part[3]),
    )


def diagonal_mask():
    rows = 2 * GROUP
    return jnp.where((iota((rows, rows), 0) % GROUP) // BLOCK == lane_block(rows), 1.0, 0.0).astype(bf16)


def spread(own, far, mask):
    own, far = own.astype(bf16), far.astype(bf16)
    times = GROUP // BLOCK
    return jnp.concatenate([own] * times + [far] * times, axis=0) * mask


def head_stack(pair, lanes):
    zero = jnp.zeros_like(pair)
    return jnp.concatenate(
        [jnp.where(lanes < HEAD, pair, zero), jnp.where(lanes < HEAD, zero, pair)], axis=0
    )


def head_lanes():
    return iota((GROUP, LANES), 1)


def by_lane(values):
    at = iota((1, GROUP), 1) // BLOCK
    return jnp.where(
        at < 2,
        jnp.where(at < 1, values[0], values[1]),
        jnp.where(at < 3, values[2], values[3]),
    )


def gather_far(dst, src, partners):
    for c, p in enumerate(partners):
        dst[GROUP + c * BLOCK : GROUP + (c + 1) * BLOCK, :] = src[pl.ds(pl.multiple_of(p * BLOCK, BLOCK), BLOCK), :]


def attend_kernel(lens, partner, bias, q_ref, k_ref, v_ref, o_ref, p_ref, mask_ref, *, slot):
    tile, width = q_ref.shape
    step = pl.program_id(0)
    pairs = width // LANES
    per = GROUP // BLOCK

    @pl.when(step == 0)
    def _():
        mask_ref[...] = diagonal_mask()

    ends = ends_of(lens, slot)
    scale = 1.0 / math.sqrt(HEAD)

    def some_groups(turn, carry):
        mask = mask_ref[...]
        lanes = head_lanes()
        key = iota((BLOCK, GROUP), 0)
        query = iota((BLOCK, GROUP), 1)
        work = []
        for part in range(ABREAST):
            g = turn * ABREAST + part
            first = step * (tile // BLOCK) + g * per
            partners = [partner[0, first + c] for c in range(per)]
            rows = pl.ds(pl.multiple_of(first * BLOCK, GROUP), GROUP)
            q_rows = pl.ds(pl.multiple_of(g * GROUP, GROUP), GROUP)
            spans = [rows] + [pl.ds(pl.multiple_of(p * BLOCK, BLOCK), BLOCK) for p in partners]
            own_place = (first + query // BLOCK) * BLOCK + key
            far_place = by_lane(partners) * BLOCK + key
            own_live = (own_place < end_at(own_place, ends, slot)) | (query % BLOCK == key)
            far_live = far_place < end_at(far_place, ends, slot)
            own_live = jnp.concatenate([own_live.astype(f32)] * 2, axis=1) > 0.5
            far_live = jnp.concatenate([far_live.astype(f32)] * 2, axis=1) > 0.5
            lane_bias = by_lane([bias[0, first + c] for c in range(per)])
            lane_bias = jnp.concatenate([lane_bias] * 2, axis=1)
            for pair in range(pairs):
                work.append((g, pair, spans, q_rows, own_live, far_live, lane_bias))
        scores = []
        for g, pair, spans, q_rows, *_ in work:
            cols = slice(pair * LANES, (pair + 1) * LANES)
            q_two = head_stack(q_ref[q_rows, cols], lanes)
            k_all = jnp.concatenate([k_ref[at, cols] for at in spans], axis=0)
            scores.append(dot_nt(k_all, q_two))
        probs = []
        for score, (g, pair, spans, q_rows, own_live, far_live, lane_bias) in zip(scores, work):
            own = jnp.where(own_live, compact(score[:GROUP]) * scale, masked)
            far = jnp.where(far_live, compact(score[GROUP:]) * scale + lane_bias, masked)
            top = jnp.maximum(
                jnp.max(own, axis=0, keepdims=True), jnp.max(far, axis=0, keepdims=True)
            )
            own = jnp.exp(own - top)
            far = jnp.exp(far - top)
            total = jnp.sum(own, axis=0, keepdims=True) + jnp.sum(far, axis=0, keepdims=True)
            inverse = 1.0 / total
            probs.append(((own * inverse).astype(bf16), (far * inverse).astype(bf16)))
        mixes = []
        for (own, far), (g, pair, spans, *_) in zip(probs, work):
            cols = slice(pair * LANES, (pair + 1) * LANES)
            v_all = jnp.concatenate([v_ref[at, cols] for at in spans], axis=0)
            mixes.append(dot(v_all.T, spread(own, far, mask)))
        for mixed, (own, far), (g, pair, spans, q_rows, *_) in zip(mixes, probs, work):
            at = pl.multiple_of(g * 2 * BLOCK, 2 * BLOCK)
            p_ref[pair, pl.ds(at, BLOCK), :] = own
            p_ref[pair, pl.ds(at + BLOCK, BLOCK), :] = far
            o_ref[pair * LANES : pair * LANES + HEAD, q_rows] = mixed[:HEAD, :GROUP].astype(bf16)
            o_ref[pair * LANES + HEAD : (pair + 1) * LANES, q_rows] = mixed[HEAD:, GROUP:].astype(bf16)
        return carry

    lax.fori_loop(0, tile // GROUP // ABREAST, some_groups, 0)


def attend(lens, partner, bias, q, k, v):
    slot, width = q.shape
    grid = slot // TILE
    pairs, per_tile = width // LANES, (TILE // GROUP) * 2 * BLOCK
    return pl.pallas_call(
        functools.partial(attend_kernel, slot=slot),
        grid=(grid,),
        in_specs=[
            smem(),
            smem(),
            smem(),
            pl.BlockSpec((TILE, width), lambda i: (i, 0)),
            whole(k.shape),
            whole(v.shape),
        ],
        out_specs=[
            pl.BlockSpec((width, TILE), lambda i: (0, i)),
            pl.BlockSpec((pairs, per_tile, 2 * GROUP), lambda i: (0, i, 0)),
        ],
        out_shape=[
            jax.ShapeDtypeStruct((width, slot), bf16),
            jax.ShapeDtypeStruct((pairs, grid * per_tile, 2 * GROUP), bf16),
        ],
        scratch_shapes=[
            pltpu.VMEM((2 * GROUP, 2 * GROUP), bf16),
        ],
        compiler_params=params(),
        cost_estimate=pl.CostEstimate(
            flops=20 * 10**9, bytes_accessed=slot * width * 10, transcendentals=slot * 512
        ),
        name="attend",
    )(lens, partner, bias, q, k, v)


def attend_back_kernel(
    partner, q_ref, do_ref, p_ref, k_ref, v_ref,
    dq_ref, dk_ref, dv_ref, db_ref,
    mask_ref, dk_sum, dv_sum, db_sum,
):
    tile = q_ref.shape[0]
    step = pl.program_id(0)
    per = GROUP // BLOCK

    @pl.when(step == 0)
    def _():
        mask_ref[...] = diagonal_mask()
        dk_sum[...] = jnp.zeros_like(dk_sum)
        dv_sum[...] = jnp.zeros_like(dv_sum)

    scale = 1.0 / math.sqrt(HEAD)
    lanes = head_lanes()
    mask = mask_ref[...]
    work, d_probs, seconds, thirds = [], [], [], []
    for g in range(tile // GROUP):
        first = step * (tile // BLOCK) + g * per
        partners = [partner[0, first + c] for c in range(per)]
        rows = pl.ds(pl.multiple_of(first * BLOCK, GROUP), GROUP)
        spans = [rows] + [pl.ds(pl.multiple_of(p * BLOCK, BLOCK), BLOCK) for p in partners]
        q_rows = slice(g * GROUP, (g + 1) * GROUP)
        q_two = head_stack(q_ref[q_rows, :], lanes)
        do_two = head_stack(do_ref[q_rows, :], lanes)
        v_all = jnp.concatenate([v_ref[at, :] for at in spans], axis=0)
        work.append((g, spans, q_rows, q_two, do_two))
        d_probs.append(dot_nt(v_all, do_two))
    for d_prob, (g, *_) in zip(d_probs, work):
        at = g * 2 * BLOCK
        own_b = p_ref[0, at : at + BLOCK, :]
        far_b = p_ref[0, at + BLOCK : at + 2 * BLOCK, :]
        own, far = own_b.astype(f32), far_b.astype(f32)
        d_own, d_far = compact(d_prob[:GROUP]), compact(d_prob[GROUP:])
        delta = jnp.sum(own * d_own, axis=0, keepdims=True) + jnp.sum(
            far * d_far, axis=0, keepdims=True
        )
        d_own = own * (d_own - delta)
        d_far = far * (d_far - delta)
        d_bias = jnp.sum(d_far, axis=0, keepdims=True)
        db_sum[pl.ds(step * (tile // GROUP) + g, 1), :] = d_bias[:, :GROUP] + d_bias[:, GROUP:]
        seconds.append((spread(d_own * scale, d_far * scale, mask), spread(own_b, far_b, mask)))
    for (d_scores, prob), (g, spans, q_rows, q_two, do_two) in zip(seconds, work):
        k_all = jnp.concatenate([k_ref[at, :] for at in spans], axis=0)
        thirds.append((dot(d_scores, q_two), dot(prob, do_two), dot(k_all.T, d_scores)))
    for (dk, dv, dq), (g, spans, q_rows, *_) in zip(thirds, work):
        dq = jnp.concatenate([dq[:HEAD, :GROUP], dq[HEAD:, GROUP:]], axis=0)
        dq_ref[q_rows, :] = dq.T.astype(bf16)
        dk_sum[spans[0], :] += dk[:GROUP]
        dv_sum[spans[0], :] += dv[:GROUP]
        for c in range(per):
            here = slice(GROUP + c * BLOCK, GROUP + (c + 1) * BLOCK)
            dk_sum[spans[1 + c], :] += dk[here]
            dv_sum[spans[1 + c], :] += dv[here]

    @pl.when(step == pl.num_programs(0) - 1)
    def _():
        dk_ref[...] = dk_sum[...].astype(bf16)
        dv_ref[...] = dv_sum[...].astype(bf16)
        groups = db_sum.shape[0]
        blocks = groups * per
        pick = (iota((GROUP, blocks), 0) // BLOCK == iota((GROUP, blocks), 1) % per).astype(f32)
        sums = dot(db_sum[...], pick, highest)
        mine = iota((groups, blocks), 1) // per == iota((groups, blocks), 0)
        db_ref[...] = jnp.sum(jnp.where(mine, sums, 0.0), axis=0, keepdims=True)


def attend_back(pair, partner, q, d_o, probs, k, v):
    slot = q.shape[0]
    grid = slot // WIDE
    per_tile = (WIDE // GROUP) * 2 * BLOCK
    row = pl.BlockSpec((WIDE, LANES), lambda i: (i, pair))
    once = pl.BlockSpec((slot, LANES), lambda i: (0, pair), pipeline_mode=pl.Buffered(1))
    out = jax.ShapeDtypeStruct((slot, LANES), bf16)
    return pl.pallas_call(
        attend_back_kernel,
        grid=(grid,),
        in_specs=[
            smem(),
            row,
            row,
            pl.BlockSpec((1, per_tile, 2 * GROUP), lambda i: (pair, i, 0)),
            once,
            once,
        ],
        out_specs=[
            pl.BlockSpec((WIDE, LANES), lambda i: (i, 0)),
            whole((slot, LANES)),
            whole((slot, LANES)),
            whole((1, slot // BLOCK)),
        ],
        out_shape=[out, out, out, jax.ShapeDtypeStruct((1, slot // BLOCK), f32)],
        scratch_shapes=[
            pltpu.VMEM((2 * GROUP, 2 * GROUP), bf16),
            pltpu.VMEM((slot, LANES), f32),
            pltpu.VMEM((slot, LANES), f32),
            pltpu.VMEM((slot // GROUP, GROUP), f32),
        ],
        compiler_params=params(),
        cost_estimate=pl.CostEstimate(
            flops=10 * 10**9, bytes_accessed=slot * LANES * 16, transcendentals=0
        ),
        name="attend_back",
    )(partner, q, d_o, probs, k, v)


def ffn_kernel(
    x_ref, dy_ref, o_ref, norms_ref, w_ref,
    out_ref, dx_ref, do_ref, g_ref, g_norm_ref,
    h_scr, ht_scr, dyt_scr, y_scr, dh_scr, gt_scr,
):
    tile, width = x_ref.shape
    hidden = gt_scr.shape[1]
    slabs = hidden // width
    parts = width // ROWS
    whole_rows = slice(slabs * ROWS, (slabs + 1) * ROWS)
    out_rows = slice((slabs + 1) * ROWS, (2 * slabs + 1) * ROWS)
    step = pl.program_id(0)

    @pl.when(step == 0)
    def _():
        g_ref[...] = jnp.zeros_like(g_ref)
        gt_scr[...] = jnp.zeros_like(gt_scr)
        g_norm_ref[...] = jnp.zeros_like(g_norm_ref)

    o_t = o_ref[...]
    w_o = w_ref[:, whole_rows, :].reshape(width, width)
    x_one = x_ref[...].astype(f32) + dot(o_t.T, w_o)
    hat, rstd = norm_stats(x_one)
    h_two = (hat * norms_ref[2:3, :] + norms_ref[3:4, :]).astype(bf16)
    h_scr[...] = h_two
    ht_scr[...] = h_two.T
    dyt_scr[...] = dy_ref[...].T
    y_scr[...] = x_one
    dh_scr[...] = jnp.zeros_like(dh_scr)
    root = math.sqrt(2.0 / math.pi)

    def before(c):
        w_in = w_ref[:, c * ROWS : (c + 1) * ROWS, :].reshape(width, width)
        share = parts // slabs
        w_out = w_ref[c * share : (c + 1) * share, out_rows, :].reshape(width, width)
        act = dot(h_scr[...], w_in)
        d_hid = dot_nt(dy_ref[...], w_out)
        return w_in, w_out, act, d_hid

    def between(act, d_hid):
        square = act * act
        curve = jnp.tanh(act * (root + (root * 0.044715) * square))
        gate = 0.5 + 0.5 * curve
        hid = act * gate
        slope = gate + hid * (1.0 - curve) * (root + (3.0 * root * 0.044715) * square)
        return hid.astype(bf16), (d_hid * slope).astype(bf16)

    def after(c, w_in, w_out, hid, d_act):
        cols = slice(c * width, (c + 1) * width)
        y_scr[...] += dot(hid, w_out)
        gt_scr[:, cols] += dot(dyt_scr[...], hid)
        slab = slice(c * ROWS, (c + 1) * ROWS)
        g_ref[:, slab, :] += dot(ht_scr[...], d_act).reshape(parts, ROWS, width)
        dh_scr[...] += dot_nt(d_act, w_in)

    ahead = before(0)
    for c in range(slabs):
        w_in, w_out, act, d_hid = ahead
        if c + 1 < slabs:
            ahead = before(c + 1)
        hid, d_act = between(act, d_hid)
        after(c, w_in, w_out, hid, d_act)
    out_ref[...] = y_scr[...].astype(bf16)
    d_h = dh_scr[...]
    g_norm_ref[2:3, :] += jnp.sum(d_h * hat, axis=0, keepdims=True)
    g_norm_ref[3:4, :] += jnp.sum(d_h, axis=0, keepdims=True)
    d_x = dy_ref[...].astype(f32) + norm_back(d_h, hat, rstd, norms_ref[2:3, :])
    dx_ref[...] = d_x
    d_z = d_x.astype(bf16)
    g_ref[:, whole_rows, :] += dot(o_t, d_z).reshape(parts, ROWS, width)
    do_ref[...] = dot_nt(d_z, w_o).astype(bf16)

    @pl.when(step == pl.num_programs(0) - 1)
    def _():
        share = parts // slabs
        for c in range(slabs):
            g_ref[c * share : (c + 1) * share, out_rows, :] = gt_scr[
                :, c * width : (c + 1) * width
            ].T.reshape(share, slabs * ROWS, width)


def ffn(x, dy, o_t, norms, w_two):
    slot, width = x.shape
    hidden = (w_two.shape[1] // ROWS - 1) // 2 * width
    grid = slot // TILE
    row = pl.BlockSpec((TILE, width), lambda i: (i, 0))

    def once(shape):
        return pl.BlockSpec(shape, lambda i: (0,) * len(shape), pipeline_mode=pl.Buffered(1))

    return pl.pallas_call(
        ffn_kernel,
        grid=(grid,),
        in_specs=[
            row,
            row,
            pl.BlockSpec((width, TILE), lambda i: (0, i)),
            once(norms.shape),
            once(w_two.shape),
        ],
        out_specs=[row, row, row, once(w_two.shape), once((8, width))],
        out_shape=[
            jax.ShapeDtypeStruct((slot, width), bf16),
            jax.ShapeDtypeStruct((slot, width), f32),
            jax.ShapeDtypeStruct((slot, width), bf16),
            jax.ShapeDtypeStruct(w_two.shape, f32),
            jax.ShapeDtypeStruct((8, width), f32),
        ],
        scratch_shapes=[
            pltpu.VMEM((TILE, width), bf16),
            pltpu.VMEM((width, TILE), bf16),
            pltpu.VMEM((width, TILE), bf16),
            pltpu.VMEM((TILE, width), f32),
            pltpu.VMEM((TILE, width), f32),
            pltpu.VMEM((width, hidden), f32),
        ],
        compiler_params=params(),
        cost_estimate=pl.CostEstimate(
            flops=2 * slot * width * (3 * width + 6 * hidden),
            bytes_accessed=slot * width * 14,
            transcendentals=slot * hidden,
        ),
        name="ffn",
    )(x, dy, o_t, norms, w_two)


def project_back_kernel(
    lens, x_ref, dx_ref, du_ref, norms_ref, w_ref, g_sort_ref, g_two_ref, *refs, slot
):
    *d_refs, grad_ref, g_ref, g_norm_ref = refs
    tile, width = x_ref.shape
    step = pl.program_id(0)

    @pl.when(step == 0)
    def _():
        g_ref[...] = jnp.zeros_like(g_ref)
        g_norm_ref[...] = jnp.zeros_like(g_norm_ref)

    pairs = width // LANES
    ends = ends_of(lens, slot)
    blocks = SUB // BLOCK
    first = []
    for r in range(0, tile, SUB):
        rows = slice(r, r + SUB)
        places = step * tile + r + iota((SUB, 1), 0)
        live = places < end_at(places, ends, slot)
        d_u = du_ref[r // BLOCK : r // BLOCK + blocks, :].reshape(blocks, 1, width)
        d_h = jnp.broadcast_to(d_u, (blocks, BLOCK, width)).reshape(SUB, width)
        d_h = jnp.where(live, d_h, 0.0)
        for part in range(3):
            cols = slice(part * width, (part + 1) * width)
            d_part = jnp.concatenate(
                [ref[rows, :] for ref in d_refs[part * pairs : (part + 1) * pairs]], axis=1
            )
            d_h = d_h + dot_nt(d_part, w_ref[:, cols])
        first.append(d_h)
    hats = []
    for r, d_h in zip(range(0, tile, SUB), first):
        rows = slice(r, r + SUB)
        hat, rstd = norm_stats(x_ref[rows, :].astype(f32))
        hats.append((hat * norms_ref[0:1, :] + norms_ref[1:2, :]).astype(bf16))
        g_norm_ref[0:1, :] += jnp.sum(d_h * hat, axis=0, keepdims=True)
        g_norm_ref[1:2, :] += jnp.sum(d_h, axis=0, keepdims=True)
        grad_ref[rows, :] = dx_ref[rows, :] + norm_back(d_h, hat, rstd, norms_ref[0:1, :])
    h_one = jnp.concatenate(hats, axis=0)
    for part in range(3):
        cols = slice(part * width, (part + 1) * width)
        d_part = jnp.concatenate([ref[...] for ref in d_refs[part * pairs : (part + 1) * pairs]], axis=1)
        g_ref[:, cols] += dot_tn(h_one, d_part)

    @pl.when(step == pl.num_programs(0) - 1)
    def _():
        g_ref[:, 3 * width : 3 * width + LANES] = g_sort_ref[...]
        small = g_norm_ref[...] + g_two_ref[...]
        rest = jnp.zeros((LANES - small.shape[0], width), f32)
        g_ref[:, 3 * width + LANES :] = jnp.concatenate([small, rest], axis=0).T


def project_back(lens, x, d_x, d_q, d_k, d_v, d_u, norms, w_one, g_sort, g_two):
    slot, width = x.shape
    grid = slot // WIDE
    row = pl.BlockSpec((WIDE, width), lambda i: (i, 0))

    def once(shape):
        return pl.BlockSpec(shape, lambda i: (0, 0), pipeline_mode=pl.Buffered(1))

    return pl.pallas_call(
        functools.partial(project_back_kernel, slot=slot),
        grid=(grid,),
        in_specs=[
            smem(),
            row,
            row,
            pl.BlockSpec((WIDE // BLOCK, width), lambda i: (i, 0)),
            once(norms.shape),
            once(w_one.shape),
            once(g_sort.shape),
            once(g_two.shape),
        ]
        + [pl.BlockSpec((WIDE, LANES), lambda i: (i, 0))] * (3 * width // LANES),
        out_specs=[row, once(w_one.shape)],
        out_shape=[
            jax.ShapeDtypeStruct((slot, width), f32),
            jax.ShapeDtypeStruct(w_one.shape, f32),
        ],
        scratch_shapes=[pltpu.VMEM((8, width), f32)],
        compiler_params=params(),
        cost_estimate=pl.CostEstimate(
            flops=2 * slot * width * 6 * width, bytes_accessed=slot * width * 18, transcendentals=0
        ),
        name="project_back",
    )(lens, x, d_x, d_u, norms, w_one, g_sort, g_two, *d_q, *d_k, *d_v)


def pack_kernel(wqkv, wo, wsort, win, wout, norms_t, one_ref, two_ref):
    rows, wide = wqkv.shape
    width = wo.shape[1]
    one_ref[:, :wide] = wqkv[...].astype(bf16)
    one_ref[:, wide : wide + LANES] = wsort[...].astype(bf16)
    few = norms_t.shape[0]
    tall = jnp.concatenate([norms_t[...], jnp.zeros((LANES - few, rows), f32)], axis=0)
    one_ref[:, wide + LANES :] = tall.T.astype(bf16)
    slabs = win.shape[1] // width
    for c in range(slabs):
        two_ref[c * rows : (c + 1) * rows, :] = win[:, c * width : (c + 1) * width].astype(bf16)
    two_ref[slabs * rows : (slabs + 1) * rows, :] = wo[...].astype(bf16)
    two_ref[(slabs + 1) * rows :, :] = wout[...].astype(bf16)


def pack(masters):
    wqkv, wo, wsort, win, wout, norms = masters
    rows = wqkv.shape[0]
    return pl.pallas_call(
        pack_kernel,
        out_shape=[
            jax.ShapeDtypeStruct((rows, wqkv.shape[1] + 2 * LANES), bf16),
            jax.ShapeDtypeStruct((rows * (win.shape[1] // wo.shape[1] + 1) + wout.shape[0], wo.shape[1]), bf16),
        ],
        compiler_params=params(),
        name="pack",
    )(wqkv, wo, wsort, win, wout, norms.T)


def adamw_kernel(one_ref, two_ref, *refs):
    masters, moments, squares, outs = refs[:6], refs[6:12], refs[12:18], refs[18:]
    rows, width = masters[1].shape
    wide = masters[0].shape[1]
    slabs = masters[3].shape[1] // width
    few = masters[5].shape[0]
    norm_grad = one_ref[:, wide + LANES :].T[:few, :]
    grads = (
        one_ref[:, :wide],
        two_ref[slabs * rows : (slabs + 1) * rows, :],
        one_ref[:, wide : wide + LANES],
        jnp.concatenate([two_ref[c * rows : (c + 1) * rows, :] for c in range(slabs)], axis=1),
        two_ref[(slabs + 1) * rows :, :],
        norm_grad,
    )
    for i in range(6):
        weight, grad = masters[i][...], grads[i]
        moment = beta_one * moments[i][...] + (1.0 - beta_one) * grad
        square = beta_two * squares[i][...] + (1.0 - beta_two) * grad * grad
        m_hat = moment / (1.0 - beta_one**STEP)
        s_hat = square / (1.0 - beta_two**STEP)
        outs[3 * i][...] = weight - rates[i] * (
            m_hat / (jnp.sqrt(s_hat) + adam_eps) + decay * weight
        )
        outs[3 * i + 1][...] = moment
        outs[3 * i + 2][...] = square


def adamw(one, two, masters, moments, squares):
    flip = lambda group: (*group[:5], group[5].T)
    args = (one, two, *flip(masters), *flip(moments), *flip(squares))
    shapes = [a.shape for a in flip(masters)]
    outs = pl.pallas_call(
        adamw_kernel,
        out_shape=[jax.ShapeDtypeStruct(shape, f32) for shape in shapes for _ in range(3)],
        compiler_params=params(),
        name="adamw",
    )(*args)
    return (*outs[:15], *[o.T for o in outs[15:]])


def regroup(gathered, size, rows, slabs):
    if rows == ROWS:
        return gathered
    times = ROWS // rows
    width = gathered.shape[-1]
    block = gathered.reshape(size // times, times, 2 * slabs + 1, rows, width)
    inner = block[:, :, : slabs + 1].transpose(0, 2, 1, 3, 4)
    outer = block[:, :, slabs + 1 :]
    return jnp.concatenate(
        [
            inner.reshape(size // times, (slabs + 1) * ROWS, width),
            outer.reshape(size // times, slabs * ROWS, width),
        ],
        axis=1,
    )


def ungroup(grads, size, rows, slabs):
    if rows == ROWS:
        return grads
    times = ROWS // rows
    width = grads.shape[-1]
    inner = grads[:, : (slabs + 1) * ROWS].reshape(size // times, slabs + 1, times, rows, width)
    outer = grads[:, (slabs + 1) * ROWS :].reshape(size // times, times, slabs, rows, width)
    block = jnp.concatenate([inner.transpose(0, 2, 1, 3, 4), outer], axis=2)
    return block.reshape(size, (2 * slabs + 1) * rows, width)


def swap(value, bit, size):
    return lax.ppermute(value, "dp", [(i, i ^ (1 << bit)) for i in range(size)])


def gather(block, size):
    count = size.bit_length() - 1
    place = lax.axis_index("dp")
    held = block.reshape((1,) * count + block.shape)
    for bit in reversed(range(count)):
        axis = count - 1 - bit
        came = swap(held, bit, size)
        upper = ((place >> bit) & 1) == 1
        held = jnp.concatenate(
            [jnp.where(upper, came, held), jnp.where(upper, held, came)], axis=axis
        )
    return held.reshape((size * block.shape[0],) + block.shape[1:])


class ScatterSum:
    def __init__(self, value, size):
        self.size, self.count = size, size.bit_length() - 1
        self.rest = value.shape[1:]
        self.held = value.reshape((2,) * self.count + value.shape[0:0] + (value.shape[0] // size,) + self.rest)
        self.bit = 0

    def begin(self):
        place = lax.axis_index("dp")
        axis = self.count - 1 - self.bit
        mine = (place >> self.bit) & 1
        sent = lax.dynamic_index_in_dim(self.held, 1 - mine, axis, keepdims=True).astype(bf16)
        self.kept = lax.dynamic_index_in_dim(self.held, mine, axis, keepdims=True)
        self.came = swap(sent, self.bit, self.size)
        self.bit += 1

    def end(self):
        self.held = self.kept + self.came.astype(f32)
        return self.held

    def finish(self):
        while self.bit < self.count:
            self.begin()
            self.end()
        return self.held.reshape((-1,) + self.rest)


def body(size, x, dy, lens, partner, *state):
    slot, width = x.shape
    masters, moments, squares = state[:6], state[6:12], state[12:]
    rows = masters[0].shape[0]
    slabs = masters[3].shape[1] // width
    pack_one, pack_two = pack(masters)
    w_one = gather(pack_one, size)
    w_two = regroup(lax.all_gather(pack_two, "dp", axis=0), size, rows, slabs)

    q, k, v, u, norms = project(lens, x, w_one)
    bias, steps = sort_net(lens, u, w_one, partner, slot)
    o_t, probs = attend(lens, partner, bias, q, k, v)
    out, d_x, d_o, g_rest, g_two = ffn(x, dy, o_t, norms, w_two)
    two = ungroup(g_rest, size, rows, slabs)
    two = ScatterSum(two.reshape((-1, width)), size)
    back = []
    for pair in range(width // LANES):
        two.begin()
        back.append(attend_back(pair, partner, q, d_o, probs, k, v))
        held = two.end()
        q, d_o, two.held = lax.optimization_barrier((q, d_o, held))
    d_q, d_k, d_v, d_bias = zip(*back)
    d_u, g_sort = sort_back(lens, u, w_one, partner, d_bias, steps, slot)
    two.begin()
    grad_in, g_one = project_back(lens, x, d_x, d_q, d_k, d_v, d_u, norms, w_one, g_sort, g_two)
    two.end()
    one = ScatterSum(g_one, size).finish()
    outs = adamw(one, two.finish(), masters, moments, squares)
    return (out, grad_in, *outs)


def solution(mesh):
    spec = P("dp", None)
    return jax.shard_map(
        functools.partial(body, mesh.shape["dp"]),
        mesh=mesh,
        in_specs=(spec,) * 22,
        out_specs=(spec,) * 20,
        check_vma=False,
    )
```

time: 428 us -> 300 us (0.70)
  Pallas kernels: 240 us -> 180 us
  starting transfers between devices: 56.2 us -> 22.8 us
  local copies, waits for them, and re-layouts: 34.6 us -> 5.49 us
  other arithmetic: 35.8 us -> 10.5 us
  between operations: 1.8 us -> 14.3 us
  waiting for transfers between devices: 58.6 us -> 65.8 us
    ppermute x60 -> x15, starting transfers between devices: 56.2 us -> 22.8 us  [swap(): return lax.ppermute(value, 'dp', [(i, i ^ 1 << bit) for i in range(size)])]
    pallas_call x1, Pallas kernels: 48.2 us -> 15.4 us  [attend(): pl.pallas_call(functools.partial(attend_kernel, slot=slot), grid=(grid,),...]
    pallas_call x1 -> x4, Pallas kernels: 56.1 us -> 36.2 us  [attend_back(): pl.pallas_call(attend_back_kernel, grid=(grid,), in_specs=[smem(), row, r...]
    convert_element_type x35 -> x10, local copies, waits for them, and re-layouts: 18.5 us -> 5.49 us  [begin(): lax.dynamic_index_in_dim(self.held, 1 - mine, axis, keepdims=True)]
    unnamed x60 -> x0, local copies, waits for them, and re-layouts: 12.6 us -> none
    pallas_call x1, Pallas kernels: 89.5 us -> 79.7 us  [ffn(): pl.pallas_call(ffn_kernel, grid=(grid,), in_specs=[row, row, pl.BlockSpec...]
    add x24 -> x8, other arithmetic: 15.8 us -> 6.5 us  [end(): self.held = self.kept + self.came.astype(f32)]
    concatenate x30 -> x5, other arithmetic: 7.19 us -> 1.55 us  [gather(): jnp.concatenate([jnp.where(upper, came, held), jnp.where(upper, held, cam...]
  transfers between devices with their start and end apart: 60 -> 16, of which waited for: 22 -> 14; matrix products, arithmetic and copies ran while one was open for 14% -> 1% of each run, Pallas kernels for 35% -> 20%
where the time goes in v2:
time: 300 us; the launch traced here: 299 us
  Pallas kernels  180 us (60%)
  waiting for transfers between devices  65.8 us (22%)
  starting transfers between devices  22.8 us (8%)
  between operations  14.3 us (5%)
  other arithmetic  10.5 us (4%)
  local copies, waits for them, and re-layouts  5.49 us (2%)
    pallas_call x1, Pallas kernels, ffn(): pl.pallas_call(ffn_kernel, grid=(grid,), in_specs=[row, row, pl.BlockSpec...  79.7 us
    ppermute x15, waiting for transfers between devices, swap(): return lax.ppermute(value, 'dp', [(i, i ^ 1 << bit) for i in range(size)])  61.7 us
    pallas_call x4, Pallas kernels, attend_back(): pl.pallas_call(attend_back_kernel, grid=(grid,), in_specs=[smem(), row, r...  36.2 us
    pallas_call x1, Pallas kernels, project_back(): pl.pallas_call(functools.partial(project_back_kernel, slot=slot), grid=(g...  23.4 us
    ppermute x15, starting transfers between devices, swap(): return lax.ppermute(value, 'dp', [(i, i ^ 1 << bit) for i in range(size)])  22.8 us
    pallas_call x1, Pallas kernels, attend(): pl.pallas_call(functools.partial(attend_kernel, slot=slot), grid=(grid,),...  15.4 us
    pallas_call x1, Pallas kernels, project(): pl.pallas_call(functools.partial(project_kernel, slot=slot), grid=(grid,)...  12.1 us
    add x8, other arithmetic, end(): self.held = self.kept + self.came.astype(f32)  6.5 us
  transfers between devices with their start and end apart: 16, of which 14 were waited for; matrix products, arithmetic and copies ran while one was open for 1% of the time, Pallas kernels for 20%

profile of v2, /device:TPU:0, one launch (start us, length us, event | category | flops | bytes accessed | tf_op | source)
XLA Modules:
  0.0 299.1 jit_solution(16929557098755797672)
XLA Ops:
  9.0 4.1 %collective-permute-start = (bf16[1,1,1,1,1,16,1792]{6,5,4,3,2,1,0:T(8,128)(2,1)}, bf16[1,1,1,1,1,16,1792]{6,5,4,3,2,1,0:T(8,128)(2,1)S(1)}, u32[]{:S(2)}, u32[]{:S(2)}) collective-permute-start(bf16[1,1,1,1,1,16,1792]{6,5,4,3,2,1,0:T(8,128)(2,1)} %bitcast.25), channel_id=1, source_target_pairs={{0,16},{1,17},{2,18},{3,19},{4,20},{5,21},{6,22},{7,23},{8,24},{9,... | collective-permute-start | bytes 172040 | tf_op jit(solution)/shard_map/ppermute | solution.py:847
  13.1 3.0 collective-permute-done
  18.3 3.5 %collective-permute-done.1 = bf16[2,1,1,1,1,16,1792]{6,5,4,3,2,1,0:T(8,128)(2,1)S(1)} collective-permute-done((bf16[2,1,1,1,1,16,1792]{6,5,4,3,2,1,0:T(8,128)(2,1)S(1)}, bf16[2,1,1,1,1,16,1792]{6,5,4,3,2,1,0:T(8,128)(2,1)S(1)}, u32[]{:S(2)}, u32[]{:S(2)}) %collective-permute-start.1) | collective-permute-done | bytes 114720 | tf_op jit(solution)/shard_map/ppermute | solution.py:847
  23.7 5.3 %collective-permute-done.2 = bf16[2,2,1,1,1,16,1792]{6,5,4,3,2,1,0:T(8,128)(2,1)S(1)} collective-permute-done((bf16[2,2,1,1,1,16,1792]{6,5,4,3,2,1,0:T(8,128)(2,1)S(1)}, bf16[2,2,1,1,1,16,1792]{6,5,4,3,2,1,0:T(8,128)(2,1)S(1)}, u32[]{:S(2)}, u32[]{:S(2)}) %collective-permute-start.2) | collective-permute-done | bytes 229408 | tf_op jit(solution)/shard_map/ppermute | solution.py:847
  30.7 6.9 %collective-permute-done.3 = bf16[2,2,2,1,1,16,1792]{6,5,4,3,2,1,0:T(8,128)(2,1)S(1)} collective-permute-done((bf16[2,2,2,1,1,16,1792]{6,5,4,3,2,1,0:T(8,128)(2,1)S(1)}, bf16[2,2,2,1,1,16,1792]{6,5,4,3,2,1,0:T(8,128)(2,1)S(1)}, u32[]{:S(2)}, u32[]{:S(2)}) %collective-permute-start.3) | collective-permute-done | bytes 458784 | tf_op jit(solution)/shard_map/ppermute | solution.py:847
  41.8 12.1 %project.1 = (bf16[4096,512]{1,0:T(8,128)(2,1)}, bf16[4096,512]{1,0:T(8,128)(2,1)}, bf16[4096,512]{1,0:T(8,128)(2,1)}, f32[128,512]{1,0:T(8,128)}, f32[8,512]{1,0:T(8,128)}) custom-call(s32[1,4]{1,0:T(1,128)} %lens.9, bf16[4096,512]{1,0:T(8,128)(2,1)} %x_ref.5, bf16[512,1792]{1,0:T(8,128)(2,1)} %bitcast.17), custom_call_target="tpu_custom_call" | custom-call | flops 6442450944 | bytes 16777216 | tf_op jit(solution)/shard_map/project/pallas_call | solution.py:127
  53.9 4.8 %sort_net.1 = (f32[1,128]{1,0:T(1,128)}, f32[16,128,128]{2,1,0:T(8,128)}) custom-call(s32[1,4]{1,0:T(1,128)} %lens.9, f32[128,512]{1,0:T(8,128)} %get-tuple-element.85.u_ref, bf16[512,1792]{1,0:T(8,128)(2,1)} %bitcast.18, s32[1,128]{1,0:T(1,128)} %partner_ref.3), custom_call_target="tpu_custom_call" | custom-call | flops 100000000 | bytes 10000000 | tf_op jit(solution)/shard_map/sort_net/pallas_call | solution.py:210
  58.7 15.4 %attend.1 = (bf16[512,4096]{1,0:T(8,128)(2,1)}, bf16[4,2048,256]{2,1,0:T(8,128)(2,1)}) custom-call(s32[1,4]{1,0:T(1,128)} %lens.9, s32[1,128]{1,0:T(1,128)} %partner_ref.3, f32[1,128]{1,0:T(1,128)} %get-tuple-element.86.bias, bf16[4096,512]{1,0:T(8,128)(2,1)} %get-tuple-element.108.q_ref, bf16[4096,512]{1,0:T(8,128)(2,1)} %get-tuple-element.88.k_ref, ...), custom_call_target="tpu_custom_call" | custom-call | flops 20000000000 | bytes 20971520 | tf_op jit(solution)/shard_map/attend/pallas_call | solution.py:396
  74.1 4.1 %all-gather.3.cloned.1.call-done = bf16[4608,512]{1,0:T(8,128)(2,1)} async-done(((bf16[144,512]{1,0:T(8,128)(2,1)}), bf16[4608,512]{1,0:T(8,128)(2,1)}) %all-gather.3.cloned.1.call-update) | async-done | bytes 4718608 | tf_op jit(solution)/shard_map/all_gather | solution.py:898
  78.2 79.7 %ffn.1 = (bf16[4096,512]{1,0:T(8,128)(2,1)}, f32[4096,512]{1,0:T(8,128)}, bf16[4096,512]{1,0:T(8,128)(2,1)}, f32[32,144,512]{2,1,0:T(8,128)}, f32[8,512]{1,0:T(8,128)}) custom-call(bf16[4096,512]{1,0:T(8,128)(2,1)} %x_ref.5, bf16[4096,512]{1,0:T(8,128)(2,1)} %dy_ref.1, bf16[512,4096]{1,0:T(8,128)(2,1)} %get-tuple-element.90.o_ref, ...), custom_call_target="tpu_custom_call" | custom-call | flops 57982058496 | bytes 29360128 | tf_op jit(solution)/shard_map/ffn/pallas_call | solution.py:624
  157.9 2.7 dynamic-slice_convert_fusion
  160.9 4.4 %collective-permute-done.5 = bf16[2,2,2,2,1,144,512]{6,5,4,3,2,1,0:T(8,128)(2,1)} collective-permute-done((bf16[2,2,2,2,1,144,512]{6,5,4,3,2,1,0:T(8,128)(2,1)S(1)}, bf16[2,2,2,2,1,144,512]{6,5,4,3,2,1,0:T(8,128)(2,1)}, u32[]{:S(2)}, u32[]{:S(2)}) %collective-permute-start.5) | collective-permute-done | bytes 2359328 | tf_op jit(solution)/shard_map/ppermute | solution.py:847
  165.3 3.9 %convert_add_fusion = f32[2,2,2,2,1,144,512]{6,5,4,3,2,1,0:T(8,128)S(1)} fusion(bf16[2,2,2,2,1,144,512]{6,5,4,3,2,1,0:T(8,128)(2,1)} %collective-permute-done.5, f32[2,2,2,2,2,144,512]{6,5,4,3,2,1,0:T(8,128)} %bitcast.22, s32[]{:T(128)S(6)} %select_n.125), kind=kLoop, calls=%fused_computation | loop fusion | flops 2359296 | bytes 11796484 | tf_op jit(solution)/shard_map/add | solution.py:881
  171.3 9.0 %attend_back.4 = (bf16[4096,128]{1,0:T(8,128)(2,1)}, bf16[4096,128]{1,0:T(8,128)(2,1)}, bf16[4096,128]{1,0:T(8,128)(2,1)}, f32[1,128]{1,0:T(1,128)}) custom-call(s32[1,128]{1,0:T(1,128)} %partner_ref.3, bf16[4096,512]{1,0:T(8,128)(2,1)} %get-tuple-element.108.q_ref, bf16[4096,512]{1,0:T(8,128)(2,1)} %get-tuple-element.109.do_ref, ...), custom_call_target="tpu_custom_call" | custom-call | flops 10000000000 | bytes 8388608 | tf_op jit(solution)/shard_map/attend_back/pallas_call | solution.py:502
  180.4 9.0 %attend_back.5 = (bf16[4096,128]{1,0:T(8,128)(2,1)}, bf16[4096,128]{1,0:T(8,128)(2,1)}, bf16[4096,128]{1,0:T(8,128)(2,1)}, f32[1,128]{1,0:T(1,128)}) custom-call(s32[1,128]{1,0:T(1,128)} %partner_ref.3, bf16[4096,512]{1,0:T(8,128)(2,1)} %get-tuple-element.108.q_ref, bf16[4096,512]{1,0:T(8,128)(2,1)} %get-tuple-element.109.do_ref, ...), custom_call_target="tpu_custom_call" | custom-call | flops 10000000000 | bytes 8388608 | tf_op jit(solution)/shard_map/attend_back/pallas_call | solution.py:502
  189.4 8.4 %collective-permute-done.6 = bf16[2,2,2,1,1,144,512]{6,5,4,3,2,1,0:T(8,128)(2,1)S(1)} collective-permute-done((bf16[2,2,2,1,1,144,512]{6,5,4,3,2,1,0:T(8,128)(2,1)S(1)}, bf16[2,2,2,1,1,144,512]{6,5,4,3,2,1,0:T(8,128)(2,1)S(1)}, u32[]{:S(2)}, u32[]{:S(2)}) %collective-permute-start.6) | collective-permute-done | bytes 1179680 | tf_op jit(solution)/shard_map/ppermute | solution.py:847
  200.2 9.1 %attend_back.6 = (bf16[4096,128]{1,0:T(8,128)(2,1)}, bf16[4096,128]{1,0:T(8,128)(2,1)}, bf16[4096,128]{1,0:T(8,128)(2,1)}, f32[1,128]{1,0:T(1,128)}) custom-call(s32[1,128]{1,0:T(1,128)} %partner_ref.3, bf16[4096,512]{1,0:T(8,128)(2,1)} %get-tuple-element.108.q_ref, bf16[4096,512]{1,0:T(8,128)(2,1)} %get-tuple-element.109.do_ref, ...), custom_call_target="tpu_custom_call" | custom-call | flops 10000000000 | bytes 8388608 | tf_op jit(solution)/shard_map/attend_back/pallas_call | solution.py:502
  209.3 3.9 %collective-permute-done.7 = bf16[2,2,1,1,1,144,512]{6,5,4,3,2,1,0:T(8,128)(2,1)S(1)} collective-permute-done((bf16[2,2,1,1,1,144,512]{6,5,4,3,2,1,0:T(8,128)(2,1)S(1)}, bf16[2,2,1,1,1,144,512]{6,5,4,3,2,1,0:T(8,128)(2,1)S(1)}, u32[]{:S(2)}, u32[]{:S(2)}) %collective-permute-start.7) | collective-permute-done | bytes 589856 | tf_op jit(solution)/shard_map/ppermute | solution.py:847
  213.4 9.0 %attend_back.7 = (bf16[4096,128]{1,0:T(8,128)(2,1)}, bf16[4096,128]{1,0:T(8,128)(2,1)}, bf16[4096,128]{1,0:T(8,128)(2,1)}, f32[1,128]{1,0:T(1,128)}) custom-call(s32[1,128]{1,0:T(1,128)} %partner_ref.3, bf16[4096,512]{1,0:T(8,128)(2,1)} %get-tuple-element.108.q_ref, bf16[4096,512]{1,0:T(8,128)(2,1)} %get-tuple-element.109.do_ref, ...), custom_call_target="tpu_custom_call" | custom-call | flops 10000000000 | bytes 8388608 | tf_op jit(solution)/shard_map/attend_back/pallas_call | solution.py:502
  222.4 4.2 %sort_back.1 = (f32[128,512]{1,0:T(8,128)}, f32[512,128]{1,0:T(8,128)}) custom-call(s32[1,4]{1,0:T(1,128)} %lens.9, f32[128,512]{1,0:T(8,128)} %get-tuple-element.85.u_ref, bf16[512,1792]{1,0:T(8,128)(2,1)} %bitcast.19, s32[1,128]{1,0:T(1,128)} %partner_ref.3, f32[16,128,128]{2,1,0:T(8,128)} %get-tuple-element.95.steps_ref, ...), custom_call_target="tpu_custom_call" | custom-call | flops 100000000 | bytes 10000000 | tf_op jit(solution)/shard_map/sort_back/pallas_call | solution.py:250
  226.7 23.4 %project_back.1 = (f32[4096,512]{1,0:T(8,128)}, f32[512,1792]{1,0:T(8,128)}) custom-call(s32[1,4]{1,0:T(1,128)} %lens.9, bf16[4096,512]{1,0:T(8,128)(2,1)} %x_ref.5, f32[4096,512]{1,0:T(8,128)} %get-tuple-element.94.dx_ref, f32[128,512]{1,0:T(8,128)} %get-tuple-element.111.du_ref, f32[8,512]{1,0:T(8,128)} %get-tuple-element.91.norms_ref, ...), custom_call_target="tpu_custom_call" | custom-call | flops 12884901888 | bytes 37748736 | tf_op jit(solution)/shard_map/project_back/pallas_call | solution.py:720
  260.0 9.6 %collective-permute-done.9 = bf16[2,2,2,1,1,16,1792]{6,5,4,3,2,1,0:T(8,128)(2,1)S(1)} collective-permute-done((bf16[2,2,2,1,1,16,1792]{6,5,4,3,2,1,0:T(8,128)(2,1)}, bf16[2,2,2,1,1,16,1792]{6,5,4,3,2,1,0:T(8,128)(2,1)S(1)}, u32[]{:S(2)}, u32[]{:S(2)}) %collective-permute-start.9) | collective-permute-done | bytes 458784 | tf_op jit(solution)/shard_map/ppermute | solution.py:847
  271.5 5.0 %collective-permute-done.10 = bf16[2,2,1,1,1,16,1792]{6,5,4,3,2,1,0:T(8,128)(2,1)S(1)} collective-permute-done((bf16[2,2,1,1,1,16,1792]{6,5,4,3,2,1,0:T(8,128)(2,1)S(1)}, bf16[2,2,1,1,1,16,1792]{6,5,4,3,2,1,0:T(8,128)(2,1)S(1)}, u32[]{:S(2)}, u32[]{:S(2)}) %collective-permute-start.10) | collective-permute-done | bytes 229408 | tf_op jit(solution)/shard_map/ppermute | solution.py:847
  283.8 4.4 %collective-permute-done.14 = bf16[1,1,1,1,1,144,512]{6,5,4,3,2,1,0:T(8,128)(2,1)S(1)} collective-permute-done((bf16[1,1,1,1,1,144,512]{6,5,4,3,2,1,0:T(8,128)(2,1)S(1)}, bf16[1,1,1,1,1,144,512]{6,5,4,3,2,1,0:T(8,128)(2,1)S(1)}, u32[]{:S(2)}, u32[]{:S(2)}) %collective-permute-start.14) | collective-permute-done | bytes 147488 | tf_op jit(solution)/shard_map/ppermute | solution.py:847
  (51 shorter events, 39.8 us)
Async XLA Ops:
  7.2 71.0 %all-gather.3.cloned.1.call-start = ((), (), s32[]{:S(2)}) async-start(), calls=%async_computation | async-start | bytes 4866048 | tf_op jit(solution)/shard_map/all_gather | solution.py:898
  9.0 7.1 %collective-permute-start = (bf16[1,1,1,1,1,16,1792]{6,5,4,3,2,1,0:T(8,128)(2,1)}, bf16[1,1,1,1,1,16,1792]{6,5,4,3,2,1,0:T(8,128)(2,1)S(1)}, u32[]{:S(2)}, u32[]{:S(2)}) collective-permute-start(bf16[1,1,1,1,1,16,1792]{6,5,4,3,2,1,0:T(8,128)(2,1)} %bitcast.25), channel_id=1, source_target_pairs={{0,16},{1,17},{2,18},{3,19},{4,20},{5,21},{6,22},{7,23},{8,24},{9,... | collective-permute-start | bytes 172040 | tf_op jit(solution)/shard_map/ppermute | solution.py:847
  17.0 4.9 %collective-permute-start.1 = (bf16[2,1,1,1,1,16,1792]{6,5,4,3,2,1,0:T(8,128)(2,1)S(1)}, bf16[2,1,1,1,1,16,1792]{6,5,4,3,2,1,0:T(8,128)(2,1)S(1)}, u32[]{:S(2)}, u32[]{:S(2)}) collective-permute-start(bf16[2,1,1,1,1,16,1792]{6,5,4,3,2,1,0:T(8,128)(2,1)S(1)} %pad_maximum_fusion.4), channel_id=1, source_target_pairs={{0,8},{1,9},{2,10},{3,11},{4,12},{5,13},{6,14},{7,15},{8,0},{9,1},... | collective-permute-start | bytes 344072 | tf_op jit(solution)/shard_map/ppermute | solution.py:847
  21.9 7.1 %collective-permute-start.2 = (bf16[2,2,1,1,1,16,1792]{6,5,4,3,2,1,0:T(8,128)(2,1)S(1)}, bf16[2,2,1,1,1,16,1792]{6,5,4,3,2,1,0:T(8,128)(2,1)S(1)}, u32[]{:S(2)}, u32[]{:S(2)}) collective-permute-start(bf16[2,2,1,1,1,16,1792]{6,5,4,3,2,1,0:T(8,128)(2,1)S(1)} %pad_maximum_fusion.3), channel_id=1, source_target_pairs={{0,4},{1,5},{2,6},{3,7},{4,0},{5,1},{6,2},{7,3},{8,12},{9,13},{10,... | collective-permute-start | bytes 688136 | tf_op jit(solution)/shard_map/ppermute | solution.py:847
  29.1 8.5 %collective-permute-start.3 = (bf16[2,2,2,1,1,16,1792]{6,5,4,3,2,1,0:T(8,128)(2,1)S(1)}, bf16[2,2,2,1,1,16,1792]{6,5,4,3,2,1,0:T(8,128)(2,1)S(1)}, u32[]{:S(2)}, u32[]{:S(2)}) collective-permute-start(bf16[2,2,2,1,1,16,1792]{6,5,4,3,2,1,0:T(8,128)(2,1)S(1)} %pad_maximum_fusion.2), channel_id=1, source_target_pairs={{0,2},{1,3},{2,0},{3,1},{4,6},{5,7},{6,4},{7,5},{8,10},{9,11},{10,... | collective-permute-start | bytes 1376264 | tf_op jit(solution)/shard_map/ppermute | solution.py:847
  37.8 2.5 collective-permute-start.4
  160.6 4.7 %collective-permute-start.5 = (bf16[2,2,2,2,1,144,512]{6,5,4,3,2,1,0:T(8,128)(2,1)S(1)}, bf16[2,2,2,2,1,144,512]{6,5,4,3,2,1,0:T(8,128)(2,1)}, u32[]{:S(2)}, u32[]{:S(2)}) collective-permute-start(bf16[2,2,2,2,1,144,512]{6,5,4,3,2,1,0:T(8,128)(2,1)S(1)} %dynamic-slice_convert_fusion), channel_id=1, source_target_pairs={{0,1},{1,0},{2,3},{3,2},{4,5},{5,4},{6,7},{7,6},{8,9},{9,8},{10,11... | collective-permute-start | bytes 7077896 | tf_op jit(solution)/shard_map/ppermute | solution.py:847
  169.4 28.3 %collective-permute-start.6 = (bf16[2,2,2,1,1,144,512]{6,5,4,3,2,1,0:T(8,128)(2,1)S(1)}, bf16[2,2,2,1,1,144,512]{6,5,4,3,2,1,0:T(8,128)(2,1)S(1)}, u32[]{:S(2)}, u32[]{:S(2)}) collective-permute-start(bf16[2,2,2,1,1,144,512]{6,5,4,3,2,1,0:T(8,128)(2,1)S(1)} %dynamic-slice_convert_fusion.1), channel_id=1, source_target_pairs={{0,2},{1,3},{2,0},{3,1},{4,6},{5,7},{6,4},{7,5},{8,10},{9,11},{10,... | collective-permute-start | bytes 3538952 | tf_op jit(solution)/shard_map/ppermute | solution.py:847
  198.3 14.9 %collective-permute-start.7 = (bf16[2,2,1,1,1,144,512]{6,5,4,3,2,1,0:T(8,128)(2,1)S(1)}, bf16[2,2,1,1,1,144,512]{6,5,4,3,2,1,0:T(8,128)(2,1)S(1)}, u32[]{:S(2)}, u32[]{:S(2)}) collective-permute-start(bf16[2,2,1,1,1,144,512]{6,5,4,3,2,1,0:T(8,128)(2,1)S(1)} %dynamic-slice_convert_fusion.3), channel_id=1, source_target_pairs={{0,4},{1,5},{2,6},{3,7},{4,0},{5,1},{6,2},{7,3},{8,12},{9,13},{10,... | collective-permute-start | bytes 1769480 | tf_op jit(solution)/shard_map/ppermute | solution.py:847
  251.7 2.5 collective-permute-start.8
  256.8 12.8 %collective-permute-start.9 = (bf16[2,2,2,1,1,16,1792]{6,5,4,3,2,1,0:T(8,128)(2,1)}, bf16[2,2,2,1,1,16,1792]{6,5,4,3,2,1,0:T(8,128)(2,1)S(1)}, u32[]{:S(2)}, u32[]{:S(2)}) collective-permute-start(bf16[2,2,2,1,1,16,1792]{6,5,4,3,2,1,0:T(8,128)(2,1)} %dynamic-slice_convert_fusion.4), channel_id=1, source_target_pairs={{0,2},{1,3},{2,0},{3,1},{4,6},{5,7},{6,4},{7,5},{8,10},{9,11},{10,... | collective-permute-start | bytes 1376264 | tf_op jit(solution)/shard_map/ppermute | solution.py:847
  258.4 13.0 %collective-permute-start.13 = (bf16[2,1,1,1,1,144,512]{6,5,4,3,2,1,0:T(8,128)(2,1)S(1)}, bf16[2,1,1,1,1,144,512]{6,5,4,3,2,1,0:T(8,128)(2,1)S(1)}, u32[]{:S(2)}, u32[]{:S(2)}) collective-permute-start(bf16[2,1,1,1,1,144,512]{6,5,4,3,2,1,0:T(8,128)(2,1)S(1)} %dynamic-slice_convert_fusion.5), channel_id=1, source_target_pairs={{0,8},{1,9},{2,10},{3,11},{4,12},{5,13},{6,14},{7,15},{8,0},{9,1},... | collective-permute-start | bytes 884744 | tf_op jit(solution)/shard_map/ppermute | solution.py:847
  269.7 6.9 %collective-permute-start.10 = (bf16[2,2,1,1,1,16,1792]{6,5,4,3,2,1,0:T(8,128)(2,1)S(1)}, bf16[2,2,1,1,1,16,1792]{6,5,4,3,2,1,0:T(8,128)(2,1)S(1)}, u32[]{:S(2)}, u32[]{:S(2)}) collective-permute-start(bf16[2,2,1,1,1,16,1792]{6,5,4,3,2,1,0:T(8,128)(2,1)S(1)} %dynamic-slice_convert_fusion.6), channel_id=1, source_target_pairs={{0,4},{1,5},{2,6},{3,7},{4,0},{5,1},{6,2},{7,3},{8,12},{9,13},{10,... | collective-permute-start | bytes 688136 | tf_op jit(solution)/shard_map/ppermute | solution.py:847
  276.7 5.0 %collective-permute-start.11 = (bf16[2,1,1,1,1,16,1792]{6,5,4,3,2,1,0:T(8,128)(2,1)S(1)}, bf16[2,1,1,1,1,16,1792]{6,5,4,3,2,1,0:T(8,128)(2,1)S(1)}, u32[]{:S(2)}, u32[]{:S(2)}) collective-permute-start(bf16[2,1,1,1,1,16,1792]{6,5,4,3,2,1,0:T(8,128)(2,1)S(1)} %dynamic-slice_convert_fusion.8), channel_id=1, source_target_pairs={{0,8},{1,9},{2,10},{3,11},{4,12},{5,13},{6,14},{7,15},{8,0},{9,1},... | collective-permute-start | bytes 344072 | tf_op jit(solution)/shard_map/ppermute | solution.py:847
  278.4 9.8 %collective-permute-start.14 = (bf16[1,1,1,1,1,144,512]{6,5,4,3,2,1,0:T(8,128)(2,1)S(1)}, bf16[1,1,1,1,1,144,512]{6,5,4,3,2,1,0:T(8,128)(2,1)S(1)}, u32[]{:S(2)}, u32[]{:S(2)}) collective-permute-start(bf16[1,1,1,1,1,144,512]{6,5,4,3,2,1,0:T(8,128)(2,1)S(1)} %dynamic-slice_convert_fusion.7), channel_id=1, source_target_pairs={{0,16},{1,17},{2,18},{3,19},{4,20},{5,21},{6,22},{7,23},{8,24},{9,... | collective-permute-start | bytes 442376 | tf_op jit(solution)/shard_map/ppermute | solution.py:847
  281.7 7.3 %collective-permute-start.12 = (bf16[1,1,1,1,1,16,1792]{6,5,4,3,2,1,0:T(8,128)(2,1)S(1)}, bf16[1,1,1,1,1,16,1792]{6,5,4,3,2,1,0:T(8,128)(2,1)S(1)}, u32[]{:S(2)}, u32[]{:S(2)}) collective-permute-start(bf16[1,1,1,1,1,16,1792]{6,5,4,3,2,1,0:T(8,128)(2,1)S(1)} %dynamic-slice_convert_fusion.9), channel_id=1, source_target_pairs={{0,16},{1,17},{2,18},{3,19},{4,20},{5,21},{6,22},{7,23},{8,24},{9,... | collective-permute-start | bytes 172040 | tf_op jit(solution)/shard_map/ppermute | solution.py:847
Sparse Core Ops, SparseCore 0:
  11.5 66.6 all-gather.2

commit v3 on v2

--- a/solution.py
+++ b/solution.py
@@ -532,9 +532,9 @@
 
 
 def ffn_kernel(
-    x_ref, dy_ref, o_ref, norms_ref, w_ref,
-    out_ref, dx_ref, do_ref, g_ref, g_norm_ref,
-    h_scr, ht_scr, dyt_scr, y_scr, dh_scr, gt_scr,
+    place, x_ref, dy_ref, o_ref, norms_ref, w_ref,
+    out_ref, dx_ref, do_ref, sent_ref, kept_ref, g_norm_ref,
+    g_ref, h_scr, ht_scr, dyt_scr, y_scr, dh_scr, hat_scr, gt_scr,
 ):
     tile, width = x_ref.shape
     hidden = gt_scr.shape[1]
@@ -544,31 +544,21 @@
     out_rows = slice((slabs + 1) * ROWS, (2 * slabs + 1) * ROWS)
     step = pl.program_id(0)
 
-    @pl.when(step == 0)
-    def _():
-        g_ref[...] = jnp.zeros_like(g_ref)
-        gt_scr[...] = jnp.zeros_like(gt_scr)
-        g_norm_ref[...] = jnp.zeros_like(g_norm_ref)
-
-    o_t = o_ref[...]
+    share = parts // slabs
+    fresh = step == 0
+
+    def add_to(ref, at, value):
+        ref[at] = value + jnp.where(fresh, 0.0, ref[at])
+
+    root = math.sqrt(2.0 / math.pi)
+    w_in = [w_ref[:, c * ROWS : (c + 1) * ROWS, :].reshape(width, width) for c in range(slabs)]
+    w_out = [
+        w_ref[c * share : (c + 1) * share, out_rows, :].reshape(width, width) for c in range(slabs)
+    ]
     w_o = w_ref[:, whole_rows, :].reshape(width, width)
-    x_one = x_ref[...].astype(f32) + dot(o_t.T, w_o)
-    hat, rstd = norm_stats(x_one)
-    h_two = (hat * norms_ref[2:3, :] + norms_ref[3:4, :]).astype(bf16)
-    h_scr[...] = h_two
-    ht_scr[...] = h_two.T
-    dyt_scr[...] = dy_ref[...].T
-    y_scr[...] = x_one
-    dh_scr[...] = jnp.zeros_like(dh_scr)
-    root = math.sqrt(2.0 / math.pi)
-
-    def before(c):
-        w_in = w_ref[:, c * ROWS : (c + 1) * ROWS, :].reshape(width, width)
-        share = parts // slabs
-        w_out = w_ref[c * share : (c + 1) * share, out_rows, :].reshape(width, width)
-        act = dot(h_scr[...], w_in)
-        d_hid = dot_nt(dy_ref[...], w_out)
-        return w_in, w_out, act, d_hid
+
+    def d_hidden(c):
+        return dot_nt(dy_ref[...], w_out[c])
 
     def between(act, d_hid):
         square = act * act
@@ -578,44 +568,71 @@
         slope = gate + hid * (1.0 - curve) * (root + (3.0 * root * 0.044715) * square)
         return hid.astype(bf16), (d_hid * slope).astype(bf16)
 
-    def after(c, w_in, w_out, hid, d_act):
+    o_t = o_ref[...]
+    x_one = x_ref[...].astype(f32) + dot(o_t.T, w_o)
+    d_hid = d_hidden(0)
+    dyt_scr[...] = dy_ref[...].T
+    hat, rstd = norm_stats(x_one)
+    h_two = (hat * norms_ref[2:3, :] + norms_ref[3:4, :]).astype(bf16)
+    h_scr[...] = h_two
+    hat_scr[...] = hat
+    y_scr[...] = x_one
+    act = dot(h_scr[...], w_in[0])
+    ht_scr[...] = h_two.T
+    for c in range(slabs):
+        this_act, this_d = act, d_hid
+        if c + 1 < slabs:
+            d_hid = d_hidden(c + 1)
+            act = dot(h_scr[...], w_in[c + 1])
+        hid, d_act = between(this_act, this_d)
+        more = dot_nt(d_act, w_in[c])
+        dh_scr[...] = more if c == 0 else dh_scr[...] + more
+        y_scr[...] += dot(hid, w_out[c])
         cols = slice(c * width, (c + 1) * width)
-        y_scr[...] += dot(hid, w_out)
-        gt_scr[:, cols] += dot(dyt_scr[...], hid)
-        slab = slice(c * ROWS, (c + 1) * ROWS)
-        g_ref[:, slab, :] += dot(ht_scr[...], d_act).reshape(parts, ROWS, width)
-        dh_scr[...] += dot_nt(d_act, w_in)
-
-    ahead = before(0)
-    for c in range(slabs):
-        w_in, w_out, act, d_hid = ahead
-        if c + 1 < slabs:
-            ahead = before(c + 1)
-        hid, d_act = between(act, d_hid)
-        after(c, w_in, w_out, hid, d_act)
-    out_ref[...] = y_scr[...].astype(bf16)
+        add_to(gt_scr, (slice(None), cols), dot(dyt_scr[...], hid))
+        slab = (slice(None), slice(c * ROWS, (c + 1) * ROWS), slice(None))
+        add_to(g_ref, slab, dot(ht_scr[...], d_act).reshape(parts, ROWS, width))
     d_h = dh_scr[...]
-    g_norm_ref[2:3, :] += jnp.sum(d_h * hat, axis=0, keepdims=True)
-    g_norm_ref[3:4, :] += jnp.sum(d_h, axis=0, keepdims=True)
+    hat = hat_scr[...]
     d_x = dy_ref[...].astype(f32) + norm_back(d_h, hat, rstd, norms_ref[2:3, :])
     dx_ref[...] = d_x
     d_z = d_x.astype(bf16)
-    g_ref[:, whole_rows, :] += dot(o_t, d_z).reshape(parts, ROWS, width)
     do_ref[...] = dot_nt(d_z, w_o).astype(bf16)
+    add_to(g_ref, (slice(None), whole_rows, slice(None)), dot(o_t, d_z).reshape(parts, ROWS, width))
+    add_to(g_norm_ref, (slice(2, 3), slice(None)), jnp.sum(d_h * hat, axis=0, keepdims=True))
+    add_to(g_norm_ref, (slice(3, 4), slice(None)), jnp.sum(d_h, axis=0, keepdims=True))
+    out_ref[...] = y_scr[...].astype(bf16)
+
+    @pl.when(fresh)
+    def _():
+        g_norm_ref[0:2, :] = jnp.zeros_like(g_norm_ref[0:2, :])
+        g_norm_ref[4:, :] = jnp.zeros_like(g_norm_ref[4:, :])
 
     @pl.when(step == pl.num_programs(0) - 1)
     def _():
-        share = parts // slabs
         for c in range(slabs):
             g_ref[c * share : (c + 1) * share, out_rows, :] = gt_scr[
                 :, c * width : (c + 1) * width
             ].T.reshape(share, slabs * ROWS, width)
-
-
-def ffn(x, dy, o_t, norms, w_two):
+        halves(place, sent_ref, kept_ref, lambda i: g_ref[i])
+
+
+def halves(place, sent_ref, kept_ref, block):
+    mine = place[0] & 1
+
+    def one(i, carry):
+        sent_ref[i] = block(2 * i + 1 - mine).astype(bf16)
+        kept_ref[i] = block(2 * i + mine)
+        return carry
+
+    lax.fori_loop(0, sent_ref.shape[0], one, 0)
+
+
+def ffn(place, x, dy, o_t, norms, w_two):
     slot, width = x.shape
     hidden = (w_two.shape[1] // ROWS - 1) // 2 * width
     grid = slot // TILE
+    half = (w_two.shape[0] // 2, *w_two.shape[1:])
     row = pl.BlockSpec((TILE, width), lambda i: (i, 0))
 
     def once(shape):
@@ -625,24 +642,28 @@
         ffn_kernel,
         grid=(grid,),
         in_specs=[
+            smem(),
             row,
             row,
             pl.BlockSpec((width, TILE), lambda i: (0, i)),
             once(norms.shape),
             once(w_two.shape),
         ],
-        out_specs=[row, row, row, once(w_two.shape), once((8, width))],
+        out_specs=[row, row, row, once(half), once(half), once((8, width))],
         out_shape=[
             jax.ShapeDtypeStruct((slot, width), bf16),
             jax.ShapeDtypeStruct((slot, width), f32),
             jax.ShapeDtypeStruct((slot, width), bf16),
-            jax.ShapeDtypeStruct(w_two.shape, f32),
+            jax.ShapeDtypeStruct(half, bf16),
+            jax.ShapeDtypeStruct(half, f32),
             jax.ShapeDtypeStruct((8, width), f32),
         ],
         scratch_shapes=[
+            pltpu.VMEM(w_two.shape, f32),
             pltpu.VMEM((TILE, width), bf16),
             pltpu.VMEM((width, TILE), bf16),
             pltpu.VMEM((width, TILE), bf16),
+            pltpu.VMEM((TILE, width), f32),
             pltpu.VMEM((TILE, width), f32),
             pltpu.VMEM((TILE, width), f32),
             pltpu.VMEM((width, hidden), f32),
@@ -654,13 +675,13 @@
             transcendentals=slot * hidden,
         ),
         name="ffn",
-    )(x, dy, o_t, norms, w_two)
+    )(place, x, dy, o_t, norms, w_two)
 
 
 def project_back_kernel(
-    lens, x_ref, dx_ref, du_ref, norms_ref, w_ref, g_sort_ref, g_two_ref, *refs, slot
+    place, lens, x_ref, dx_ref, du_ref, norms_ref, w_ref, g_sort_ref, g_two_ref, *refs, slot
 ):
-    *d_refs, grad_ref, g_ref, g_norm_ref = refs
+    *d_refs, grad_ref, sent_ref, kept_ref, g_ref, g_norm_ref = refs
     tile, width = x_ref.shape
     step = pl.program_id(0)
 
@@ -672,8 +693,9 @@
     pairs = width // LANES
     ends = ends_of(lens, slot)
     blocks = SUB // BLOCK
-    first = []
-    for r in range(0, tile, SUB):
+    starts = range(0, tile, SUB)
+    d_hs, hats, rstds, h_ones = [], [], [], []
+    for r in starts:
         rows = slice(r, r + SUB)
         places = step * tile + r + iota((SUB, 1), 0)
         live = places < end_at(places, ends, slot)
@@ -686,20 +708,30 @@
                 [ref[rows, :] for ref in d_refs[part * pairs : (part + 1) * pairs]], axis=1
             )
             d_h = d_h + dot_nt(d_part, w_ref[:, cols])
-        first.append(d_h)
-    hats = []
-    for r, d_h in zip(range(0, tile, SUB), first):
-        rows = slice(r, r + SUB)
+        d_hs.append(d_h)
         hat, rstd = norm_stats(x_ref[rows, :].astype(f32))
-        hats.append((hat * norms_ref[0:1, :] + norms_ref[1:2, :]).astype(bf16))
-        g_norm_ref[0:1, :] += jnp.sum(d_h * hat, axis=0, keepdims=True)
-        g_norm_ref[1:2, :] += jnp.sum(d_h, axis=0, keepdims=True)
-        grad_ref[rows, :] = dx_ref[rows, :] + norm_back(d_h, hat, rstd, norms_ref[0:1, :])
-    h_one = jnp.concatenate(hats, axis=0)
+        hats.append(hat)
+        rstds.append(rstd)
+        h_ones.append((hat * norms_ref[0:1, :] + norms_ref[1:2, :]).astype(bf16))
+    h_one = jnp.concatenate(h_ones, axis=0)
+
+    def back(at):
+        rows = slice(at * SUB, (at + 1) * SUB)
+        g_norm_ref[0:1, :] += jnp.sum(d_hs[at] * hats[at], axis=0, keepdims=True)
+        g_norm_ref[1:2, :] += jnp.sum(d_hs[at], axis=0, keepdims=True)
+        grad_ref[rows, :] = dx_ref[rows, :] + norm_back(
+            d_hs[at], hats[at], rstds[at], norms_ref[0:1, :]
+        )
+
+    done = 0
     for part in range(3):
         cols = slice(part * width, (part + 1) * width)
         d_part = jnp.concatenate([ref[...] for ref in d_refs[part * pairs : (part + 1) * pairs]], axis=1)
         g_ref[:, cols] += dot_tn(h_one, d_part)
+        until = len(starts) * (part + 1) // 3
+        for at in range(done, until):
+            back(at)
+        done = until
 
     @pl.when(step == pl.num_programs(0) - 1)
     def _():
@@ -707,20 +739,29 @@
         small = g_norm_ref[...] + g_two_ref[...]
         rest = jnp.zeros((LANES - small.shape[0], width), f32)
         g_ref[:, 3 * width + LANES :] = jnp.concatenate([small, rest], axis=0).T
-
-
-def project_back(lens, x, d_x, d_q, d_k, d_v, d_u, norms, w_one, g_sort, g_two):
+        rows = sent_ref.shape[1]
+        halves(
+            place,
+            sent_ref,
+            kept_ref,
+            lambda i: g_ref[pl.ds(pl.multiple_of(i * rows, rows), rows), :],
+        )
+
+
+def project_back(place, lens, x, d_x, d_q, d_k, d_v, d_u, norms, w_one, g_sort, g_two):
     slot, width = x.shape
     grid = slot // WIDE
     row = pl.BlockSpec((WIDE, width), lambda i: (i, 0))
+    half = (width // ROWS // 2, ROWS, w_one.shape[1])
 
     def once(shape):
-        return pl.BlockSpec(shape, lambda i: (0, 0), pipeline_mode=pl.Buffered(1))
+        return pl.BlockSpec(shape, lambda i: (0,) * len(shape), pipeline_mode=pl.Buffered(1))
 
     return pl.pallas_call(
         functools.partial(project_back_kernel, slot=slot),
         grid=(grid,),
         in_specs=[
+            smem(),
             smem(),
             row,
             row,
@@ -731,18 +772,19 @@
             once(g_two.shape),
         ]
         + [pl.BlockSpec((WIDE, LANES), lambda i: (i, 0))] * (3 * width // LANES),
-        out_specs=[row, once(w_one.shape)],
+        out_specs=[row, once(half), once(half)],
         out_shape=[
             jax.ShapeDtypeStruct((slot, width), f32),
-            jax.ShapeDtypeStruct(w_one.shape, f32),
-        ],
-        scratch_shapes=[pltpu.VMEM((8, width), f32)],
+            jax.ShapeDtypeStruct(half, bf16),
+            jax.ShapeDtypeStruct(half, f32),
+        ],
+        scratch_shapes=[pltpu.VMEM(w_one.shape, f32), pltpu.VMEM((8, width), f32)],
         compiler_params=params(),
         cost_estimate=pl.CostEstimate(
             flops=2 * slot * width * 6 * width, bytes_accessed=slot * width * 18, transcendentals=0
         ),
         name="project_back",
-    )(lens, x, d_x, d_u, norms, w_one, g_sort, g_two, *d_q, *d_k, *d_v)
+    )(place, lens, x, d_x, d_u, norms, w_one, g_sort, g_two, *d_q, *d_k, *d_v)
 
 
 def pack_kernel(wqkv, wo, wsort, win, wout, norms_t, one_ref, two_ref):
@@ -774,7 +816,9 @@
     )(wqkv, wo, wsort, win, wout, norms.T)
 
 
-def adamw_kernel(one_ref, two_ref, *refs):
+def adamw_kernel(one_kept, one_came, two_kept, two_came, *refs):
+    one_ref = one_kept[...] + one_came[...].astype(f32)
+    two_ref = two_kept[...] + two_came[...].astype(f32)
     masters, moments, squares, outs = refs[:6], refs[6:12], refs[12:18], refs[18:]
     rows, width = masters[1].shape
     wide = masters[0].shape[1]
@@ -804,7 +848,7 @@
 
 def adamw(one, two, masters, moments, squares):
     flip = lambda group: (*group[:5], group[5].T)
-    args = (one, two, *flip(masters), *flip(moments), *flip(squares))
+    args = (*one, *two, *flip(masters), *flip(moments), *flip(squares))
     shapes = [a.shape for a in flip(masters)]
     outs = pl.pallas_call(
         adamw_kernel,
@@ -832,15 +876,22 @@
     )
 
 
-def ungroup(grads, size, rows, slabs):
+def device_halves(place, sent, kept, size, rows, slabs):
     if rows == ROWS:
-        return grads
+        return sent, kept
+    mine = place[0] & 1
+    low = jnp.where(mine == 0, kept, sent.astype(f32))
+    high = jnp.where(mine == 0, sent.astype(f32), kept)
+    grads = jnp.stack([low, high], axis=1).reshape((-1,) + kept.shape[1:])
     times = ROWS // rows
     width = grads.shape[-1]
-    inner = grads[:, : (slabs + 1) * ROWS].reshape(size // times, slabs + 1, times, rows, width)
-    outer = grads[:, (slabs + 1) * ROWS :].reshape(size // times, times, slabs, rows, width)
+    cut = (slabs + 1) * ROWS
+    inner = grads[:, :cut].reshape(size // times, slabs + 1, times, rows, width)
+    outer = grads[:, cut:].reshape(size // times, times, slabs, rows, width)
     block = jnp.concatenate([inner.transpose(0, 2, 1, 3, 4), outer], axis=2)
-    return block.reshape(size, (2 * slabs + 1) * rows, width)
+    block = block.reshape(size // 2, 2, (2 * slabs + 1) * rows, width)
+    sent = lax.dynamic_index_in_dim(block, 1 - mine, 1, keepdims=False).astype(bf16)
+    return sent, lax.dynamic_index_in_dim(block, mine, 1, keepdims=False)
 
 
 def swap(value, bit, size):
@@ -861,31 +912,67 @@
     return held.reshape((size * block.shape[0],) + block.shape[1:])
 
 
+def pick(value, bit, index, lead):
+    return lax.dynamic_index_in_dim(value, index, lead.index(bit), keepdims=False)
+
+
 class ScatterSum:
-    def __init__(self, value, size):
+    def __init__(self, sent, kept, size, axis):
         self.size, self.count = size, size.bit_length() - 1
-        self.rest = value.shape[1:]
-        self.held = value.reshape((2,) * self.count + value.shape[0:0] + (value.shape[0] // size,) + self.rest)
-        self.bit = 0
-
-    def begin(self):
-        place = lax.axis_index("dp")
-        axis = self.count - 1 - self.bit
-        mine = (place >> self.bit) & 1
-        sent = lax.dynamic_index_in_dim(self.held, 1 - mine, axis, keepdims=True).astype(bf16)
-        self.kept = lax.dynamic_index_in_dim(self.held, mine, axis, keepdims=True)
-        self.came = swap(sent, self.bit, self.size)
-        self.bit += 1
-
-    def end(self):
-        self.held = self.kept + self.came.astype(f32)
-        return self.held
-
-    def finish(self):
-        while self.bit < self.count:
-            self.begin()
-            self.end()
-        return self.held.reshape((-1,) + self.rest)
+        self.axis = axis
+        self.bits = list(range(self.count - 1, 0, -1))
+        self.place = lax.axis_index("dp")
+        self.rest = kept.shape[1:]
+        lead = (2,) * (self.count - 1)
+        self.kept = [(kept.reshape(lead + self.rest), self.bits)]
+        self.came = [swap(sent, 0, size).reshape(lead + self.rest)]
+        self.plan = [(1, 2), (2, 1)] + [(bit,) for bit in range(3, self.count)]
+
+    def step(self):
+        bits = self.plan.pop(0)
+        parts = []
+        if len(bits) > len(self.kept):
+            kept, lead = self.kept[0]
+            middle = len(lead) + self.axis
+            cut = kept.shape[middle] // 2
+            for turn in range(2):
+                at = (slice(None),) * middle + (slice(turn * cut, (turn + 1) * cut),)
+                parts.append((kept[at], self.came[0][at], lead))
+        elif len(bits) < len(self.kept):
+            lead = self.kept[0][1]
+            middle = len(lead) + self.axis
+            parts = [
+                (
+                    jnp.concatenate([kept for kept, _ in self.kept], axis=middle),
+                    jnp.concatenate(self.came, axis=middle),
+                    lead,
+                )
+            ]
+        else:
+            parts = [(kept, came, lead) for (kept, lead), came in zip(self.kept, self.came)]
+        self.kept, self.came, self.sent = [], [], []
+        for bit, (kept, came, lead) in zip(bits, parts):
+            mine = (self.place >> bit) & 1
+            self.sent.append(
+                (pick(kept, bit, 1 - mine, lead) + pick(came, bit, 1 - mine, lead).astype(f32)).astype(bf16)
+            )
+            left = [b for b in lead if b != bit]
+            self.kept.append((pick(kept, bit, mine, lead) + pick(came, bit, mine, lead).astype(f32), left))
+        self.bits = bits
+
+    def send(self):
+        self.came = [swap(sent, bit, self.size) for sent, bit in zip(self.sent, self.bits)]
+
+    def after(self, values):
+        self.came, values = lax.optimization_barrier((self.came, values))
+        return values
+
+    def before(self, values):
+        self.sent, values = lax.optimization_barrier((self.sent, values))
+        return values
+
+    def last(self):
+        return self.kept[0][0].reshape(self.rest), self.came[0].reshape(self.rest)
 
 
 def body(size, x, dy, lens, partner, *state):
@@ -893,6 +980,7 @@
     masters, moments, squares = state[:6], state[6:12], state[12:]
     rows = masters[0].shape[0]
     slabs = masters[3].shape[1] // width
+    place = lax.axis_index("dp").astype(jnp.int32).reshape((1,))
     pack_one, pack_two = pack(masters)
     w_one = gather(pack_one, size)
     w_two = regroup(lax.all_gather(pack_two, "dp", axis=0), size, rows, slabs)
@@ -900,22 +988,43 @@
     q, k, v, u, norms = project(lens, x, w_one)
     bias, steps = sort_net(lens, u, w_one, partner, slot)
     o_t, probs = attend(lens, partner, bias, q, k, v)
-    out, d_x, d_o, g_rest, g_two = ffn(x, dy, o_t, norms, w_two)
-    two = ungroup(g_rest, size, rows, slabs)
-    two = ScatterSum(two.reshape((-1, width)), size)
-    back = []
-    for pair in range(width // LANES):
-        two.begin()
-        back.append(attend_back(pair, partner, q, d_o, probs, k, v))
-        held = two.end()
-        q, d_o, two.held = lax.optimization_barrier((q, d_o, held))
-    d_q, d_k, d_v, d_bias = zip(*back)
-    d_u, g_sort = sort_back(lens, u, w_one, partner, d_bias, steps, slot)
-    two.begin()
-    grad_in, g_one = project_back(lens, x, d_x, d_q, d_k, d_v, d_u, norms, w_one, g_sort, g_two)
-    two.end()
-    one = ScatterSum(g_one, size).finish()
-    outs = adamw(one, two.finish(), masters, moments, squares)
+    out, d_x, d_o, sent, kept, g_two = ffn(place, x, dy, o_t, norms, w_two)
+    sent, kept = device_halves(place, sent, kept, size, rows, slabs)
+    two = ScatterSum(sent, kept, size, 0)
+
+    def back(pair):
+        return attend_back(pair, partner, q, d_o, probs, k, v)
+
+    back_0 = two.after(back(0))
+    two.step()
+    q, d_o = two.before((q, d_o))
+    two.send()
+    back_1 = back(1)
+    back_2 = back(2)
+    back_1, back_2 = two.after((back_1, back_2))
+    two.step()
+    q, d_o = two.before((q, d_o))
+    two.send()
+    back_3 = two.after(back(3))
+    two.step()
+    u, back_3 = two.before((u, back_3))
+    two.send()
+    d_q, d_k, d_v, d_bias = zip(back_0, back_1, back_2, back_3)
+    d_u, g_sort = two.after(sort_back(lens, u, w_one, partner, d_bias, steps, slot))
+    while two.plan:
+        two.step()
+        d_u = two.before(d_u)
+        two.send()
+    grad_in, sent, kept = project_back(
+        place, lens, x, d_x, d_q, d_k, d_v, d_u, norms, w_one, g_sort, g_two
+    )
+    grad_in, sent, kept = two.after((grad_in, sent, kept))
+    sent, kept = device_halves(place, sent, kept, size, rows, 0)
+    one = ScatterSum(sent, kept, size, 1)
+    while one.plan:
+        one.step()
+        one.send()
+    outs = adamw(one.last(), two.last(), masters, moments, squares)
     return (out, grad_in, *outs)
 
 

time: 300 us -> 277 us (0.923)
  waiting for transfers between devices: 65.8 us -> 47.3 us
  Pallas kernels: 180 us -> 174 us
  local copies, waits for them, and re-layouts: 5.49 us -> 10.9 us
  other arithmetic: 10.5 us -> 5.81 us
    ppermute x15 -> x19, waiting for transfers between devices: 61.7 us -> 43.3 us  [swap(): return lax.ppermute(value, 'dp', [(i, i ^ 1 << bit) for i in range(size)])]
    slice x0 -> x7, local copies, waits for them, and re-layouts: none -> 6.48 us  [step(): parts.append((kept[at], self.came[0][at], lead))]
    pallas_call x1, Pallas kernels: 79.7 us -> 73.7 us  [ffn(): pl.pallas_call(ffn_kernel, grid=(grid,), in_specs=[smem(), row, row, pl.B...]
    convert_element_type x10 -> x0, local copies, waits for them, and re-layouts: 5.49 us -> none  [begin(): lax.dynamic_index_in_dim(self.held, 1 - mine, axis, keepdims=True)]
    add x8 -> x4, other arithmetic: 6.5 us -> 1.25 us  [step(): pick(kept, bit, mine, lead) + pick(came, bit, mine, lead).astype(f32)]
    unnamed x0 -> x10, local copies, waits for them, and re-layouts: none -> 3.28 us
    ppermute x15 -> x19, starting transfers between devices: 22.8 us -> 23.2 us  [swap(): return lax.ppermute(value, 'dp', [(i, i ^ 1 << bit) for i in range(size)])]
  transfers between devices with their start and end apart: 16 -> 20, of which waited for: 14 -> 13; matrix products, arithmetic and copies ran while one was open for 1% -> 3% of each run, Pallas kernels for 20% -> 35%
where the time goes in v3:
time: 277 us; the launch traced here: 276 us
  Pallas kernels  174 us (63%)
  waiting for transfers between devices  47.3 us (17%)
  starting transfers between devices  23.2 us (8%)
  between operations  14.4 us (5%)
  local copies, waits for them, and re-layouts  10.9 us (4%)
  other arithmetic  5.81 us (2%)
    pallas_call x1, Pallas kernels, ffn(): pl.pallas_call(ffn_kernel, grid=(grid,), in_specs=[smem(), row, row, pl.B...  73.7 us
    ppermute x19, waiting for transfers between devices, swap(): return lax.ppermute(value, 'dp', [(i, i ^ 1 << bit) for i in range(size)])  43.3 us
    pallas_call x4, Pallas kernels, attend_back(): pl.pallas_call(attend_back_kernel, grid=(grid,), in_specs=[smem(), row, r...  36.1 us
    pallas_call x1, Pallas kernels, project_back(): pl.pallas_call(functools.partial(project_back_kernel, slot=slot), grid=(g...  23.4 us
    ppermute x19, starting transfers between devices, swap(): return lax.ppermute(value, 'dp', [(i, i ^ 1 << bit) for i in range(size)])  23.2 us
    pallas_call x1, Pallas kernels, attend(): pl.pallas_call(functools.partial(attend_kernel, slot=slot), grid=(grid,),...  15.4 us
    pallas_call x1, Pallas kernels, project(): pl.pallas_call(functools.partial(project_kernel, slot=slot), grid=(grid,)...  12.1 us
    slice x7, local copies, waits for them, and re-layouts, step(): parts.append((kept[at], self.came[0][at], lead))  6.48 us
  transfers between devices with their start and end apart: 20, of which 13 were waited for; matrix products, arithmetic and copies ran while one was open for 3% of the time, Pallas kernels for 35%

profile of v3, /device:TPU:0, one launch (start us, length us, event | category | flops | bytes accessed | tf_op | source)
XLA Modules:
  0.0 275.9 jit_solution(12243813501570190844)
XLA Ops:
  9.0 4.1 %collective-permute-start = (bf16[1,1,1,1,1,16,1792]{6,5,4,3,2,1,0:T(8,128)(2,1)}, bf16[1,1,1,1,1,16,1792]{6,5,4,3,2,1,0:T(8,128)(2,1)S(1)}, u32[]{:S(2)}, u32[]{:S(2)}) collective-permute-start(bf16[1,1,1,1,1,16,1792]{6,5,4,3,2,1,0:T(8,128)(2,1)} %bitcast.121), channel_id=1, source_target_pairs={{0,16},{1,17},{2,18},{3,19},{4,20},{5,21},{6,22},{7,23},{8,24},{9,... | collective-permute-start | bytes 172040 | tf_op jit(solution)/shard_map/ppermute | solution.py:898
  13.1 3.0 %collective-permute-done = bf16[1,1,1,1,1,16,1792]{6,5,4,3,2,1,0:T(8,128)(2,1)S(1)} collective-permute-done((bf16[1,1,1,1,1,16,1792]{6,5,4,3,2,1,0:T(8,128)(2,1)}, bf16[1,1,1,1,1,16,1792]{6,5,4,3,2,1,0:T(8,128)(2,1)S(1)}, u32[]{:S(2)}, u32[]{:S(2)}) %collective-permute-start) | collective-permute-done | bytes 57376 | tf_op jit(solution)/shard_map/ppermute | solution.py:898
  18.3 3.5 %collective-permute-done.1 = bf16[2,1,1,1,1,16,1792]{6,5,4,3,2,1,0:T(8,128)(2,1)S(1)} collective-permute-done((bf16[2,1,1,1,1,16,1792]{6,5,4,3,2,1,0:T(8,128)(2,1)S(1)}, bf16[2,1,1,1,1,16,1792]{6,5,4,3,2,1,0:T(8,128)(2,1)S(1)}, u32[]{:S(2)}, u32[]{:S(2)}) %collective-permute-start.1) | collective-permute-done | bytes 114720 | tf_op jit(solution)/shard_map/ppermute | solution.py:898
  23.7 5.3 %collective-permute-done.2 = bf16[2,2,1,1,1,16,1792]{6,5,4,3,2,1,0:T(8,128)(2,1)S(1)} collective-permute-done((bf16[2,2,1,1,1,16,1792]{6,5,4,3,2,1,0:T(8,128)(2,1)S(1)}, bf16[2,2,1,1,1,16,1792]{6,5,4,3,2,1,0:T(8,128)(2,1)S(1)}, u32[]{:S(2)}, u32[]{:S(2)}) %collective-permute-start.2) | collective-permute-done | bytes 229408 | tf_op jit(solution)/shard_map/ppermute | solution.py:898
  30.7 6.9 %collective-permute-done.3 = bf16[2,2,2,1,1,16,1792]{6,5,4,3,2,1,0:T(8,128)(2,1)S(1)} collective-permute-done((bf16[2,2,2,1,1,16,1792]{6,5,4,3,2,1,0:T(8,128)(2,1)S(1)}, bf16[2,2,2,1,1,16,1792]{6,5,4,3,2,1,0:T(8,128)(2,1)S(1)}, u32[]{:S(2)}, u32[]{:S(2)}) %collective-permute-start.3) | collective-permute-done | bytes 458784 | tf_op jit(solution)/shard_map/ppermute | solution.py:898
  37.8 2.5 collective-permute-done.4
  41.8 12.1 %project.1 = (bf16[4096,512]{1,0:T(8,128)(2,1)}, bf16[4096,512]{1,0:T(8,128)(2,1)}, bf16[4096,512]{1,0:T(8,128)(2,1)}, f32[128,512]{1,0:T(8,128)}, f32[8,512]{1,0:T(8,128)}) custom-call(s32[1,4]{1,0:T(1,128)} %lens.9, bf16[4096,512]{1,0:T(8,128)(2,1)} %x_ref.5, bf16[512,1792]{1,0:T(8,128)(2,1)} %bitcast.112), custom_call_target="tpu_custom_call" | custom-call | flops 6442450944 | bytes 16777216 | tf_op jit(solution)/shard_map/project/pallas_call | solution.py:127
  54.0 4.8 %sort_net.1 = (f32[1,128]{1,0:T(1,128)}, f32[16,128,128]{2,1,0:T(8,128)}) custom-call(s32[1,4]{1,0:T(1,128)} %lens.9, f32[128,512]{1,0:T(8,128)} %get-tuple-element.168.u_ref, bf16[512,1792]{1,0:T(8,128)(2,1)} %bitcast.113, s32[1,128]{1,0:T(1,128)} %partner_ref.3), custom_call_target="tpu_custom_call" | custom-call | flops 100000000 | bytes 10000000 | tf_op jit(solution)/shard_map/sort_net/pallas_call | solution.py:210
  58.8 15.4 %attend.1 = (bf16[512,4096]{1,0:T(8,128)(2,1)}, bf16[4,2048,256]{2,1,0:T(8,128)(2,1)}) custom-call(s32[1,4]{1,0:T(1,128)} %lens.9, s32[1,128]{1,0:T(1,128)} %partner_ref.3, f32[1,128]{1,0:T(1,128)} %get-tuple-element.122.bias, bf16[4096,512]{1,0:T(8,128)(2,1)} %get-tuple-element.155.q_ref, bf16[4096,512]{1,0:T(8,128)(2,1)} %get-tuple-element.124.k_ref, ...), custom_call_target="tpu_custom_call" | custom-call | flops 20000000000 | bytes 20971520 | tf_op jit(solution)/shard_map/attend/pallas_call | solution.py:396
  74.2 4.0 %all-gather.3.cloned.1.call-done = bf16[4608,512]{1,0:T(8,128)(2,1)} async-done(((bf16[144,512]{1,0:T(8,128)(2,1)}), bf16[4608,512]{1,0:T(8,128)(2,1)}) %all-gather.3.cloned.1.call-update) | async-done | bytes 4718608 | tf_op jit(solution)/shard_map/all_gather | solution.py:986
  78.2 73.7 %ffn.1 = (bf16[4096,512]{1,0:T(8,128)(2,1)}, f32[4096,512]{1,0:T(8,128)}, bf16[4096,512]{1,0:T(8,128)(2,1)}, bf16[16,144,512]{2,1,0:T(8,128)(2,1)}, f32[16,144,512]{2,1,0:T(8,128)}, /*index=5*/f32[8,512]{1,0:T(8,128)}) custom-call(s32[1]{0:T(128)} %bitcast.place, bf16[4096,512]{1,0:T(8,128)(2,1)} %x_ref.5, bf16[4096,512]{1,0:T(8,128)(2,1)} %dy_ref.1, ...), custom_call_target="tpu_custom_call" | custom-call | flops 57982058496 | bytes 29360128 | tf_op jit(solution)/shard_map/ffn/pallas_call | solution.py:641
  152.2 3.2 %fusion.38 = (f32[2,2,2,2,72,512]{5,4,3,2,1,0:T(8,128)S(1)}, f32[2,2,2,2,72,512]{5,4,3,2,1,0:T(8,128)S(1)}) fusion(f32[2,2,2,2,144,512]{5,4,3,2,1,0:T(8,128)} %bitcast.118), kind=kLoop, calls=%fused_computation.97 | loop fusion | bytes 9437184 | tf_op jit(solution)/shard_map/slice | solution.py:940
  156.0 9.1 %attend_back.4 = (bf16[4096,128]{1,0:T(8,128)(2,1)}, bf16[4096,128]{1,0:T(8,128)(2,1)}, bf16[4096,128]{1,0:T(8,128)(2,1)}, f32[1,128]{1,0:T(1,128)}) custom-call(s32[1,128]{1,0:T(1,128)} %partner_ref.3, bf16[4096,512]{1,0:T(8,128)(2,1)} %get-tuple-element.155.q_ref, bf16[4096,512]{1,0:T(8,128)(2,1)} %get-tuple-element.156.do_ref, ...), custom_call_target="tpu_custom_call" | custom-call | flops 10000000000 | bytes 8388608 | tf_op jit(solution)/shard_map/attend_back/pallas_call | solution.py:502
  172.5 9.0 %attend_back.5 = (bf16[4096,128]{1,0:T(8,128)(2,1)}, bf16[4096,128]{1,0:T(8,128)(2,1)}, bf16[4096,128]{1,0:T(8,128)(2,1)}, f32[1,128]{1,0:T(1,128)}) custom-call(s32[1,128]{1,0:T(1,128)} %partner_ref.3, bf16[4096,512]{1,0:T(8,128)(2,1)} %get-tuple-element.155.q_ref, bf16[4096,512]{1,0:T(8,128)(2,1)} %get-tuple-element.156.do_ref, ...), custom_call_target="tpu_custom_call" | custom-call | flops 10000000000 | bytes 8388608 | tf_op jit(solution)/shard_map/attend_back/pallas_call | solution.py:502
  181.5 9.0 %attend_back.6 = (bf16[4096,128]{1,0:T(8,128)(2,1)}, bf16[4096,128]{1,0:T(8,128)(2,1)}, bf16[4096,128]{1,0:T(8,128)(2,1)}, f32[1,128]{1,0:T(1,128)}) custom-call(s32[1,128]{1,0:T(1,128)} %partner_ref.3, bf16[4096,512]{1,0:T(8,128)(2,1)} %get-tuple-element.155.q_ref, bf16[4096,512]{1,0:T(8,128)(2,1)} %get-tuple-element.156.do_ref, ...), custom_call_target="tpu_custom_call" | custom-call | flops 10000000000 | bytes 8388608 | tf_op jit(solution)/shard_map/attend_back/pallas_call | solution.py:502
  193.1 9.0 %attend_back.7 = (bf16[4096,128]{1,0:T(8,128)(2,1)}, bf16[4096,128]{1,0:T(8,128)(2,1)}, bf16[4096,128]{1,0:T(8,128)(2,1)}, f32[1,128]{1,0:T(1,128)}) custom-call(s32[1,128]{1,0:T(1,128)} %partner_ref.3, bf16[4096,512]{1,0:T(8,128)(2,1)} %get-tuple-element.155.q_ref, bf16[4096,512]{1,0:T(8,128)(2,1)} %get-tuple-element.156.do_ref, ...), custom_call_target="tpu_custom_call" | custom-call | flops 10000000000 | bytes 8388608 | tf_op jit(solution)/shard_map/attend_back/pallas_call | solution.py:502
  204.3 4.2 %sort_back.1 = (f32[128,512]{1,0:T(8,128)}, f32[512,128]{1,0:T(8,128)}) custom-call(s32[1,4]{1,0:T(1,128)} %lens.9, f32[128,512]{1,0:T(8,128)} %get-tuple-element.168.u_ref, bf16[512,1792]{1,0:T(8,128)(2,1)} %bitcast.114, s32[1,128]{1,0:T(1,128)} %partner_ref.3, f32[16,128,128]{2,1,0:T(8,128)} %get-tuple-element.169.steps_ref, ...), custom_call_target="tpu_custom_call" | custom-call | flops 100000000 | bytes 10000000 | tf_op jit(solution)/shard_map/sort_back/pallas_call | solution.py:250
  208.5 2.2 collective-permute-done.10
  213.4 23.4 %project_back.1 = (f32[4096,512]{1,0:T(8,128)}, bf16[16,16,1792]{2,1,0:T(8,128)(2,1)}, f32[16,16,1792]{2,1,0:T(8,128)}) custom-call(s32[1]{0:T(128)} %bitcast.place, s32[1,4]{1,0:T(1,128)} %lens.9, bf16[4096,512]{1,0:T(8,128)(2,1)} %x_ref.5, f32[4096,512]{1,0:T(8,128)} %get-tuple-element.179.dx_ref, f32[128,512]{1,0:T(8,128)} %get-tuple-element.180.du_ref, ...), custom_call_target="tpu_custom_call" | custom-call | flops 12884901888 | bytes 37748736 | tf_op jit(solution)/shard_map/project_back/pallas_call | solution.py:760
  242.1 6.8 %collective-permute-done.13 = bf16[2,2,2,16,896]{4,3,0,1,2:T(8,128)(2,1)S(1)} collective-permute-done((bf16[2,2,2,16,896]{4,3,0,1,2:T(8,128)(2,1)S(1)}, bf16[2,2,2,16,896]{4,3,0,1,2:T(8,128)(2,1)S(1)}, u32[]{:S(2)}, u32[]{:S(2)}) %collective-permute-start.13) | collective-permute-done | bytes 229408 | tf_op jit(solution)/shard_map/ppermute | solution.py:898
  251.0 2.7 collective-permute-done.15
  255.1 4.3 %collective-permute-done.17 = bf16[2,16,1792]{2,1,0:T(8,128)(2,1)S(1)} collective-permute-done((bf16[2,16,1792]{2,1,0:T(8,128)(2,1)S(1)}, bf16[2,16,1792]{2,1,0:T(8,128)(2,1)S(1)}, u32[]{:S(2)}, u32[]{:S(2)}) %collective-permute-start.17) | collective-permute-done | bytes 114720 | tf_op jit(solution)/shard_map/ppermute | solution.py:898
  261.0 4.6 %collective-permute-done.18.one_came = bf16[16,1792]{1,0:T(8,128)(2,1)S(1)} collective-permute-done((bf16[16,1792]{1,0:T(8,128)(2,1)S(1)}, bf16[16,1792]{1,0:T(8,128)(2,1)S(1)}, u32[]{:S(2)}, u32[]{:S(2)}) %collective-permute-start.18) | collective-permute-done | bytes 57376 | tf_op jit(solution)/shard_map/ppermute | solution.py:898
  266.3 2.7 adamw.1
  (79 shorter events, 36.0 us)
Async XLA Ops:
  7.2 71.0 %all-gather.3.cloned.1.call-start = ((), (), s32[]{:S(2)}) async-start(), calls=%async_computation | async-start | bytes 4866048 | tf_op jit(solution)/shard_map/all_gather | solution.py:986
  9.0 7.1 %collective-permute-start = (bf16[1,1,1,1,1,16,1792]{6,5,4,3,2,1,0:T(8,128)(2,1)}, bf16[1,1,1,1,1,16,1792]{6,5,4,3,2,1,0:T(8,128)(2,1)S(1)}, u32[]{:S(2)}, u32[]{:S(2)}) collective-permute-start(bf16[1,1,1,1,1,16,1792]{6,5,4,3,2,1,0:T(8,128)(2,1)} %bitcast.121), channel_id=1, source_target_pairs={{0,16},{1,17},{2,18},{3,19},{4,20},{5,21},{6,22},{7,23},{8,24},{9,... | collective-permute-start | bytes 172040 | tf_op jit(solution)/shard_map/ppermute | solution.py:898
  17.0 4.9 %collective-permute-start.1 = (bf16[2,1,1,1,1,16,1792]{6,5,4,3,2,1,0:T(8,128)(2,1)S(1)}, bf16[2,1,1,1,1,16,1792]{6,5,4,3,2,1,0:T(8,128)(2,1)S(1)}, u32[]{:S(2)}, u32[]{:S(2)}) collective-permute-start(bf16[2,1,1,1,1,16,1792]{6,5,4,3,2,1,0:T(8,128)(2,1)S(1)} %pad_maximum_fusion.4), channel_id=1, source_target_pairs={{0,8},{1,9},{2,10},{3,11},{4,12},{5,13},{6,14},{7,15},{8,0},{9,1},... | collective-permute-start | bytes 344072 | tf_op jit(solution)/shard_map/ppermute | solution.py:898
  21.9 7.1 %collective-permute-start.2 = (bf16[2,2,1,1,1,16,1792]{6,5,4,3,2,1,0:T(8,128)(2,1)S(1)}, bf16[2,2,1,1,1,16,1792]{6,5,4,3,2,1,0:T(8,128)(2,1)S(1)}, u32[]{:S(2)}, u32[]{:S(2)}) collective-permute-start(bf16[2,2,1,1,1,16,1792]{6,5,4,3,2,1,0:T(8,128)(2,1)S(1)} %pad_maximum_fusion.3), channel_id=1, source_target_pairs={{0,4},{1,5},{2,6},{3,7},{4,0},{5,1},{6,2},{7,3},{8,12},{9,13},{10,... | collective-permute-start | bytes 688136 | tf_op jit(solution)/shard_map/ppermute | solution.py:898
  29.1 8.5 %collective-permute-start.3 = (bf16[2,2,2,1,1,16,1792]{6,5,4,3,2,1,0:T(8,128)(2,1)S(1)}, bf16[2,2,2,1,1,16,1792]{6,5,4,3,2,1,0:T(8,128)(2,1)S(1)}, u32[]{:S(2)}, u32[]{:S(2)}) collective-permute-start(bf16[2,2,2,1,1,16,1792]{6,5,4,3,2,1,0:T(8,128)(2,1)S(1)} %pad_maximum_fusion.2), channel_id=1, source_target_pairs={{0,2},{1,3},{2,0},{3,1},{4,6},{5,7},{6,4},{7,5},{8,10},{9,11},{10,... | collective-permute-start | bytes 1376264 | tf_op jit(solution)/shard_map/ppermute | solution.py:898
  37.8 2.5 collective-permute-start.4
  151.9 13.2 %collective-permute-start.5 = (bf16[16,144,512]{2,1,0:T(8,128)(2,1)}, bf16[16,144,512]{2,1,0:T(8,128)(2,1)S(1)}, u32[]{:S(2)}, u32[]{:S(2)}) collective-permute-start(bf16[16,144,512]{2,1,0:T(8,128)(2,1)} %get-tuple-element.131), channel_id=1, source_target_pairs={{0,1},{1,0},{2,3},{3,2},{4,5},{5,4},{6,7},{7,6},{8,9},{9,8},{10,11... | collective-permute-start | bytes 7077896 | tf_op jit(solution)/shard_map/ppermute | solution.py:898
  165.2 1.4 copy-start.1
  166.6 1.4 copy-start
  166.6 2.1 slice-start.1
  170.4 20.1 %collective-permute-start.6 = (bf16[2,2,2,72,512]{4,3,0,1,2:T(8,128)(2,1)S(1)}, bf16[2,2,2,72,512]{4,3,0,1,2:T(8,128)(2,1)S(1)}, u32[]{:S(2)}, u32[]{:S(2)}) collective-permute-start(bf16[2,2,2,72,512]{4,3,0,1,2:T(8,128)(2,1)S(1)} %get-tuple-element.139), channel_id=1, source_target_pairs={{0,2},{1,3},{2,0},{3,1},{4,6},{5,7},{6,4},{7,5},{8,10},{9,11},{10,... | collective-permute-start | bytes 1769480 | tf_op jit(solution)/shard_map/ppermute | solution.py:898
  172.3 18.3 %collective-permute-start.7 = (bf16[2,2,2,72,512]{4,3,0,1,2:T(8,128)(2,1)S(1)}, bf16[2,2,2,72,512]{4,3,0,1,2:T(8,128)(2,1)S(1)}, u32[]{:S(2)}, u32[]{:S(2)}) collective-permute-start(bf16[2,2,2,72,512]{4,3,0,1,2:T(8,128)(2,1)S(1)} %get-tuple-element.140), channel_id=1, source_target_pairs={{0,4},{1,5},{2,6},{3,7},{4,0},{5,1},{6,2},{7,3},{8,12},{9,13},{10,... | collective-permute-start | bytes 1769480 | tf_op jit(solution)/shard_map/ppermute | solution.py:898
  191.0 11.1 %collective-permute-start.8 = (bf16[2,2,72,512]{3,2,0,1:T(8,128)(2,1)S(1)}, bf16[2,2,72,512]{3,2,0,1:T(8,128)(2,1)S(1)}, u32[]{:S(2)}, u32[]{:S(2)}) collective-permute-start(bf16[2,2,72,512]{3,2,0,1:T(8,128)(2,1)S(1)} %get-tuple-element.153), channel_id=1, source_target_pairs={{0,4},{1,5},{2,6},{3,7},{4,0},{5,1},{6,2},{7,3},{8,12},{9,13},{10,... | collective-permute-start | bytes 884744 | tf_op jit(solution)/shard_map/ppermute | solution.py:898
  192.8 9.3 %collective-permute-start.9 = (bf16[2,2,72,512]{3,2,0,1:T(8,128)(2,1)S(1)}, bf16[2,2,72,512]{3,2,0,1:T(8,128)(2,1)S(1)}, u32[]{:S(2)}, u32[]{:S(2)}) collective-permute-start(bf16[2,2,72,512]{3,2,0,1:T(8,128)(2,1)S(1)} %get-tuple-element.154), channel_id=1, source_target_pairs={{0,2},{1,3},{2,0},{3,1},{4,6},{5,7},{6,4},{7,5},{8,10},{9,11},{10,... | collective-permute-start | bytes 884744 | tf_op jit(solution)/shard_map/ppermute | solution.py:898
  202.4 8.3 %collective-permute-start.10 = (bf16[2,144,512]{2,1,0:T(8,128)(2,1)S(1)}, bf16[2,144,512]{2,1,0:T(8,128)(2,1)S(1)}, u32[]{:S(2)}, u32[]{:S(2)}) collective-permute-start(bf16[2,144,512]{2,1,0:T(8,128)(2,1)S(1)} %get-tuple-element.167), channel_id=1, source_target_pairs={{0,8},{1,9},{2,10},{3,11},{4,12},{5,13},{6,14},{7,15},{8,0},{9,1},... | collective-permute-start | bytes 884744 | tf_op jit(solution)/shard_map/ppermute | solution.py:898
  211.5 25.3 %collective-permute-start.11 = (bf16[144,512]{1,0:T(8,128)(2,1)S(1)}, bf16[144,512]{1,0:T(8,128)(2,1)S(1)}, u32[]{:S(2)}, u32[]{:S(2)}) collective-permute-start(bf16[144,512]{1,0:T(8,128)(2,1)S(1)} %get-tuple-element.178), channel_id=1, source_target_pairs={{0,16},{1,17},{2,18},{3,19},{4,20},{5,21},{6,22},{7,23},{8,24},{9,... | collective-permute-start | bytes 442376 | tf_op jit(solution)/shard_map/ppermute | solution.py:898
  236.8 1.7 copy-start.2
  236.8 2.7 collective-permute-start.12
  239.8 9.7 %collective-permute-start.14 = (bf16[2,2,2,16,896]{4,3,0,1,2:T(8,128)(2,1)S(1)}, bf16[2,2,2,16,896]{4,3,0,1,2:T(8,128)(2,1)S(1)}, u32[]{:S(2)}, u32[]{:S(2)}) collective-permute-start(bf16[2,2,2,16,896]{4,3,0,1,2:T(8,128)(2,1)S(1)} %fusion.21), channel_id=1, source_target_pairs={{0,4},{1,5},{2,6},{3,7},{4,0},{5,1},{6,2},{7,3},{8,12},{9,13},{10,... | collective-permute-start | bytes 688136 | tf_op jit(solution)/shard_map/ppermute | solution.py:898
  241.4 7.4 %collective-permute-start.13 = (bf16[2,2,2,16,896]{4,3,0,1,2:T(8,128)(2,1)S(1)}, bf16[2,2,2,16,896]{4,3,0,1,2:T(8,128)(2,1)S(1)}, u32[]{:S(2)}, u32[]{:S(2)}) collective-permute-start(bf16[2,2,2,16,896]{4,3,0,1,2:T(8,128)(2,1)S(1)} %fusion.20), channel_id=1, source_target_pairs={{0,2},{1,3},{2,0},{3,1},{4,6},{5,7},{6,4},{7,5},{8,10},{9,11},{10,... | collective-permute-start | bytes 688136 | tf_op jit(solution)/shard_map/ppermute | solution.py:898
  248.9 4.9 %collective-permute-start.15 = (bf16[2,2,16,896]{3,2,0,1:T(8,128)(2,1)S(1)}, bf16[2,2,16,896]{3,2,0,1:T(8,128)(2,1)S(1)}, u32[]{:S(2)}, u32[]{:S(2)}) collective-permute-start(bf16[2,2,16,896]{3,2,0,1:T(8,128)(2,1)S(1)} %get-tuple-element.254), channel_id=1, source_target_pairs={{0,4},{1,5},{2,6},{3,7},{4,0},{5,1},{6,2},{7,3},{8,12},{9,13},{10,... | collective-permute-start | bytes 344072 | tf_op jit(solution)/shard_map/ppermute | solution.py:898
  249.6 4.9 %collective-permute-start.16 = (bf16[2,2,16,896]{3,2,0,1:T(8,128)(2,1)S(1)}, bf16[2,2,16,896]{3,2,0,1:T(8,128)(2,1)S(1)}, u32[]{:S(2)}, u32[]{:S(2)}) collective-permute-start(bf16[2,2,16,896]{3,2,0,1:T(8,128)(2,1)S(1)} %get-tuple-element.252), channel_id=1, source_target_pairs={{0,2},{1,3},{2,0},{3,1},{4,6},{5,7},{6,4},{7,5},{8,10},{9,11},{10,... | collective-permute-start | bytes 344072 | tf_op jit(solution)/shard_map/ppermute | solution.py:898
  254.5 4.9 %collective-permute-start.17 = (bf16[2,16,1792]{2,1,0:T(8,128)(2,1)S(1)}, bf16[2,16,1792]{2,1,0:T(8,128)(2,1)S(1)}, u32[]{:S(2)}, u32[]{:S(2)}) collective-permute-start(bf16[2,16,1792]{2,1,0:T(8,128)(2,1)S(1)} %get-tuple-element.250), channel_id=1, source_target_pairs={{0,8},{1,9},{2,10},{3,11},{4,12},{5,13},{6,14},{7,15},{8,0},{9,1},... | collective-permute-start | bytes 344072 | tf_op jit(solution)/shard_map/ppermute | solution.py:898
  260.0 5.7 %collective-permute-start.18 = (bf16[16,1792]{1,0:T(8,128)(2,1)S(1)}, bf16[16,1792]{1,0:T(8,128)(2,1)S(1)}, u32[]{:S(2)}, u32[]{:S(2)}) collective-permute-start(bf16[16,1792]{1,0:T(8,128)(2,1)S(1)} %get-tuple-element.262), channel_id=1, source_target_pairs={{0,16},{1,17},{2,18},{3,19},{4,20},{5,21},{6,22},{7,23},{8,24},{9,... | collective-permute-start | bytes 172040 | tf_op jit(solution)/shard_map/ppermute | solution.py:898
  (2 other events, 1.9 us)
Sparse Core Ops, SparseCore 0:
  11.5 66.6 all-gather.2

commit v4 on v3

--- a/solution.py
+++ b/solution.py
@@ -95,9 +95,24 @@
     return pl.BlockSpec(memory_space=pltpu.SMEM)
 
 
-def project_kernel(lens, x_ref, w_ref, q_ref, k_ref, v_ref, u_ref, norms_ref, *, slot):
+def project_kernel(
+    place, lens, x_ref, near_ref, far_ref, q_ref, k_ref, v_ref, u_ref, norms_ref, w_ref, *, slot
+):
     tile, width = x_ref.shape
     base = pl.program_id(0) * tile
+
+    @pl.when(pl.program_id(0) == 0)
+    def _():
+        rows = near_ref.shape[1]
+        mine = place[0] & 1
+        for half in range(near_ref.shape[0]):
+            at = (place[0] >> 1) ^ half
+            w_ref[2 * half * rows : (2 * half + 1) * rows, :] = jnp.where(
+                mine == 0, near_ref[at], far_ref[at]
+            )
+            w_ref[(2 * half + 1) * rows : (2 * half + 2) * rows, :] = jnp.where(
+                mine == 0, far_ref[at], near_ref[at]
+            )
 
     @pl.when(pl.program_id(0) == 0)
     def _():
@@ -119,21 +134,23 @@
     u_ref[...] = dot(pick, h_one)
 
 
-def project(lens, x, w_one):
+def project(place, lens, x, near, far):
     slot, width = x.shape
+    w_shape = (2 * near.shape[0] * near.shape[1], near.shape[2])
     grid = slot // WIDE
     row = pl.BlockSpec((WIDE, width), lambda i: (i, 0))
     out = jax.ShapeDtypeStruct((slot, width), bf16)
     return pl.pallas_call(
         functools.partial(project_kernel, slot=slot),
         grid=(grid,),
-        in_specs=[smem(), row, whole(w_one.shape)],
+        in_specs=[smem(), smem(), row, whole(near.shape), whole(far.shape)],
         out_specs=[
             row,
             row,
             row,
             pl.BlockSpec((WIDE // BLOCK, width), lambda i: (i, 0)),
             whole((8, width)),
+            whole(w_shape),
         ],
         out_shape=[
             out,
@@ -141,13 +158,14 @@
             out,
             jax.ShapeDtypeStruct((slot // BLOCK, width), f32),
             jax.ShapeDtypeStruct((8, width), f32),
+            jax.ShapeDtypeStruct(w_shape, bf16),
         ],
         compiler_params=params(),
         cost_estimate=pl.CostEstimate(
             flops=2 * slot * width * 3 * width, bytes_accessed=slot * width * 8, transcendentals=0
         ),
         name="project",
-    )(lens, x, w_one)
+    )(place, lens, x, near, far)
 
 
 def sort_parts(lens, u_ref, ws_ref, slot):
@@ -533,8 +551,8 @@
 
 def ffn_kernel(
     place, x_ref, dy_ref, o_ref, norms_ref, w_ref,
-    out_ref, dx_ref, do_ref, sent_ref, kept_ref, g_norm_ref,
-    g_ref, h_scr, ht_scr, dyt_scr, y_scr, dh_scr, hat_scr, gt_scr,
+    out_ref, dx_ref, do_ref, sent_in, sent_out, kept_in, kept_out, g_norm_ref,
+    g_ref, h_scr, ht_scr, dyt_scr, y_scr, dh_scr, hat_scr, gt_scr, *, sorted_bits,
 ):
     tile, width = x_ref.shape
     hidden = gt_scr.shape[1]
@@ -551,11 +569,19 @@
         ref[at] = value + jnp.where(fresh, 0.0, ref[at])
 
     root = math.sqrt(2.0 / math.pi)
-    w_in = [w_ref[:, c * ROWS : (c + 1) * ROWS, :].reshape(width, width) for c in range(slabs)]
-    w_out = [
-        w_ref[c * share : (c + 1) * share, out_rows, :].reshape(width, width) for c in range(slabs)
-    ]
-    w_o = w_ref[:, whole_rows, :].reshape(width, width)
+    few = w_ref.shape[0]
+
+    def blocks_of(first, count, at):
+        if count <= few:
+            part = slice(first % few, first % few + count)
+            return w_ref[part, first // few, at, :].reshape(-1, width)
+        return jnp.concatenate(
+            [w_ref[:, upper, at, :].reshape(-1, width) for upper in range(count // few)], axis=0
+        )
+
+    w_in = [blocks_of(0, parts, slice(c * ROWS, (c + 1) * ROWS)) for c in range(slabs)]
+    w_out = [blocks_of(c * share, share, out_rows) for c in range(slabs)]
+    w_o = blocks_of(0, parts, whole_rows)
 
     def d_hidden(c):
         return dot_nt(dy_ref[...], w_out[c])
@@ -614,32 +640,47 @@
             g_ref[c * share : (c + 1) * share, out_rows, :] = gt_scr[
                 :, c * width : (c + 1) * width
             ].T.reshape(share, slabs * ROWS, width)
-        halves(place, sent_ref, kept_ref, lambda i: g_ref[i])
-
-
-def halves(place, sent_ref, kept_ref, block):
+        first = (slabs + 1) * ROWS
+        halves(
+            place,
+            (sent_in, sent_out, kept_in, kept_out),
+            lambda i, part: g_ref[i, first:] if part else g_ref[i, :first],
+            sorted_bits,
+        )
+
+
+def halves(place, refs, block, sorted_bits):
     mine = place[0] & 1
+    parts = len(refs) // 2
+    high = refs[0].shape[0] // 2
 
     def one(i, carry):
-        sent_ref[i] = block(2 * i + 1 - mine).astype(bf16)
-        kept_ref[i] = block(2 * i + mine)
+        low, next_low, rest = i & 1, (i >> 1) & 1, i >> 2
+        spots = [low * high + next_low * (high // 2) + rest, next_low * high + low * (high // 2) + rest]
+        for part in range(parts):
+            at = spots[part] if sorted_bits else i
+            refs[part][at] = block(2 * i + 1 - mine, part).astype(bf16)
+            refs[parts + part][at] = block(2 * i + mine, part)
         return carry
 
-    lax.fori_loop(0, sent_ref.shape[0], one, 0)
-
-
-def ffn(place, x, dy, o_t, norms, w_two):
+    lax.fori_loop(0, 2 * high, one, 0)
+
+
+def ffn(place, x, dy, o_t, norms, w_two, sorted_bits):
     slot, width = x.shape
-    hidden = (w_two.shape[1] // ROWS - 1) // 2 * width
+    hidden = (w_two.shape[2] // ROWS - 1) // 2 * width
+    blocks = (w_two.shape[0] * w_two.shape[1], *w_two.shape[2:])
     grid = slot // TILE
-    half = (w_two.shape[0] // 2, *w_two.shape[1:])
+    first = hidden // width * ROWS + ROWS
+    half_in = (blocks[0] // 2, first, width)
+    half_out = (blocks[0] // 2, blocks[1] - first, width)
     row = pl.BlockSpec((TILE, width), lambda i: (i, 0))
 
     def once(shape):
         return pl.BlockSpec(shape, lambda i: (0,) * len(shape), pipeline_mode=pl.Buffered(1))
 
     return pl.pallas_call(
-        ffn_kernel,
+        functools.partial(ffn_kernel, sorted_bits=sorted_bits),
         grid=(grid,),
         in_specs=[
             smem(),
@@ -649,17 +690,23 @@
             once(norms.shape),
             once(w_two.shape),
         ],
-        out_specs=[row, row, row, once(half), once(half), once((8, width))],
+        out_specs=[
+            row, row, row,
+            once(half_in), once(half_out), once(half_in), once(half_out),
+            once((8, width)),
+        ],
         out_shape=[
             jax.ShapeDtypeStruct((slot, width), bf16),
             jax.ShapeDtypeStruct((slot, width), f32),
             jax.ShapeDtypeStruct((slot, width), bf16),
-            jax.ShapeDtypeStruct(half, bf16),
-            jax.ShapeDtypeStruct(half, f32),
+            jax.ShapeDtypeStruct(half_in, bf16),
+            jax.ShapeDtypeStruct(half_out, bf16),
+            jax.ShapeDtypeStruct(half_in, f32),
+            jax.ShapeDtypeStruct(half_out, f32),
             jax.ShapeDtypeStruct((8, width), f32),
         ],
         scratch_shapes=[
-            pltpu.VMEM(w_two.shape, f32),
+            pltpu.VMEM(blocks, f32),
             pltpu.VMEM((TILE, width), bf16),
             pltpu.VMEM((width, TILE), bf16),
             pltpu.VMEM((width, TILE), bf16),
@@ -679,9 +726,10 @@
 
 
 def project_back_kernel(
-    place, lens, x_ref, dx_ref, du_ref, norms_ref, w_ref, g_sort_ref, g_two_ref, *refs, slot
+    place, lens, x_ref, dx_ref, du_ref, norms_ref, w_ref, g_sort_ref, g_two_ref, *refs, slot,
+    sorted_bits,
 ):
-    *d_refs, grad_ref, sent_ref, kept_ref, g_ref, g_norm_ref = refs
+    *d_refs, grad_ref, sent_a, sent_b, kept_a, kept_b, g_ref, g_norm_ref = refs
     tile, width = x_ref.shape
     step = pl.program_id(0)
 
@@ -739,26 +787,30 @@
         small = g_norm_ref[...] + g_two_ref[...]
         rest = jnp.zeros((LANES - small.shape[0], width), f32)
         g_ref[:, 3 * width + LANES :] = jnp.concatenate([small, rest], axis=0).T
-        rows = sent_ref.shape[1]
+        cols = sent_a.shape[2]
         halves(
             place,
-            sent_ref,
-            kept_ref,
-            lambda i: g_ref[pl.ds(pl.multiple_of(i * rows, rows), rows), :],
+            (sent_a, sent_b, kept_a, kept_b),
+            lambda i, part: g_ref[
+                pl.ds(pl.multiple_of(i * ROWS, ROWS), ROWS), part * cols : (part + 1) * cols
+            ],
+            sorted_bits,
         )
 
 
-def project_back(place, lens, x, d_x, d_q, d_k, d_v, d_u, norms, w_one, g_sort, g_two):
+def project_back(
+    place, lens, x, d_x, d_q, d_k, d_v, d_u, norms, w_one, g_sort, g_two, sorted_bits
+):
     slot, width = x.shape
     grid = slot // WIDE
     row = pl.BlockSpec((WIDE, width), lambda i: (i, 0))
-    half = (width // ROWS // 2, ROWS, w_one.shape[1])
+    half = (width // ROWS // 2, ROWS, w_one.shape[1] // 2)
 
     def once(shape):
         return pl.BlockSpec(shape, lambda i: (0,) * len(shape), pipeline_mode=pl.Buffered(1))
 
     return pl.pallas_call(
-        functools.partial(project_back_kernel, slot=slot),
+        functools.partial(project_back_kernel, slot=slot, sorted_bits=sorted_bits),
         grid=(grid,),
         in_specs=[
             smem(),
@@ -772,10 +824,12 @@
             once(g_two.shape),
         ]
         + [pl.BlockSpec((WIDE, LANES), lambda i: (i, 0))] * (3 * width // LANES),
-        out_specs=[row, once(half), once(half)],
+        out_specs=[row] + [once(half)] * 4,
         out_shape=[
             jax.ShapeDtypeStruct((slot, width), f32),
             jax.ShapeDtypeStruct(half, bf16),
+            jax.ShapeDtypeStruct(half, bf16),
+            jax.ShapeDtypeStruct(half, f32),
             jax.ShapeDtypeStruct(half, f32),
         ],
         scratch_shapes=[pltpu.VMEM(w_one.shape, f32), pltpu.VMEM((8, width), f32)],
@@ -816,9 +870,10 @@
     )(wqkv, wo, wsort, win, wout, norms.T)
 
 
-def adamw_kernel(one_kept, one_came, two_kept, two_came, *refs):
-    one_ref = one_kept[...] + one_came[...].astype(f32)
-    two_ref = two_kept[...] + two_came[...].astype(f32)
+def adamw_kernel(*refs, ones, twos):
+    one_ref = sum(ref[...].astype(f32) for ref in refs[:ones])
+    two_ref = sum(ref[...].astype(f32) for ref in refs[ones : ones + twos])
+    refs = refs[ones + twos :]
     masters, moments, squares, outs = refs[:6], refs[6:12], refs[12:18], refs[18:]
     rows, width = masters[1].shape
     wide = masters[0].shape[1]
@@ -851,7 +906,7 @@
     args = (*one, *two, *flip(masters), *flip(moments), *flip(squares))
     shapes = [a.shape for a in flip(masters)]
     outs = pl.pallas_call(
-        adamw_kernel,
+        functools.partial(adamw_kernel, ones=len(one), twos=len(two)),
         out_shape=[jax.ShapeDtypeStruct(shape, f32) for shape in shapes for _ in range(3)],
         compiler_params=params(),
         name="adamw",
@@ -859,11 +914,9 @@
     return (*outs[:15], *[o.T for o in outs[15:]])
 
 
-def regroup(gathered, size, rows, slabs):
-    if rows == ROWS:
-        return gathered
+def regroup(gathered, rows, slabs):
+    size, width = gathered.shape[0], gathered.shape[-1]
     times = ROWS // rows
-    width = gathered.shape[-1]
     block = gathered.reshape(size // times, times, 2 * slabs + 1, rows, width)
     inner = block[:, :, : slabs + 1].transpose(0, 2, 1, 3, 4)
     outer = block[:, :, slabs + 1 :]
@@ -873,95 +926,89 @@
             outer.reshape(size // times, slabs * ROWS, width),
         ],
         axis=1,
-    )
-
-
-def device_halves(place, sent, kept, size, rows, slabs):
+    )[:, None]
+
+
+def device_halves(place, sent, kept, size, rows, slabs, axis):
     if rows == ROWS:
         return sent, kept
+    cut = kept[0].shape[axis + 1] * rows // ROWS if slabs else kept[0].shape[axis + 1]
+    sent, kept = jnp.concatenate(sent, axis=axis + 1), jnp.concatenate(kept, axis=axis + 1)
     mine = place[0] & 1
     low = jnp.where(mine == 0, kept, sent.astype(f32))
     high = jnp.where(mine == 0, sent.astype(f32), kept)
     grads = jnp.stack([low, high], axis=1).reshape((-1,) + kept.shape[1:])
     times = ROWS // rows
     width = grads.shape[-1]
-    cut = (slabs + 1) * ROWS
-    inner = grads[:, :cut].reshape(size // times, slabs + 1, times, rows, width)
-    outer = grads[:, cut:].reshape(size // times, times, slabs, rows, width)
+    wide = (slabs + 1) * ROWS
+    inner = grads[:, :wide].reshape(size // times, slabs + 1, times, rows, width)
+    outer = grads[:, wide:].reshape(size // times, times, slabs, rows, width)
     block = jnp.concatenate([inner.transpose(0, 2, 1, 3, 4), outer], axis=2)
     block = block.reshape(size // 2, 2, (2 * slabs + 1) * rows, width)
-    sent = lax.dynamic_index_in_dim(block, 1 - mine, 1, keepdims=False).astype(bf16)
-    return sent, lax.dynamic_index_in_dim(block, mine, 1, keepdims=False)
-
-
-def swap(value, bit, size):
-    return lax.ppermute(value, "dp", [(i, i ^ (1 << bit)) for i in range(size)])
+    count = size.bit_length() - 1
+    results = []
+    for index, kind in ((1 - mine, bf16), (mine, f32)):
+        half = lax.dynamic_index_in_dim(block, index, 1, keepdims=False).astype(kind)
+        for part, lead in zip(jnp.split(half, [cut], axis=axis + 1), ((1, 2), (2, 1))):
+            bits = part.reshape((2,) * (count - 1) + part.shape[1:])
+            order = [count - 1 - bit for bit in lead] + list(range(count - 3))
+            order += list(range(count - 1, bits.ndim))
+            results.append(bits.transpose(order).reshape(part.shape))
+    return results[:2], results[2:]
+
+
+def swap(value, mask, size):
+    return lax.ppermute(value, "dp", [(i, i ^ mask) for i in range(size)])
+
+
+def masks_of(bits):
+    return [sum(((turn >> at) & 1) << bit for at, bit in enumerate(bits)) for turn in range(2 ** len(bits))]
+
+
+def fours(count):
+    return [tuple(range(bit, min(bit + 2, count))) for bit in range(3, count, 2)]
 
 
 def gather(block, size):
-    count = size.bit_length() - 1
-    place = lax.axis_index("dp")
-    held = block.reshape((1,) * count + block.shape)
-    for bit in reversed(range(count)):
-        axis = count - 1 - bit
-        came = swap(held, bit, size)
-        upper = ((place >> bit) & 1) == 1
-        held = jnp.concatenate(
-            [jnp.where(upper, came, held), jnp.where(upper, held, came)], axis=axis
-        )
-    return held.reshape((size * block.shape[0],) + block.shape[1:])
-
-
-def pick(value, bit, index, lead):
-    return lax.dynamic_index_in_dim(value, index, lead.index(bit), keepdims=False)
+    held = block[None]
+    for bits in fours(size.bit_length() - 1)[::-1] + [(2,), (1,)]:
+        came = [swap(held, mask, size) for mask in masks_of(bits)[1:]]
+        held = jnp.stack([held, *came], axis=1).reshape((-1,) + block.shape)
+    return held, swap(held, 1, size)
 
 
 class ScatterSum:
     def __init__(self, sent, kept, size, axis):
-        self.size, self.count = size, size.bit_length() - 1
-        self.axis = axis
-        self.bits = list(range(self.count - 1, 0, -1))
+        self.size, self.axis = size, axis
         self.place = lax.axis_index("dp")
-        self.rest = kept.shape[1:]
-        lead = (2,) * (self.count - 1)
-        self.kept = [(kept.reshape(lead + self.rest), self.bits)]
-        self.came = [swap(sent, 0, size).reshape(lead + self.rest)]
-        self.plan = [(1, 2), (2, 1)] + [(bit,) for bit in range(3, self.count)]
+        self.plan = [(1, 2), (2, 1)] + fours(size.bit_length() - 1)[::-1]
+        self.kept, self.sent, self.masks = list(kept), list(sent), [1, 1]
+
+    def send(self):
+        self.came = [swap(sent, mask, self.size) for sent, mask in zip(self.sent, self.masks)]
+
+    def cut(self, ways, index, values):
+        parts = [value.reshape((ways, -1) + value.shape[1:]) for value in values]
+        parts = [lax.dynamic_index_in_dim(part, index, 0, keepdims=False) for part in parts]
+        return sum(part.astype(f32) for part in parts)
 
     def step(self):
         bits = self.plan.pop(0)
-        parts = []
-        if len(bits) > len(self.kept):
-            kept, lead = self.kept[0]
-            middle = len(lead) + self.axis
-            cut = kept.shape[middle] // 2
-            for turn in range(2):
-                at = (slice(None),) * middle + (slice(turn * cut, (turn + 1) * cut),)
-                parts.append((kept[at], self.came[0][at], lead))
-        elif len(bits) < len(self.kept):
-            lead = self.kept[0][1]
-            middle = len(lead) + self.axis
-            parts = [
-                (
-                    jnp.concatenate([kept for kept, _ in self.kept], axis=middle),
-                    jnp.concatenate(self.came, axis=middle),
-                    lead,
-                )
-            ]
-        else:
-            parts = [(kept, came, lead) for (kept, lead), came in zip(self.kept, self.came)]
-        self.kept, self.came, self.sent = [], [], []
-        for bit, (kept, came, lead) in zip(bits, parts):
-            mine = (self.place >> bit) & 1
-            self.sent.append(
-                (pick(kept, bit, 1 - mine, lead) + pick(came, bit, 1 - mine, lead).astype(f32)).astype(bf16)
-            )
-            left = [b for b in lead if b != bit]
-            self.kept.append((pick(kept, bit, mine, lead) + pick(came, bit, mine, lead).astype(f32), left))
-        self.bits = bits
-
-    def send(self):
-        self.came = [swap(sent, bit, self.size) for sent, bit in zip(self.sent, self.bits)]
+        if bits[0] < 3:
+            kept, came = self.kept, self.came
+            mine = [(self.place >> bit) & 1 for bit in bits]
+            self.kept = [self.cut(2, m, pair) for m, pair in zip(mine, zip(kept, came))]
+            self.sent = [self.cut(2, 1 - m, pair).astype(bf16) for m, pair in zip(mine, zip(kept, came))]
+            self.masks = [1 << bit for bit in bits]
+            return
+        values = [*self.kept, *self.came]
+        if len(self.kept) == 2:
+            values = [jnp.concatenate(pair, axis=self.axis + 1) for pair in (self.kept, self.came)]
+        ways = 2 ** len(bits)
+        mine = (self.place >> bits[0]) & (ways - 1)
+        self.kept = [self.cut(ways, mine, values)]
+        self.sent = [self.cut(ways, mine ^ turn, values).astype(bf16) for turn in range(1, ways)]
+        self.masks = masks_of(bits)[1:]
 
     def after(self, values):
         self.came, values = lax.optimization_barrier((self.came, values))
@@ -972,7 +1019,7 @@
         return values
 
     def last(self):
-        return self.kept[0][0].reshape(self.rest), self.came[0].reshape(self.rest)
+        return [value.reshape(value.shape[1:]) for value in (*self.kept, *self.came)]
 
 
 def body(size, x, dy, lens, partner, *state):
@@ -982,45 +1029,47 @@
     slabs = masters[3].shape[1] // width
     place = lax.axis_index("dp").astype(jnp.int32).reshape((1,))
     pack_one, pack_two = pack(masters)
-    w_one = gather(pack_one, size)
-    w_two = regroup(lax.all_gather(pack_two, "dp", axis=0), size, rows, slabs)
-
-    q, k, v, u, norms = project(lens, x, w_one)
+    near, far = gather(pack_one, size)
+    if rows == ROWS:
+        w_two = lax.all_gather(pack_two, "dp", axis=0)[:, None]
+    else:
+        w_two = regroup(lax.all_gather(pack_two, "dp", axis=0), rows, slabs)
+
+    q, k, v, u, norms, w_one = project(place, lens, x, near, far)
     bias, steps = sort_net(lens, u, w_one, partner, slot)
     o_t, probs = attend(lens, partner, bias, q, k, v)
-    out, d_x, d_o, sent, kept, g_two = ffn(place, x, dy, o_t, norms, w_two)
-    sent, kept = device_halves(place, sent, kept, size, rows, slabs)
+    direct = rows == ROWS
+    out, d_x, d_o, *parts, g_two = ffn(place, x, dy, o_t, norms, w_two, direct)
+    sent, kept = device_halves(place, parts[:2], parts[2:], size, rows, slabs, 0)
     two = ScatterSum(sent, kept, size, 0)
+    two.send()
 
     def back(pair):
         return attend_back(pair, partner, q, d_o, probs, k, v)
 
+    def next_stage(values):
+        two.step()
+        values = two.before(values)
+        two.send()
+        return values
+
     back_0 = two.after(back(0))
-    two.step()
-    q, d_o = two.before((q, d_o))
-    two.send()
-    back_1 = back(1)
-    back_2 = back(2)
-    back_1, back_2 = two.after((back_1, back_2))
-    two.step()
-    q, d_o = two.before((q, d_o))
-    two.send()
+    q, d_o = next_stage((q, d_o))
+    back_1, back_2 = two.after((back(1), back(2)))
+    q, d_o = next_stage((q, d_o))
     back_3 = two.after(back(3))
-    two.step()
-    u, back_3 = two.before((u, back_3))
-    two.send()
+    u, back_3 = next_stage((u, back_3))
     d_q, d_k, d_v, d_bias = zip(back_0, back_1, back_2, back_3)
-    d_u, g_sort = two.after(sort_back(lens, u, w_one, partner, d_bias, steps, slot))
+    d_u, g_sort = sort_back(lens, u, w_one, partner, d_bias, steps, slot)
     while two.plan:
-        two.step()
-        d_u = two.before(d_u)
-        two.send()
-    grad_in, sent, kept = project_back(
-        place, lens, x, d_x, d_q, d_k, d_v, d_u, norms, w_one, g_sort, g_two
+        d_u = next_stage(two.after(d_u))
+    grad_in, *parts = project_back(
+        place, lens, x, d_x, d_q, d_k, d_v, d_u, norms, w_one, g_sort, g_two, direct
     )
-    grad_in, sent, kept = two.after((grad_in, sent, kept))
-    sent, kept = device_halves(place, sent, kept, size, rows, 0)
+    grad_in, parts = two.after((grad_in, parts))
+    sent, kept = device_halves(place, parts[:2], parts[2:], size, rows, 0, 1)
     one = ScatterSum(sent, kept, size, 1)
+    one.send()
     while one.plan:
         one.step()
         one.send()

time: 277 us -> 266 us (0.960)
  waiting for transfers between devices: 47.3 us -> 38.7 us
  local copies, waits for them, and re-layouts: 10.9 us -> 3.15 us
  starting transfers between devices: 23.2 us -> 28.1 us
    slice x7 -> x0, local copies, waits for them, and re-layouts: 6.48 us -> none  [step(): parts.append((kept[at], self.came[0][at], lead))]
    ppermute x19 -> x24, waiting for transfers between devices: 43.3 us -> 36.8 us  [swap(): return lax.ppermute(value, 'dp', [(i, i ^ mask) for i in range(size)])]
    ppermute x19 -> x24, starting transfers between devices: 23.2 us -> 28.1 us  [swap(): return lax.ppermute(value, 'dp', [(i, i ^ mask) for i in range(size)])]
  transfers between devices with their start and end apart: 20 -> 25, of which waited for: 13 -> 12; matrix products, arithmetic and copies ran while one was open for 3% -> 1% of each run, Pallas kernels for 35% -> 37%
where the time goes in v4:
time: 266 us; the launch traced here: 265 us
  Pallas kernels  176 us (66%)
  waiting for transfers between devices  38.7 us (15%)
  starting transfers between devices  28.1 us (11%)
  between operations  14.4 us (5%)
  other arithmetic  5.17 us (2%)
  local copies, waits for them, and re-layouts  3.15 us (1%)
    pallas_call x1, Pallas kernels, ffn(): pl.pallas_call(functools.partial(ffn_kernel, sorted_bits=sorted_bits), gr...  73.8 us
    ppermute x24, waiting for transfers between devices, swap(): return lax.ppermute(value, 'dp', [(i, i ^ mask) for i in range(size)])  36.8 us
    pallas_call x4, Pallas kernels, attend_back(): pl.pallas_call(attend_back_kernel, grid=(grid,), in_specs=[smem(), row, r...  36.4 us
    ppermute x24, starting transfers between devices, swap(): return lax.ppermute(value, 'dp', [(i, i ^ mask) for i in range(size)])  28.1 us
    pallas_call x1, Pallas kernels, project_back(): pl.pallas_call(functools.partial(project_back_kernel, slot=slot, sorted_b...  23.5 us
    pallas_call x1, Pallas kernels, attend(): pl.pallas_call(functools.partial(attend_kernel, slot=slot), grid=(grid,),...  15.5 us
    pallas_call x1, Pallas kernels, project(): pl.pallas_call(functools.partial(project_kernel, slot=slot), grid=(grid,)...  12.8 us
  transfers between devices with their start and end apart: 25, of which 12 were waited for; matrix products, arithmetic and copies ran while one was open for 1% of the time, Pallas kernels for 37%

profile of v4, /device:TPU:0, one launch (start us, length us, event | category | flops | bytes accessed | tf_op | source)
XLA Modules:
  0.0 265.1 jit_solution(4766104614771910084)
XLA Ops:
  9.0 3.1 %collective-permute-start = (bf16[1,16,1792]{2,1,0:T(8,128)(2,1)}, bf16[1,16,1792]{2,1,0:T(8,128)(2,1)S(1)}, u32[]{:S(2)}, u32[]{:S(2)}) collective-permute-start(bf16[1,16,1792]{2,1,0:T(8,128)(2,1)} %bitcast.100), channel_id=1, source_target_pairs={{0,8},{1,9},{2,10},{3,11},{4,12},{5,13},{6,14},{7,15},{8,0},{9,1},... | collective-permute-start | bytes 172040 | tf_op jit(solution)/shard_map/ppermute | solution.py:961
  12.1 2.6 collective-permute-start.1
  14.7 3.8 %collective-permute-done.1 = bf16[1,16,1792]{2,1,0:T(8,128)(2,1)S(1)} collective-permute-done((bf16[1,16,1792]{2,1,0:T(8,128)(2,1)}, bf16[1,16,1792]{2,1,0:T(8,128)(2,1)S(1)}, u32[]{:S(2)}, u32[]{:S(2)}) %collective-permute-start.1) | collective-permute-done | bytes 57376 | tf_op jit(solution)/shard_map/ppermute | solution.py:961
  18.5 2.4 collective-permute-done.2
  23.3 5.3 %collective-permute-done.3 = bf16[4,16,1792]{2,1,0:T(8,128)(2,1)S(1)} collective-permute-done((bf16[4,16,1792]{2,1,0:T(8,128)(2,1)S(1)}, bf16[4,16,1792]{2,1,0:T(8,128)(2,1)S(1)}, u32[]{:S(2)}, u32[]{:S(2)}) %collective-permute-start.3) | collective-permute-done | bytes 229408 | tf_op jit(solution)/shard_map/ppermute | solution.py:961
  30.2 8.3 %collective-permute-done.4 = bf16[8,16,1792]{2,1,0:T(8,128)(2,1)S(1)} collective-permute-done((bf16[8,16,1792]{2,1,0:T(8,128)(2,1)S(1)}, bf16[8,16,1792]{2,1,0:T(8,128)(2,1)S(1)}, u32[]{:S(2)}, u32[]{:S(2)}) %collective-permute-start.4) | collective-permute-done | bytes 458784 | tf_op jit(solution)/shard_map/ppermute | solution.py:961
  38.8 2.5 collective-permute-done.5.far_ref
  42.3 12.8 %project.1 = (bf16[4096,512]{1,0:T(8,128)(2,1)}, bf16[4096,512]{1,0:T(8,128)(2,1)}, bf16[4096,512]{1,0:T(8,128)(2,1)}, f32[128,512]{1,0:T(8,128)}, f32[8,512]{1,0:T(8,128)}, /*index=5*/bf16[512,1792]{1,0:T(8,128)(2,1)}) custom-call(s32[1]{0:T(128)} %bitcast.place, s32[1,4]{1,0:T(1,128)} %lens.9, bf16[4096,512]{1,0:T(8,128)(2,1)} %x_ref.5, ...), custom_call_target="tpu_custom_call" | custom-call | flops 6442450944 | bytes 16777216 | tf_op jit(solution)/shard_map/project/pallas_call | solution.py:143
  55.0 4.9 %sort_net.1 = (f32[1,128]{1,0:T(1,128)}, f32[16,128,128]{2,1,0:T(8,128)}) custom-call(s32[1,4]{1,0:T(1,128)} %lens.9, f32[128,512]{1,0:T(8,128)} %get-tuple-element.182.u_ref, bf16[512,1792]{1,0:T(8,128)(2,1)} %get-tuple-element.129.ws_ref.w_ref, s32[1,128]{1,0:T(1,128)} %partner_ref.3), custom_call_target="tpu_custom_call" | custom-call | flops 100000000 | bytes 10000000 | tf_op jit(solution)/shard_map/sort_net/pallas_call | solution.py:228
  59.9 15.5 %attend.1 = (bf16[512,4096]{1,0:T(8,128)(2,1)}, bf16[4,2048,256]{2,1,0:T(8,128)(2,1)}) custom-call(s32[1,4]{1,0:T(1,128)} %lens.9, s32[1,128]{1,0:T(1,128)} %partner_ref.3, f32[1,128]{1,0:T(1,128)} %get-tuple-element.130.bias, bf16[4096,512]{1,0:T(8,128)(2,1)} %get-tuple-element.166.q_ref, bf16[4096,512]{1,0:T(8,128)(2,1)} %get-tuple-element.132.k_ref, ...), custom_call_target="tpu_custom_call" | custom-call | flops 20000000000 | bytes 20971520 | tf_op jit(solution)/shard_map/attend/pallas_call | solution.py:414
  75.3 1.9 all-gather.3.cloned.1.call-done
  77.2 73.8 %ffn.1 = (bf16[4096,512]{1,0:T(8,128)(2,1)}, f32[4096,512]{1,0:T(8,128)}, bf16[4096,512]{1,0:T(8,128)(2,1)}, bf16[16,80,512]{2,1,0:T(8,128)(2,1)}, bf16[16,64,51...) custom-call(s32[1]{0:T(128)} %bitcast.place, bf16[4096,512]{1,0:T(8,128)(2,1)} %x_ref.5, ...), custom_call_target="tpu_custom_call" | custom-call | flops 57982058496 | bytes 29360128 | tf_op jit(solution)/shard_map/ffn/pallas_call | solution.py:682
  151.6 9.1 %attend_back.4 = (bf16[4096,128]{1,0:T(8,128)(2,1)}, bf16[4096,128]{1,0:T(8,128)(2,1)}, bf16[4096,128]{1,0:T(8,128)(2,1)}, f32[1,128]{1,0:T(1,128)}) custom-call(s32[1,128]{1,0:T(1,128)} %partner_ref.3, bf16[4096,512]{1,0:T(8,128)(2,1)} %get-tuple-element.166.q_ref, bf16[4096,512]{1,0:T(8,128)(2,1)} %get-tuple-element.167.do_ref, ...), custom_call_target="tpu_custom_call" | custom-call | flops 10000000000 | bytes 8388608 | tf_op jit(solution)/shard_map/attend_back/pallas_call | solution.py:520
  165.4 9.1 %attend_back.6 = (bf16[4096,128]{1,0:T(8,128)(2,1)}, bf16[4096,128]{1,0:T(8,128)(2,1)}, bf16[4096,128]{1,0:T(8,128)(2,1)}, f32[1,128]{1,0:T(1,128)}) custom-call(s32[1,128]{1,0:T(1,128)} %partner_ref.3, bf16[4096,512]{1,0:T(8,128)(2,1)} %get-tuple-element.166.q_ref, bf16[4096,512]{1,0:T(8,128)(2,1)} %get-tuple-element.167.do_ref, ...), custom_call_target="tpu_custom_call" | custom-call | flops 10000000000 | bytes 8388608 | tf_op jit(solution)/shard_map/attend_back/pallas_call | solution.py:520
  174.5 9.1 %attend_back.5 = (bf16[4096,128]{1,0:T(8,128)(2,1)}, bf16[4096,128]{1,0:T(8,128)(2,1)}, bf16[4096,128]{1,0:T(8,128)(2,1)}, f32[1,128]{1,0:T(1,128)}) custom-call(s32[1,128]{1,0:T(1,128)} %partner_ref.3, bf16[4096,512]{1,0:T(8,128)(2,1)} %get-tuple-element.166.q_ref, bf16[4096,512]{1,0:T(8,128)(2,1)} %get-tuple-element.167.do_ref, ...), custom_call_target="tpu_custom_call" | custom-call | flops 10000000000 | bytes 8388608 | tf_op jit(solution)/shard_map/attend_back/pallas_call | solution.py:520
  185.7 9.1 %attend_back.7 = (bf16[4096,128]{1,0:T(8,128)(2,1)}, bf16[4096,128]{1,0:T(8,128)(2,1)}, bf16[4096,128]{1,0:T(8,128)(2,1)}, f32[1,128]{1,0:T(1,128)}) custom-call(s32[1,128]{1,0:T(1,128)} %partner_ref.3, bf16[4096,512]{1,0:T(8,128)(2,1)} %get-tuple-element.166.q_ref, bf16[4096,512]{1,0:T(8,128)(2,1)} %get-tuple-element.167.do_ref, ...), custom_call_target="tpu_custom_call" | custom-call | flops 10000000000 | bytes 8388608 | tf_op jit(solution)/shard_map/attend_back/pallas_call | solution.py:520
  195.7 1.8 collective-permute-start.12
  200.1 4.2 %sort_back.1 = (f32[128,512]{1,0:T(8,128)}, f32[512,128]{1,0:T(8,128)}) custom-call(s32[1,4]{1,0:T(1,128)} %lens.9, f32[128,512]{1,0:T(8,128)} %get-tuple-element.182.u_ref, bf16[512,1792]{1,0:T(8,128)(2,1)} %get-tuple-element.129.ws_ref.w_ref, s32[1,128]{1,0:T(1,128)} %partner_ref.3, f32[16,128,128]{2,1,0:T(8,128)} %get-tuple-element.183.steps_ref, ...), custom_call_target="tpu_custom_call" | custom-call | flops 100000000 | bytes 10000000 | tf_op jit(solution)/shard_map/sort_back/pallas_call | solution.py:268
  204.3 23.5 %project_back.1 = (f32[4096,512]{1,0:T(8,128)}, bf16[16,16,896]{2,1,0:T(8,128)(2,1)}, bf16[16,16,896]{2,1,0:T(8,128)(2,1)}, f32[16,16,896]{2,1,0:T(8,128)}, f32[16,16,896]{2,1,0:T(8,128)}) custom-call(s32[1]{0:T(128)} %bitcast.place, s32[1,4]{1,0:T(1,128)} %lens.9, bf16[4096,512]{1,0:T(8,128)(2,1)} %x_ref.5, f32[4096,512]{1,0:T(8,128)} %get-tuple-element.181.dx_ref, ...), custom_call_target="tpu_custom_call" | custom-call | flops 12884901888 | bytes 37748736 | tf_op jit(solution)/shard_map/project_back/pallas_call | solution.py:812
  233.9 5.0 %collective-permute-done.16 = bf16[8,16,896]{2,1,0:T(8,128)(2,1)S(1)} collective-permute-done((bf16[8,16,896]{2,1,0:T(8,128)(2,1)S(1)}, bf16[8,16,896]{2,1,0:T(8,128)(2,1)S(1)}, u32[]{:S(2)}, u32[]{:S(2)}) %collective-permute-start.16) | collective-permute-done | bytes 229408 | tf_op jit(solution)/shard_map/ppermute | solution.py:961
  241.6 2.2 collective-permute-done.19
  250.5 2.3 collective-permute-done.22
  252.8 2.0 collective-permute-done.23
  255.4 2.9 %adamw.1 = (f32[16,1536]{1,0:T(8,128)}, f32[16,1536]{1,0:T(8,128)}, f32[16,1536]{1,0:T(8,128)}, f32[16,512]{1,0:T(8,128)}, f32[16,512]{1,0:T(8,128)}, /*index=5*...) custom-call(f32[16,1792]{1,0:T(8,128)} %get-tuple-element.251.refs_0, ...), custom_call_target="tpu_custom_call" | custom-call | tf_op jit(solution)/shard_map/adamw/pallas_call | solution.py:908
  (80 shorter events, 33.8 us)
Async XLA Ops:
  7.2 70.0 %all-gather.3.cloned.1.call-start = ((), (), s32[]{:S(2)}) async-start(), calls=%async_computation | async-start | bytes 4866048 | tf_op jit(solution)/shard_map/all_gather | solution.py:1034
  9.0 5.7 %collective-permute-start = (bf16[1,16,1792]{2,1,0:T(8,128)(2,1)}, bf16[1,16,1792]{2,1,0:T(8,128)(2,1)S(1)}, u32[]{:S(2)}, u32[]{:S(2)}) collective-permute-start(bf16[1,16,1792]{2,1,0:T(8,128)(2,1)} %bitcast.100), channel_id=1, source_target_pairs={{0,8},{1,9},{2,10},{3,11},{4,12},{5,13},{6,14},{7,15},{8,0},{9,1},... | collective-permute-start | bytes 172040 | tf_op jit(solution)/shard_map/ppermute | solution.py:961
  12.1 6.4 %collective-permute-start.1 = (bf16[1,16,1792]{2,1,0:T(8,128)(2,1)}, bf16[1,16,1792]{2,1,0:T(8,128)(2,1)S(1)}, u32[]{:S(2)}, u32[]{:S(2)}) collective-permute-start(bf16[1,16,1792]{2,1,0:T(8,128)(2,1)} %bitcast.101), channel_id=1, source_target_pairs={{0,16},{1,17},{2,18},{3,19},{4,20},{5,21},{6,22},{7,23},{8,24},{9,... | collective-permute-start | bytes 172040 | tf_op jit(solution)/shard_map/ppermute | solution.py:961
  14.7 6.2 %collective-permute-start.2 = (bf16[1,16,1792]{2,1,0:T(8,128)(2,1)}, bf16[1,16,1792]{2,1,0:T(8,128)(2,1)S(1)}, u32[]{:S(2)}, u32[]{:S(2)}) collective-permute-start(bf16[1,16,1792]{2,1,0:T(8,128)(2,1)} %bitcast.102), channel_id=1, source_target_pairs={{0,24},{1,25},{2,26},{3,27},{4,28},{5,29},{6,30},{7,31},{8,16},{9,... | collective-permute-start | bytes 172040 | tf_op jit(solution)/shard_map/ppermute | solution.py:961
  21.7 6.9 %collective-permute-start.3 = (bf16[4,16,1792]{2,1,0:T(8,128)(2,1)S(1)}, bf16[4,16,1792]{2,1,0:T(8,128)(2,1)S(1)}, u32[]{:S(2)}, u32[]{:S(2)}) collective-permute-start(bf16[4,16,1792]{2,1,0:T(8,128)(2,1)S(1)} %get-tuple-element.259), channel_id=1, source_target_pairs={{0,4},{1,5},{2,6},{3,7},{4,0},{5,1},{6,2},{7,3},{8,12},{9,13},{10,... | collective-permute-start | bytes 688136 | tf_op jit(solution)/shard_map/ppermute | solution.py:961
  28.7 9.9 %collective-permute-start.4 = (bf16[8,16,1792]{2,1,0:T(8,128)(2,1)S(1)}, bf16[8,16,1792]{2,1,0:T(8,128)(2,1)S(1)}, u32[]{:S(2)}, u32[]{:S(2)}) collective-permute-start(bf16[8,16,1792]{2,1,0:T(8,128)(2,1)S(1)} %bitcast.78), channel_id=1, source_target_pairs={{0,2},{1,3},{2,0},{3,1},{4,6},{5,7},{6,4},{7,5},{8,10},{9,11},{10,... | collective-permute-start | bytes 1376264 | tf_op jit(solution)/shard_map/ppermute | solution.py:961
  38.8 2.5 collective-permute-start.5
  151.0 9.7 %collective-permute-start.6 = (bf16[16,80,512]{2,1,0:T(8,128)(2,1)}, bf16[16,80,512]{2,1,0:T(8,128)(2,1)S(1)}, u32[]{:S(2)}, u32[]{:S(2)}) collective-permute-start(bf16[16,80,512]{2,1,0:T(8,128)(2,1)} %get-tuple-element.139), channel_id=1, source_target_pairs={{0,1},{1,0},{2,3},{3,2},{4,5},{5,4},{6,7},{7,6},{8,9},{9,8},{10,11... | collective-permute-start | bytes 3932168 | tf_op jit(solution)/shard_map/ppermute | solution.py:961
  151.3 9.4 %collective-permute-start.7 = (bf16[16,64,512]{2,1,0:T(8,128)(2,1)}, bf16[16,64,512]{2,1,0:T(8,128)(2,1)S(1)}, u32[]{:S(2)}, u32[]{:S(2)}) collective-permute-start(bf16[16,64,512]{2,1,0:T(8,128)(2,1)} %get-tuple-element.140), channel_id=1, source_target_pairs={{0,1},{1,0},{2,3},{3,2},{4,5},{5,4},{6,7},{7,6},{8,9},{9,8},{10,11... | collective-permute-start | bytes 3145736 | tf_op jit(solution)/shard_map/ppermute | solution.py:961
  162.9 20.7 %collective-permute-start.8 = (bf16[8,80,512]{2,1,0:T(8,128)(2,1)S(1)}, bf16[8,80,512]{2,1,0:T(8,128)(2,1)S(1)}, u32[]{:S(2)}, u32[]{:S(2)}) collective-permute-start(bf16[8,80,512]{2,1,0:T(8,128)(2,1)S(1)} %get-tuple-element.150), channel_id=1, source_target_pairs={{0,2},{1,3},{2,0},{3,1},{4,6},{5,7},{6,4},{7,5},{8,10},{9,11},{10,... | collective-permute-start | bytes 1966088 | tf_op jit(solution)/shard_map/ppermute | solution.py:961
  164.4 19.2 %collective-permute-start.9 = (bf16[8,64,512]{2,1,0:T(8,128)(2,1)S(1)}, bf16[8,64,512]{2,1,0:T(8,128)(2,1)S(1)}, u32[]{:S(2)}, u32[]{:S(2)}) collective-permute-start(bf16[8,64,512]{2,1,0:T(8,128)(2,1)S(1)} %get-tuple-element.151), channel_id=1, source_target_pairs={{0,4},{1,5},{2,6},{3,7},{4,0},{5,1},{6,2},{7,3},{8,12},{9,13},{10,... | collective-permute-start | bytes 1572872 | tf_op jit(solution)/shard_map/ppermute | solution.py:961
  184.0 10.8 %collective-permute-start.10 = (bf16[4,80,512]{2,1,0:T(8,128)(2,1)S(1)}, bf16[4,80,512]{2,1,0:T(8,128)(2,1)S(1)}, u32[]{:S(2)}, u32[]{:S(2)}) collective-permute-start(bf16[4,80,512]{2,1,0:T(8,128)(2,1)S(1)} %get-tuple-element.164), channel_id=1, source_target_pairs={{0,4},{1,5},{2,6},{3,7},{4,0},{5,1},{6,2},{7,3},{8,12},{9,13},{10,... | collective-permute-start | bytes 983048 | tf_op jit(solution)/shard_map/ppermute | solution.py:961
  185.0 9.7 %collective-permute-start.11 = (bf16[4,64,512]{2,1,0:T(8,128)(2,1)S(1)}, bf16[4,64,512]{2,1,0:T(8,128)(2,1)S(1)}, u32[]{:S(2)}, u32[]{:S(2)}) collective-permute-start(bf16[4,64,512]{2,1,0:T(8,128)(2,1)S(1)} %get-tuple-element.165), channel_id=1, source_target_pairs={{0,2},{1,3},{2,0},{3,1},{4,6},{5,7},{6,4},{7,5},{8,10},{9,11},{10,... | collective-permute-start | bytes 786440 | tf_op jit(solution)/shard_map/ppermute | solution.py:961
  195.7 32.1 %collective-permute-start.12 = (bf16[1,144,512]{2,1,0:T(8,128)(2,1)S(1)}, bf16[1,144,512]{2,1,0:T(8,128)(2,1)S(1)}, u32[]{:S(2)}, u32[]{:S(2)}) collective-permute-start(bf16[1,144,512]{2,1,0:T(8,128)(2,1)S(1)} %get-tuple-element.178), channel_id=1, source_target_pairs={{0,8},{1,9},{2,10},{3,11},{4,12},{5,13},{6,14},{7,15},{8,0},{9,1},... | collective-permute-start | bytes 442376 | tf_op jit(solution)/shard_map/ppermute | solution.py:961
  197.6 30.3 %collective-permute-start.13 = (bf16[1,144,512]{2,1,0:T(8,128)(2,1)S(1)}, bf16[1,144,512]{2,1,0:T(8,128)(2,1)S(1)}, u32[]{:S(2)}, u32[]{:S(2)}) collective-permute-start(bf16[1,144,512]{2,1,0:T(8,128)(2,1)S(1)} %get-tuple-element.179), channel_id=1, source_target_pairs={{0,16},{1,17},{2,18},{3,19},{4,20},{5,21},{6,22},{7,23},{8,24},{9,... | collective-permute-start | bytes 442376 | tf_op jit(solution)/shard_map/ppermute | solution.py:961
  198.4 29.5 %collective-permute-start.14 = (bf16[1,144,512]{2,1,0:T(8,128)(2,1)S(1)}, bf16[1,144,512]{2,1,0:T(8,128)(2,1)S(1)}, u32[]{:S(2)}, u32[]{:S(2)}) collective-permute-start(bf16[1,144,512]{2,1,0:T(8,128)(2,1)S(1)} %get-tuple-element.180), channel_id=1, source_target_pairs={{0,24},{1,25},{2,26},{3,27},{4,28},{5,29},{6,30},{7,31},{8,16},{9,... | collective-permute-start | bytes 442376 | tf_op jit(solution)/shard_map/ppermute | solution.py:961
  228.0 4.7 %collective-permute-start.17 = (bf16[16,16,896]{2,1,0:T(8,128)(2,1)}, bf16[16,16,896]{2,1,0:T(8,128)(2,1)S(1)}, u32[]{:S(2)}, u32[]{:S(2)}) collective-permute-start(bf16[16,16,896]{2,1,0:T(8,128)(2,1)} %get-tuple-element.212), channel_id=1, source_target_pairs={{0,1},{1,0},{2,3},{3,2},{4,5},{5,4},{6,7},{7,6},{8,9},{9,8},{10,11... | collective-permute-start | bytes 1376264 | tf_op jit(solution)/shard_map/ppermute | solution.py:961
  231.2 7.7 %collective-permute-start.16 = (bf16[8,16,896]{2,1,0:T(8,128)(2,1)S(1)}, bf16[8,16,896]{2,1,0:T(8,128)(2,1)S(1)}, u32[]{:S(2)}, u32[]{:S(2)}) collective-permute-start(bf16[8,16,896]{2,1,0:T(8,128)(2,1)S(1)} %get-tuple-element.248), channel_id=1, source_target_pairs={{0,2},{1,3},{2,0},{3,1},{4,6},{5,7},{6,4},{7,5},{8,10},{9,11},{10,... | collective-permute-start | bytes 688136 | tf_op jit(solution)/shard_map/ppermute | solution.py:961
  232.8 7.6 %collective-permute-start.18 = (bf16[8,16,896]{2,1,0:T(8,128)(2,1)S(1)}, bf16[8,16,896]{2,1,0:T(8,128)(2,1)S(1)}, u32[]{:S(2)}, u32[]{:S(2)}) collective-permute-start(bf16[8,16,896]{2,1,0:T(8,128)(2,1)S(1)} %get-tuple-element.246), channel_id=1, source_target_pairs={{0,4},{1,5},{2,6},{3,7},{4,0},{5,1},{6,2},{7,3},{8,12},{9,13},{10,... | collective-permute-start | bytes 688136 | tf_op jit(solution)/shard_map/ppermute | solution.py:961
  239.0 4.9 %collective-permute-start.19 = (bf16[4,16,896]{2,1,0:T(8,128)(2,1)S(1)}, bf16[4,16,896]{2,1,0:T(8,128)(2,1)S(1)}, u32[]{:S(2)}, u32[]{:S(2)}) collective-permute-start(bf16[4,16,896]{2,1,0:T(8,128)(2,1)S(1)} %get-tuple-element.256), channel_id=1, source_target_pairs={{0,4},{1,5},{2,6},{3,7},{4,0},{5,1},{6,2},{7,3},{8,12},{9,13},{10,... | collective-permute-start | bytes 344072 | tf_op jit(solution)/shard_map/ppermute | solution.py:961
  240.5 4.9 %collective-permute-start.20 = (bf16[4,16,896]{2,1,0:T(8,128)(2,1)S(1)}, bf16[4,16,896]{2,1,0:T(8,128)(2,1)S(1)}, u32[]{:S(2)}, u32[]{:S(2)}) collective-permute-start(bf16[4,16,896]{2,1,0:T(8,128)(2,1)S(1)} %get-tuple-element.254), channel_id=1, source_target_pairs={{0,2},{1,3},{2,0},{3,1},{4,6},{5,7},{6,4},{7,5},{8,10},{9,11},{10,... | collective-permute-start | bytes 344072 | tf_op jit(solution)/shard_map/ppermute | solution.py:961
  246.1 4.4 %collective-permute-start.21 = (bf16[1,16,1792]{2,1,0:T(8,128)(2,1)S(1)}, bf16[1,16,1792]{2,1,0:T(8,128)(2,1)S(1)}, u32[]{:S(2)}, u32[]{:S(2)}) collective-permute-start(bf16[1,16,1792]{2,1,0:T(8,128)(2,1)S(1)} %get-tuple-element.252), channel_id=1, source_target_pairs={{0,8},{1,9},{2,10},{3,11},{4,12},{5,13},{6,14},{7,15},{8,0},{9,1},... | collective-permute-start | bytes 172040 | tf_op jit(solution)/shard_map/ppermute | solution.py:961
  247.1 5.7 %collective-permute-start.22 = (bf16[1,16,1792]{2,1,0:T(8,128)(2,1)S(1)}, bf16[1,16,1792]{2,1,0:T(8,128)(2,1)S(1)}, u32[]{:S(2)}, u32[]{:S(2)}) collective-permute-start(bf16[1,16,1792]{2,1,0:T(8,128)(2,1)S(1)} %get-tuple-element.253), channel_id=1, source_target_pairs={{0,16},{1,17},{2,18},{3,19},{4,20},{5,21},{6,22},{7,23},{8,24},{9,... | collective-permute-start | bytes 172040 | tf_op jit(solution)/shard_map/ppermute | solution.py:961
  248.8 6.0 %collective-permute-start.23 = (bf16[1,16,1792]{2,1,0:T(8,128)(2,1)S(1)}, bf16[1,16,1792]{2,1,0:T(8,128)(2,1)S(1)}, u32[]{:S(2)}, u32[]{:S(2)}) collective-permute-start(bf16[1,16,1792]{2,1,0:T(8,128)(2,1)S(1)} %get-tuple-element.250), channel_id=1, source_target_pairs={{0,24},{1,25},{2,26},{3,27},{4,28},{5,29},{6,30},{7,31},{8,16},{9,... | collective-permute-start | bytes 172040 | tf_op jit(solution)/shard_map/ppermute | solution.py:961
  (12 other events, 43.1 us)
Sparse Core Ops, SparseCore 0:
  10.9 66.2 all-gather.2

commit v5 on v4

--- a/solution.py
+++ b/solution.py
@@ -83,12 +83,16 @@
     return rstd * (d_hat - mean_d - hat * mean_dh)
 
 
-def params(limit=56 << 20):
-    return pltpu.CompilerParams(vmem_limit_bytes=limit)
+def params(mebibytes):
+    return pltpu.CompilerParams(vmem_limit_bytes=mebibytes << 20)
 
 
 def whole(shape):
     return pl.BlockSpec(shape, lambda *_: (0,) * len(shape))
+
+
+def in_hbm(*values):
+    return [pltpu.with_memory_space_constraint(value, pltpu.HBM) for value in values]
 
 
 def smem():
@@ -160,12 +164,12 @@
             jax.ShapeDtypeStruct((8, width), f32),
             jax.ShapeDtypeStruct(w_shape, bf16),
         ],
-        compiler_params=params(),
+        compiler_params=params(12),
         cost_estimate=pl.CostEstimate(
             flops=2 * slot * width * 3 * width, bytes_accessed=slot * width * 8, transcendentals=0
         ),
         name="project",
-    )(place, lens, x, near, far)
+    )(place, lens, *in_hbm(x, near, far))
 
 
 def sort_parts(lens, u_ref, ws_ref, slot):
@@ -234,7 +238,7 @@
             jax.ShapeDtypeStruct((2 * SINK, blocks, blocks), f32),
         ],
         grid=(1,),
-        compiler_params=params(),
+        compiler_params=params(8),
         cost_estimate=pl.CostEstimate(flops=10**8, bytes_accessed=10**7, transcendentals=10**6),
         name="sort_net",
     )(lens, u, w_sort, partner)
@@ -281,7 +285,7 @@
             jax.ShapeDtypeStruct((width, 2 * SORT), f32),
         ],
         grid=(1,),
-        compiler_params=params(),
+        compiler_params=params(8),
         cost_estimate=pl.CostEstimate(flops=10**8, bytes_accessed=10**7, transcendentals=10**6),
         name="sort_back",
     )(lens, u, w_sort, partner, steps, *d_bias)
@@ -410,6 +414,7 @@
 def attend(lens, partner, bias, q, k, v):
     slot, width = q.shape
     grid = slot // TILE
+    once = pl.BlockSpec((slot, width), lambda i: (0, 0), pipeline_mode=pl.Buffered(1))
     pairs, per_tile = width // LANES, (TILE // GROUP) * 2 * BLOCK
     return pl.pallas_call(
         functools.partial(attend_kernel, slot=slot),
@@ -419,21 +424,21 @@
             smem(),
             smem(),
             pl.BlockSpec((TILE, width), lambda i: (i, 0)),
-            whole(k.shape),
-            whole(v.shape),
+            once,
+            once,
         ],
         out_specs=[
             pl.BlockSpec((width, TILE), lambda i: (0, i)),
             pl.BlockSpec((pairs, per_tile, 2 * GROUP), lambda i: (0, i, 0)),
         ],
         out_shape=[
-            jax.ShapeDtypeStruct((width, slot), bf16),
-            jax.ShapeDtypeStruct((pairs, grid * per_tile, 2 * GROUP), bf16),
+            pltpu.HBM((width, slot), bf16),
+            pltpu.HBM((pairs, grid * per_tile, 2 * GROUP), bf16),
         ],
         scratch_shapes=[
             pltpu.VMEM((2 * GROUP, 2 * GROUP), bf16),
         ],
-        compiler_params=params(),
+        compiler_params=params(14),
         cost_estimate=pl.CostEstimate(
             flops=20 * 10**9, bytes_accessed=slot * width * 10, transcendentals=slot * 512
         ),
@@ -541,12 +546,12 @@
             pltpu.VMEM((slot, LANES), f32),
             pltpu.VMEM((slot // GROUP, GROUP), f32),
         ],
-        compiler_params=params(),
+        compiler_params=params(12),
         cost_estimate=pl.CostEstimate(
             flops=10 * 10**9, bytes_accessed=slot * LANES * 16, transcendentals=0
         ),
         name="attend_back",
-    )(partner, q, d_o, probs, k, v)
+    )(partner, *in_hbm(q, d_o, probs, k, v))
 
 
 def ffn_kernel(
@@ -621,8 +626,8 @@
     d_h = dh_scr[...]
     hat = hat_scr[...]
     d_x = dy_ref[...].astype(f32) + norm_back(d_h, hat, rstd, norms_ref[2:3, :])
-    dx_ref[...] = d_x
     d_z = d_x.astype(bf16)
+    dx_ref[...] = d_z
     do_ref[...] = dot_nt(d_z, w_o).astype(bf16)
     add_to(g_ref, (slice(None), whole_rows, slice(None)), dot(o_t, d_z).reshape(parts, ROWS, width))
     add_to(g_norm_ref, (slice(2, 3), slice(None)), jnp.sum(d_h * hat, axis=0, keepdims=True))
@@ -696,14 +701,14 @@
             once((8, width)),
         ],
         out_shape=[
-            jax.ShapeDtypeStruct((slot, width), bf16),
-            jax.ShapeDtypeStruct((slot, width), f32),
-            jax.ShapeDtypeStruct((slot, width), bf16),
-            jax.ShapeDtypeStruct(half_in, bf16),
-            jax.ShapeDtypeStruct(half_out, bf16),
-            jax.ShapeDtypeStruct(half_in, f32),
-            jax.ShapeDtypeStruct(half_out, f32),
-            jax.ShapeDtypeStruct((8, width), f32),
+            pltpu.HBM((slot, width), bf16),
+            pltpu.HBM((slot, width), bf16),
+            pltpu.HBM((slot, width), bf16),
+            pltpu.HBM(half_in, bf16),
+            pltpu.HBM(half_out, bf16),
+            pltpu.HBM(half_in, f32),
+            pltpu.HBM(half_out, f32),
+            pltpu.HBM((8, width), f32),
         ],
         scratch_shapes=[
             pltpu.VMEM(blocks, f32),
@@ -715,14 +720,14 @@
             pltpu.VMEM((TILE, width), f32),
             pltpu.VMEM((width, hidden), f32),
         ],
-        compiler_params=params(),
+        compiler_params=params(42),
         cost_estimate=pl.CostEstimate(
             flops=2 * slot * width * (3 * width + 6 * hidden),
             bytes_accessed=slot * width * 14,
             transcendentals=slot * hidden,
         ),
         name="ffn",
-    )(place, x, dy, o_t, norms, w_two)
+    )(place, *in_hbm(x, dy, o_t), norms, *in_hbm(w_two))
 
 
 def project_back_kernel(
@@ -767,7 +772,7 @@
         rows = slice(at * SUB, (at + 1) * SUB)
         g_norm_ref[0:1, :] += jnp.sum(d_hs[at] * hats[at], axis=0, keepdims=True)
         g_norm_ref[1:2, :] += jnp.sum(d_hs[at], axis=0, keepdims=True)
-        grad_ref[rows, :] = dx_ref[rows, :] + norm_back(
+        grad_ref[rows, :] = dx_ref[rows, :].astype(f32) + norm_back(
             d_hs[at], hats[at], rstds[at], norms_ref[0:1, :]
         )
 
@@ -833,12 +838,12 @@
             jax.ShapeDtypeStruct(half, f32),
         ],
         scratch_shapes=[pltpu.VMEM(w_one.shape, f32), pltpu.VMEM((8, width), f32)],
-        compiler_params=params(),
+        compiler_params=params(22),
         cost_estimate=pl.CostEstimate(
             flops=2 * slot * width * 6 * width, bytes_accessed=slot * width * 18, transcendentals=0
         ),
         name="project_back",
-    )(place, lens, x, d_x, d_u, norms, w_one, g_sort, g_two, *d_q, *d_k, *d_v)
+    )(place, lens, *in_hbm(x, d_x), d_u, norms, w_one, g_sort, g_two, *d_q, *d_k, *d_v)
 
 
 def pack_kernel(wqkv, wo, wsort, win, wout, norms_t, one_ref, two_ref):
@@ -865,9 +870,9 @@
             jax.ShapeDtypeStruct((rows, wqkv.shape[1] + 2 * LANES), bf16),
             jax.ShapeDtypeStruct((rows * (win.shape[1] // wo.shape[1] + 1) + wout.shape[0], wo.shape[1]), bf16),
         ],
-        compiler_params=params(),
+        compiler_params=params(8),
         name="pack",
-    )(wqkv, wo, wsort, win, wout, norms.T)
+    )(*in_hbm(wqkv, wo, wsort, win, wout), norms.T)
 
 
 def adamw_kernel(*refs, ones, twos):
@@ -908,7 +913,7 @@
     outs = pl.pallas_call(
         functools.partial(adamw_kernel, ones=len(one), twos=len(two)),
         out_shape=[jax.ShapeDtypeStruct(shape, f32) for shape in shapes for _ in range(3)],
-        compiler_params=params(),
+        compiler_params=params(12),
         name="adamw",
     )(*args)
     return (*outs[:15], *[o.T for o in outs[15:]])

time: 266 us -> 253 us (0.951)
  Pallas kernels: 176 us -> 158 us
  local copies, waits for them, and re-layouts: 3.15 us -> 8.23 us
    pallas_call x4, Pallas kernels: 36.4 us -> 30.3 us  [attend_back(): pl.pallas_call(attend_back_kernel, grid=(grid,), in_specs=[smem(), row, r...]
    unnamed x24 -> x60, local copies, waits for them, and re-layouts: 3.01 us -> 8.09 us
    pallas_call x1, Pallas kernels: 15.5 us -> 12.4 us  [attend(): pl.pallas_call(functools.partial(attend_kernel, slot=slot), grid=(grid,),...]
  transfers between devices with their start and end apart: 25 -> 25, of which waited for: 12 -> 12; matrix products, arithmetic and copies ran while one was open for 1% -> 0% of each run, Pallas kernels for 37% -> 32%
where the time goes in v5:
time: 253 us
  Pallas kernels  158 us (62%)
  waiting for transfers between devices  40.2 us (16%)
  starting transfers between devices  27.4 us (11%)
  between operations  14.6 us (6%)
  local copies, waits for them, and re-layouts  8.23 us (3%)
  other arithmetic  4.64 us (2%)
    pallas_call x1, Pallas kernels, ffn(): pl.pallas_call(functools.partial(ffn_kernel, sorted_bits=sorted_bits), gr...  73.9 us
    ppermute x24, waiting for transfers between devices, swap(): return lax.ppermute(value, 'dp', [(i, i ^ mask) for i in range(size)])  37.4 us
    pallas_call x4, Pallas kernels, attend_back(): pl.pallas_call(attend_back_kernel, grid=(grid,), in_specs=[smem(), row, r...  30.3 us
    ppermute x24, starting transfers between devices, swap(): return lax.ppermute(value, 'dp', [(i, i ^ mask) for i in range(size)])  27.3 us
    pallas_call x1, Pallas kernels, project_back(): pl.pallas_call(functools.partial(project_back_kernel, slot=slot, sorted_b...  21.4 us
    pallas_call x1, Pallas kernels, attend(): pl.pallas_call(functools.partial(attend_kernel, slot=slot), grid=(grid,),...  12.4 us
    pallas_call x1, Pallas kernels, project(): pl.pallas_call(functools.partial(project_kernel, slot=slot), grid=(grid,)...  10.8 us
    unnamed x60, local copies, waits for them, and re-layouts  8.09 us
  transfers between devices with their start and end apart: 25, of which 12 were waited for; matrix products, arithmetic and copies ran while one was open for 0% of the time, Pallas kernels for 32%

profile of v5, /device:TPU:0, one launch (start us, length us, event | category | flops | bytes accessed | tf_op | source)
XLA Modules:
  0.0 252.8 jit_solution(1469887360278855275)
XLA Ops:
  9.7 3.1 %collective-permute-start = (bf16[1,16,1792]{2,1,0:T(8,128)(2,1)S(1)}, bf16[1,16,1792]{2,1,0:T(8,128)(2,1)S(1)}, u32[]{:S(2)}, u32[]{:S(2)}) collective-permute-start(bf16[1,16,1792]{2,1,0:T(8,128)(2,1)S(1)} %bitcast.80), channel_id=1, source_target_pairs={{0,8},{1,9},{2,10},{3,11},{4,12},{5,13},{6,14},{7,15},{8,0},{9,1},... | collective-permute-start | bytes 172040 | tf_op jit(solution)/shard_map/ppermute | solution.py:966
  12.8 2.6 %collective-permute-start.1 = (bf16[1,16,1792]{2,1,0:T(8,128)(2,1)S(1)}, bf16[1,16,1792]{2,1,0:T(8,128)(2,1)S(1)}, u32[]{:S(2)}, u32[]{:S(2)}) collective-permute-start(bf16[1,16,1792]{2,1,0:T(8,128)(2,1)S(1)} %bitcast.81), channel_id=1, source_target_pairs={{0,16},{1,17},{2,18},{3,19},{4,20},{5,21},{6,22},{7,23},{8,24},{9,... | collective-permute-start | bytes 172040 | tf_op jit(solution)/shard_map/ppermute | solution.py:966
  15.3 3.6 %collective-permute-done.1 = bf16[1,16,1792]{2,1,0:T(8,128)(2,1)S(1)} collective-permute-done((bf16[1,16,1792]{2,1,0:T(8,128)(2,1)S(1)}, bf16[1,16,1792]{2,1,0:T(8,128)(2,1)S(1)}, u32[]{:S(2)}, u32[]{:S(2)}) %collective-permute-start.1) | collective-permute-done | bytes 57376 | tf_op jit(solution)/shard_map/ppermute | solution.py:966
  18.9 2.4 collective-permute-done.2
  22.9 5.4 %collective-permute-done.3 = bf16[4,16,1792]{2,1,0:T(8,128)(2,1)S(1)} collective-permute-done((bf16[4,16,1792]{2,1,0:T(8,128)(2,1)S(1)}, bf16[4,16,1792]{2,1,0:T(8,128)(2,1)S(1)}, u32[]{:S(2)}, u32[]{:S(2)}) %collective-permute-start.3) | collective-permute-done | bytes 229408 | tf_op jit(solution)/shard_map/ppermute | solution.py:966
  30.0 8.1 %collective-permute-done.4 = bf16[8,16,1792]{2,1,0:T(8,128)(2,1)S(1)} collective-permute-done((bf16[8,16,1792]{2,1,0:T(8,128)(2,1)S(1)}, bf16[8,16,1792]{2,1,0:T(8,128)(2,1)S(1)}, u32[]{:S(2)}, u32[]{:S(2)}) %collective-permute-start.4) | collective-permute-done | bytes 458784 | tf_op jit(solution)/shard_map/ppermute | solution.py:966
  38.4 2.5 collective-permute-done.5.far_ref
  41.8 10.8 %project.1 = (bf16[4096,512]{1,0:T(8,128)(2,1)S(1)}, bf16[4096,512]{1,0:T(8,128)(2,1)S(1)}, bf16[4096,512]{1,0:T(8,128)(2,1)S(1)}, f32[128,512]{1,0:T(8,128)S(1)...) custom-call(s32[1]{0:T(128)} %bitcast.place, s32[1,4]{1,0:T(1,128)S(1)} %copy-done.20, bf16[4096,512]{1,0:T(8,128)(2,1)} %x_ref.5, ...), custom_call_target="tpu_custom_call" | custom-call | flops 6442450944 | bytes 16777216 | tf_op jit(solution)/shard_map/project/pallas_call | solution.py:147
  52.6 3.4 %sort_net.1 = (f32[1,128]{1,0:T(1,128)S(1)}, f32[16,128,128]{2,1,0:T(8,128)S(1)}) custom-call(s32[1,4]{1,0:T(1,128)S(1)} %copy-done.20, f32[128,512]{1,0:T(8,128)S(1)} %get-tuple-element.182.u_ref, bf16[512,1792]{1,0:T(8,128)(2,1)S(1)} %get-tuple-element.129.ws_ref.w_ref, s32[1,128]{1,0:T(1,128)S(1)} %copy-done.19), custom_call_target="tpu_custom_call" | custom-call | flops 100000000 | bytes 10000000 | tf_op jit(solution)/shard_map/sort_net/pallas_call | solution.py:232
  56.1 12.4 %attend.1 = (bf16[512,4096]{1,0:T(8,128)(2,1)}, bf16[4,2048,256]{2,1,0:T(8,128)(2,1)}) custom-call(s32[1,4]{1,0:T(1,128)S(1)} %copy-done.20, s32[1,128]{1,0:T(1,128)S(1)} %copy-done.19, f32[1,128]{1,0:T(1,128)S(1)} %get-tuple-element.130.bias, bf16[4096,512]{1,0:T(8,128)(2,1)S(1)} %get-tuple-element.166.q_ref, ...), custom_call_target="tpu_custom_call" | custom-call | flops 20000000000 | bytes 20971520 | tf_op jit(solution)/shard_map/attend/pallas_call | solution.py:419
  68.4 2.1 copy-done.21
  72.5 2.0 copy-done.23
  74.5 2.7 %all-gather.3.cloned.1.call-done = bf16[4608,512]{1,0:T(8,128)(2,1)} async-done(((bf16[144,512]{1,0:T(8,128)(2,1)}), bf16[4608,512]{1,0:T(8,128)(2,1)}) %all-gather.3.cloned.1.call-update) | async-done | bytes 4718608 | tf_op jit(solution)/shard_map/all_gather | solution.py:1039
  77.2 73.9 %ffn.1 = (bf16[4096,512]{1,0:T(8,128)(2,1)}, bf16[4096,512]{1,0:T(8,128)(2,1)}, bf16[4096,512]{1,0:T(8,128)(2,1)}, bf16[16,80,512]{2,1,0:T(8,128)(2,1)}, bf16[16...) custom-call(s32[1]{0:T(128)} %bitcast.place, ...), custom_call_target="tpu_custom_call" | custom-call | flops 57982058496 | bytes 29360128 | tf_op jit(solution)/shard_map/ffn/pallas_call | solution.py:687
  151.7 7.7 %attend_back.4 = (bf16[4096,128]{1,0:T(8,128)(2,1)S(1)}, bf16[4096,128]{1,0:T(8,128)(2,1)S(1)}, bf16[4096,128]{1,0:T(8,128)(2,1)S(1)}, f32[1,128]{1,0:T(1,128)S(1)}) custom-call(s32[1,128]{1,0:T(1,128)S(1)} %copy-done.19, bf16[4096,512]{1,0:T(8,128)(2,1)} %copy-done.21, bf16[4096,512]{1,0:T(8,128)(2,1)} %get-tuple-element.167.do_ref, ...), custom_call_target="tpu_custom_call" | custom-call | flops 10000000000 | bytes 8388608 | tf_op jit(solution)/shard_map/attend_back/pallas_call | solution.py:525
  165.2 7.5 %attend_back.6 = (bf16[4096,128]{1,0:T(8,128)(2,1)S(1)}, bf16[4096,128]{1,0:T(8,128)(2,1)S(1)}, bf16[4096,128]{1,0:T(8,128)(2,1)S(1)}, f32[1,128]{1,0:T(1,128)S(1)}) custom-call(s32[1,128]{1,0:T(1,128)S(1)} %copy-done.19, bf16[4096,512]{1,0:T(8,128)(2,1)} %copy-done.21, bf16[4096,512]{1,0:T(8,128)(2,1)} %get-tuple-element.167.do_ref, ...), custom_call_target="tpu_custom_call" | custom-call | flops 10000000000 | bytes 8388608 | tf_op jit(solution)/shard_map/attend_back/pallas_call | solution.py:525
  172.8 7.6 %attend_back.5 = (bf16[4096,128]{1,0:T(8,128)(2,1)S(1)}, bf16[4096,128]{1,0:T(8,128)(2,1)S(1)}, bf16[4096,128]{1,0:T(8,128)(2,1)S(1)}, f32[1,128]{1,0:T(1,128)S(1)}) custom-call(s32[1,128]{1,0:T(1,128)S(1)} %copy-done.19, bf16[4096,512]{1,0:T(8,128)(2,1)} %copy-done.21, bf16[4096,512]{1,0:T(8,128)(2,1)} %get-tuple-element.167.do_ref, ...), custom_call_target="tpu_custom_call" | custom-call | flops 10000000000 | bytes 8388608 | tf_op jit(solution)/shard_map/attend_back/pallas_call | solution.py:525
  183.0 7.5 %attend_back.7 = (bf16[4096,128]{1,0:T(8,128)(2,1)S(1)}, bf16[4096,128]{1,0:T(8,128)(2,1)S(1)}, bf16[4096,128]{1,0:T(8,128)(2,1)S(1)}, f32[1,128]{1,0:T(1,128)S(1)}) custom-call(s32[1,128]{1,0:T(1,128)S(1)} %copy-done.19, bf16[4096,512]{1,0:T(8,128)(2,1)} %copy-done.21, bf16[4096,512]{1,0:T(8,128)(2,1)} %get-tuple-element.167.do_ref, ...), custom_call_target="tpu_custom_call" | custom-call | flops 10000000000 | bytes 8388608 | tf_op jit(solution)/shard_map/attend_back/pallas_call | solution.py:525
  195.3 2.5 %sort_back.1 = (f32[128,512]{1,0:T(8,128)S(1)}, f32[512,128]{1,0:T(8,128)S(1)}) custom-call(s32[1,4]{1,0:T(1,128)S(1)} %copy-done.20, f32[128,512]{1,0:T(8,128)S(1)} %get-tuple-element.182.u_ref, bf16[512,1792]{1,0:T(8,128)(2,1)S(1)} %get-tuple-element.129.ws_ref.w_ref, s32[1,128]{1,0:T(1,128)S(1)} %copy-done.19, ...), custom_call_target="tpu_custom_call" | custom-call | flops 100000000 | bytes 10000000 | tf_op jit(solution)/shard_map/sort_back/pallas_call | solution.py:272
  197.8 21.4 %project_back.1 = (f32[4096,512]{1,0:T(8,128)}, bf16[16,16,896]{2,1,0:T(8,128)(2,1)S(1)}, bf16[16,16,896]{2,1,0:T(8,128)(2,1)S(1)}, f32[16,16,896]{2,1,0:T(8,128)S(1)}, f32[16,16,896]{2,1,0:T(8,128)S(1)}) custom-call(s32[1]{0:T(128)} %bitcast.place, s32[1,4]{1,0:T(1,128)S(1)} %copy-done.20, bf16[4096,512]{1,0:T(8,128)(2,1)} %x_ref.5, ...), custom_call_target="tpu_custom_call" | custom-call | flops 12884901888 | bytes 37748736 | tf_op jit(solution)/shard_map/project_back/pallas_call | solution.py:817
  223.4 5.5 %collective-permute-done.16 = bf16[8,16,896]{2,1,0:T(8,128)(2,1)S(1)} collective-permute-done((bf16[8,16,896]{2,1,0:T(8,128)(2,1)S(1)}, bf16[8,16,896]{2,1,0:T(8,128)(2,1)S(1)}, u32[]{:S(2)}, u32[]{:S(2)}) %collective-permute-start.16) | collective-permute-done | bytes 229408 | tf_op jit(solution)/shard_map/ppermute | solution.py:966
  231.4 2.7 %collective-permute-done.19 = bf16[4,16,896]{2,1,0:T(8,128)(2,1)S(1)} collective-permute-done((bf16[4,16,896]{2,1,0:T(8,128)(2,1)S(1)}, bf16[4,16,896]{2,1,0:T(8,128)(2,1)S(1)}, u32[]{:S(2)}, u32[]{:S(2)}) %collective-permute-start.19) | collective-permute-done | bytes 114720 | tf_op jit(solution)/shard_map/ppermute | solution.py:966
  240.2 2.3 collective-permute-done.22
  242.5 2.0 collective-permute-done.23
  (116 shorter events, 36.5 us)
Async XLA Ops:
  7.2 70.0 %all-gather.3.cloned.1.call-start = ((), (), s32[]{:S(2)}) async-start(), calls=%async_computation | async-start | bytes 4866048 | tf_op jit(solution)/shard_map/all_gather | solution.py:1039
  9.7 5.7 %collective-permute-start = (bf16[1,16,1792]{2,1,0:T(8,128)(2,1)S(1)}, bf16[1,16,1792]{2,1,0:T(8,128)(2,1)S(1)}, u32[]{:S(2)}, u32[]{:S(2)}) collective-permute-start(bf16[1,16,1792]{2,1,0:T(8,128)(2,1)S(1)} %bitcast.80), channel_id=1, source_target_pairs={{0,8},{1,9},{2,10},{3,11},{4,12},{5,13},{6,14},{7,15},{8,0},{9,1},... | collective-permute-start | bytes 172040 | tf_op jit(solution)/shard_map/ppermute | solution.py:966
  12.8 6.2 %collective-permute-start.1 = (bf16[1,16,1792]{2,1,0:T(8,128)(2,1)S(1)}, bf16[1,16,1792]{2,1,0:T(8,128)(2,1)S(1)}, u32[]{:S(2)}, u32[]{:S(2)}) collective-permute-start(bf16[1,16,1792]{2,1,0:T(8,128)(2,1)S(1)} %bitcast.81), channel_id=1, source_target_pairs={{0,16},{1,17},{2,18},{3,19},{4,20},{5,21},{6,22},{7,23},{8,24},{9,... | collective-permute-start | bytes 172040 | tf_op jit(solution)/shard_map/ppermute | solution.py:966
  15.3 6.0 %collective-permute-start.2 = (bf16[1,16,1792]{2,1,0:T(8,128)(2,1)S(1)}, bf16[1,16,1792]{2,1,0:T(8,128)(2,1)S(1)}, u32[]{:S(2)}, u32[]{:S(2)}) collective-permute-start(bf16[1,16,1792]{2,1,0:T(8,128)(2,1)S(1)} %bitcast.82), channel_id=1, source_target_pairs={{0,24},{1,25},{2,26},{3,27},{4,28},{5,29},{6,30},{7,31},{8,16},{9,... | collective-permute-start | bytes 172040 | tf_op jit(solution)/shard_map/ppermute | solution.py:966
  21.4 7.0 %collective-permute-start.3 = (bf16[4,16,1792]{2,1,0:T(8,128)(2,1)S(1)}, bf16[4,16,1792]{2,1,0:T(8,128)(2,1)S(1)}, u32[]{:S(2)}, u32[]{:S(2)}) collective-permute-start(bf16[4,16,1792]{2,1,0:T(8,128)(2,1)S(1)} %get-tuple-element.259), channel_id=1, source_target_pairs={{0,4},{1,5},{2,6},{3,7},{4,0},{5,1},{6,2},{7,3},{8,12},{9,13},{10,... | collective-permute-start | bytes 688136 | tf_op jit(solution)/shard_map/ppermute | solution.py:966
  28.5 9.7 %collective-permute-start.4 = (bf16[8,16,1792]{2,1,0:T(8,128)(2,1)S(1)}, bf16[8,16,1792]{2,1,0:T(8,128)(2,1)S(1)}, u32[]{:S(2)}, u32[]{:S(2)}) collective-permute-start(bf16[8,16,1792]{2,1,0:T(8,128)(2,1)S(1)} %bitcast.94), channel_id=1, source_target_pairs={{0,2},{1,3},{2,0},{3,1},{4,6},{5,7},{6,4},{7,5},{8,10},{9,11},{10,... | collective-permute-start | bytes 1376264 | tf_op jit(solution)/shard_map/ppermute | solution.py:966
  38.4 2.5 %collective-permute-start.5 = (bf16[16,16,1792]{2,1,0:T(8,128)(2,1)S(1)}, bf16[16,16,1792]{2,1,0:T(8,128)(2,1)S(1)}, u32[]{:S(2)}, u32[]{:S(2)}) collective-permute-start(bf16[16,16,1792]{2,1,0:T(8,128)(2,1)S(1)} %bitcast.96), channel_id=1, source_target_pairs={{0,1},{1,0},{2,3},{3,2},{4,5},{5,4},{6,7},{7,6},{8,9},{9,8},{10,11... | collective-permute-start | bytes 2752520 | tf_op jit(solution)/shard_map/ppermute | solution.py:966
  151.2 8.3 %collective-permute-start.6 = (bf16[16,80,512]{2,1,0:T(8,128)(2,1)}, bf16[16,80,512]{2,1,0:T(8,128)(2,1)}, u32[]{:S(2)}, u32[]{:S(2)}) collective-permute-start(bf16[16,80,512]{2,1,0:T(8,128)(2,1)} %get-tuple-element.139), channel_id=1, source_target_pairs={{0,1},{1,0},{2,3},{3,2},{4,5},{5,4},{6,7},{7,6},{8,9},{9,8},{10,11... | collective-permute-start | bytes 3932168 | tf_op jit(solution)/shard_map/ppermute | solution.py:966
  151.4 8.0 %collective-permute-start.7 = (bf16[16,64,512]{2,1,0:T(8,128)(2,1)}, bf16[16,64,512]{2,1,0:T(8,128)(2,1)}, u32[]{:S(2)}, u32[]{:S(2)}) collective-permute-start(bf16[16,64,512]{2,1,0:T(8,128)(2,1)} %get-tuple-element.140), channel_id=1, source_target_pairs={{0,1},{1,0},{2,3},{3,2},{4,5},{5,4},{6,7},{7,6},{8,9},{9,8},{10,11... | collective-permute-start | bytes 3145736 | tf_op jit(solution)/shard_map/ppermute | solution.py:966
  163.2 17.1 %collective-permute-start.8 = (bf16[8,80,512]{2,1,0:T(8,128)(2,1)S(1)}, bf16[8,80,512]{2,1,0:T(8,128)(2,1)S(1)}, u32[]{:S(2)}, u32[]{:S(2)}) collective-permute-start(bf16[8,80,512]{2,1,0:T(8,128)(2,1)S(1)} %get-tuple-element.150), channel_id=1, source_target_pairs={{0,2},{1,3},{2,0},{3,1},{4,6},{5,7},{6,4},{7,5},{8,10},{9,11},{10,... | collective-permute-start | bytes 1966088 | tf_op jit(solution)/shard_map/ppermute | solution.py:966
  164.6 15.7 %collective-permute-start.9 = (bf16[8,64,512]{2,1,0:T(8,128)(2,1)S(1)}, bf16[8,64,512]{2,1,0:T(8,128)(2,1)S(1)}, u32[]{:S(2)}, u32[]{:S(2)}) collective-permute-start(bf16[8,64,512]{2,1,0:T(8,128)(2,1)S(1)} %get-tuple-element.151), channel_id=1, source_target_pairs={{0,4},{1,5},{2,6},{3,7},{4,0},{5,1},{6,2},{7,3},{8,12},{9,13},{10,... | collective-permute-start | bytes 1572872 | tf_op jit(solution)/shard_map/ppermute | solution.py:966
  180.8 9.7 %collective-permute-start.10 = (bf16[4,80,512]{2,1,0:T(8,128)(2,1)S(1)}, bf16[4,80,512]{2,1,0:T(8,128)(2,1)S(1)}, u32[]{:S(2)}, u32[]{:S(2)}) collective-permute-start(bf16[4,80,512]{2,1,0:T(8,128)(2,1)S(1)} %get-tuple-element.164), channel_id=1, source_target_pairs={{0,4},{1,5},{2,6},{3,7},{4,0},{5,1},{6,2},{7,3},{8,12},{9,13},{10,... | collective-permute-start | bytes 983048 | tf_op jit(solution)/shard_map/ppermute | solution.py:966
  182.3 8.2 %collective-permute-start.11 = (bf16[4,64,512]{2,1,0:T(8,128)(2,1)S(1)}, bf16[4,64,512]{2,1,0:T(8,128)(2,1)S(1)}, u32[]{:S(2)}, u32[]{:S(2)}) collective-permute-start(bf16[4,64,512]{2,1,0:T(8,128)(2,1)S(1)} %get-tuple-element.165), channel_id=1, source_target_pairs={{0,2},{1,3},{2,0},{3,1},{4,6},{5,7},{6,4},{7,5},{8,10},{9,11},{10,... | collective-permute-start | bytes 786440 | tf_op jit(solution)/shard_map/ppermute | solution.py:966
  190.8 28.4 %collective-permute-start.12 = (bf16[1,144,512]{2,1,0:T(8,128)(2,1)S(1)}, bf16[1,144,512]{2,1,0:T(8,128)(2,1)S(1)}, u32[]{:S(2)}, u32[]{:S(2)}) collective-permute-start(bf16[1,144,512]{2,1,0:T(8,128)(2,1)S(1)} %get-tuple-element.178), channel_id=1, source_target_pairs={{0,8},{1,9},{2,10},{3,11},{4,12},{5,13},{6,14},{7,15},{8,0},{9,1},... | collective-permute-start | bytes 442376 | tf_op jit(solution)/shard_map/ppermute | solution.py:966
  192.7 26.5 %collective-permute-start.13 = (bf16[1,144,512]{2,1,0:T(8,128)(2,1)S(1)}, bf16[1,144,512]{2,1,0:T(8,128)(2,1)S(1)}, u32[]{:S(2)}, u32[]{:S(2)}) collective-permute-start(bf16[1,144,512]{2,1,0:T(8,128)(2,1)S(1)} %get-tuple-element.179), channel_id=1, source_target_pairs={{0,16},{1,17},{2,18},{3,19},{4,20},{5,21},{6,22},{7,23},{8,24},{9,... | collective-permute-start | bytes 442376 | tf_op jit(solution)/shard_map/ppermute | solution.py:966
  193.6 25.6 %collective-permute-start.14 = (bf16[1,144,512]{2,1,0:T(8,128)(2,1)S(1)}, bf16[1,144,512]{2,1,0:T(8,128)(2,1)S(1)}, u32[]{:S(2)}, u32[]{:S(2)}) collective-permute-start(bf16[1,144,512]{2,1,0:T(8,128)(2,1)S(1)} %get-tuple-element.180), channel_id=1, source_target_pairs={{0,24},{1,25},{2,26},{3,27},{4,28},{5,29},{6,30},{7,31},{8,16},{9,... | collective-permute-start | bytes 442376 | tf_op jit(solution)/shard_map/ppermute | solution.py:966
  219.3 3.4 %collective-permute-start.17 = (bf16[16,16,896]{2,1,0:T(8,128)(2,1)S(1)}, bf16[16,16,896]{2,1,0:T(8,128)(2,1)S(1)}, u32[]{:S(2)}, u32[]{:S(2)}) collective-permute-start(bf16[16,16,896]{2,1,0:T(8,128)(2,1)S(1)} %get-tuple-element.212), channel_id=1, source_target_pairs={{0,1},{1,0},{2,3},{3,2},{4,5},{5,4},{6,7},{7,6},{8,9},{9,8},{10,11... | collective-permute-start | bytes 1376264 | tf_op jit(solution)/shard_map/ppermute | solution.py:966
  221.2 7.7 %collective-permute-start.16 = (bf16[8,16,896]{2,1,0:T(8,128)(2,1)S(1)}, bf16[8,16,896]{2,1,0:T(8,128)(2,1)S(1)}, u32[]{:S(2)}, u32[]{:S(2)}) collective-permute-start(bf16[8,16,896]{2,1,0:T(8,128)(2,1)S(1)} %get-tuple-element.248), channel_id=1, source_target_pairs={{0,2},{1,3},{2,0},{3,1},{4,6},{5,7},{6,4},{7,5},{8,10},{9,11},{10,... | collective-permute-start | bytes 688136 | tf_op jit(solution)/shard_map/ppermute | solution.py:966
  222.8 8.0 %collective-permute-start.18 = (bf16[8,16,896]{2,1,0:T(8,128)(2,1)S(1)}, bf16[8,16,896]{2,1,0:T(8,128)(2,1)S(1)}, u32[]{:S(2)}, u32[]{:S(2)}) collective-permute-start(bf16[8,16,896]{2,1,0:T(8,128)(2,1)S(1)} %get-tuple-element.246), channel_id=1, source_target_pairs={{0,4},{1,5},{2,6},{3,7},{4,0},{5,1},{6,2},{7,3},{8,12},{9,13},{10,... | collective-permute-start | bytes 688136 | tf_op jit(solution)/shard_map/ppermute | solution.py:966
  229.2 4.9 %collective-permute-start.19 = (bf16[4,16,896]{2,1,0:T(8,128)(2,1)S(1)}, bf16[4,16,896]{2,1,0:T(8,128)(2,1)S(1)}, u32[]{:S(2)}, u32[]{:S(2)}) collective-permute-start(bf16[4,16,896]{2,1,0:T(8,128)(2,1)S(1)} %get-tuple-element.256), channel_id=1, source_target_pairs={{0,4},{1,5},{2,6},{3,7},{4,0},{5,1},{6,2},{7,3},{8,12},{9,13},{10,... | collective-permute-start | bytes 344072 | tf_op jit(solution)/shard_map/ppermute | solution.py:966
  230.8 4.9 %collective-permute-start.20 = (bf16[4,16,896]{2,1,0:T(8,128)(2,1)S(1)}, bf16[4,16,896]{2,1,0:T(8,128)(2,1)S(1)}, u32[]{:S(2)}, u32[]{:S(2)}) collective-permute-start(bf16[4,16,896]{2,1,0:T(8,128)(2,1)S(1)} %get-tuple-element.254), channel_id=1, source_target_pairs={{0,2},{1,3},{2,0},{3,1},{4,6},{5,7},{6,4},{7,5},{8,10},{9,11},{10,... | collective-permute-start | bytes 344072 | tf_op jit(solution)/shard_map/ppermute | solution.py:966
  235.8 4.5 %collective-permute-start.21 = (bf16[1,16,1792]{2,1,0:T(8,128)(2,1)S(1)}, bf16[1,16,1792]{2,1,0:T(8,128)(2,1)S(1)}, u32[]{:S(2)}, u32[]{:S(2)}) collective-permute-start(bf16[1,16,1792]{2,1,0:T(8,128)(2,1)S(1)} %get-tuple-element.252), channel_id=1, source_target_pairs={{0,8},{1,9},{2,10},{3,11},{4,12},{5,13},{6,14},{7,15},{8,0},{9,1},... | collective-permute-start | bytes 172040 | tf_op jit(solution)/shard_map/ppermute | solution.py:966
  236.8 5.7 %collective-permute-start.22 = (bf16[1,16,1792]{2,1,0:T(8,128)(2,1)S(1)}, bf16[1,16,1792]{2,1,0:T(8,128)(2,1)S(1)}, u32[]{:S(2)}, u32[]{:S(2)}) collective-permute-start(bf16[1,16,1792]{2,1,0:T(8,128)(2,1)S(1)} %get-tuple-element.253), channel_id=1, source_target_pairs={{0,16},{1,17},{2,18},{3,19},{4,20},{5,21},{6,22},{7,23},{8,24},{9,... | collective-permute-start | bytes 172040 | tf_op jit(solution)/shard_map/ppermute | solution.py:966
  238.5 6.0 %collective-permute-start.23 = (bf16[1,16,1792]{2,1,0:T(8,128)(2,1)S(1)}, bf16[1,16,1792]{2,1,0:T(8,128)(2,1)S(1)}, u32[]{:S(2)}, u32[]{:S(2)}) collective-permute-start(bf16[1,16,1792]{2,1,0:T(8,128)(2,1)S(1)} %get-tuple-element.250), channel_id=1, source_target_pairs={{0,24},{1,25},{2,26},{3,27},{4,28},{5,29},{6,30},{7,31},{8,16},{9,... | collective-permute-start | bytes 172040 | tf_op jit(solution)/shard_map/ppermute | solution.py:966
  (30 other events, 317.7 us)
Sparse Core Ops, SparseCore 0:
  10.9 66.2 all-gather.2

commit v6 on v5

--- a/solution.py
+++ b/solution.py
@@ -807,8 +807,8 @@
     place, lens, x, d_x, d_q, d_k, d_v, d_u, norms, w_one, g_sort, g_two, sorted_bits
 ):
     slot, width = x.shape
-    grid = slot // WIDE
-    row = pl.BlockSpec((WIDE, width), lambda i: (i, 0))
+    grid = slot // TILE
+    row = pl.BlockSpec((TILE, width), lambda i: (i, 0))
     half = (width // ROWS // 2, ROWS, w_one.shape[1] // 2)
 
     def once(shape):
@@ -822,13 +822,13 @@
             smem(),
             row,
             row,
-            pl.BlockSpec((WIDE // BLOCK, width), lambda i: (i, 0)),
+            pl.BlockSpec((TILE // BLOCK, width), lambda i: (i, 0)),
             once(norms.shape),
             once(w_one.shape),
             once(g_sort.shape),
             once(g_two.shape),
         ]
-        + [pl.BlockSpec((WIDE, LANES), lambda i: (i, 0))] * (3 * width // LANES),
+        + [pl.BlockSpec((TILE, LANES), lambda i: (i, 0))] * (3 * width // LANES),
         out_specs=[row] + [once(half)] * 4,
         out_shape=[
             jax.ShapeDtypeStruct((slot, width), f32),
@@ -838,7 +838,7 @@
             jax.ShapeDtypeStruct(half, f32),
         ],
         scratch_shapes=[pltpu.VMEM(w_one.shape, f32), pltpu.VMEM((8, width), f32)],
-        compiler_params=params(22),
+        compiler_params=params(18),
         cost_estimate=pl.CostEstimate(
             flops=2 * slot * width * 6 * width, bytes_accessed=slot * width * 18, transcendentals=0
         ),

time: 253 us -> 253 us (level)
  no operation moved by 1% of the time
where the time goes in v6:
time: 253 us; the launch traced here: 252 us
  Pallas kernels  157 us (62%)
  waiting for transfers between devices  40.1 us (16%)
  starting transfers between devices  27.3 us (11%)
  between operations  14.6 us (6%)
  local copies, waits for them, and re-layouts  8.23 us (3%)
  other arithmetic  4.68 us (2%)
    pallas_call x1, Pallas kernels, ffn(): pl.pallas_call(functools.partial(ffn_kernel, sorted_bits=sorted_bits), gr...  73.9 us
    ppermute x24, waiting for transfers between devices, swap(): return lax.ppermute(value, 'dp', [(i, i ^ mask) for i in range(size)])  37.4 us
    pallas_call x4, Pallas kernels, attend_back(): pl.pallas_call(attend_back_kernel, grid=(grid,), in_specs=[smem(), row, r...  30.3 us
    ppermute x24, starting transfers between devices, swap(): return lax.ppermute(value, 'dp', [(i, i ^ mask) for i in range(size)])  27.3 us
    pallas_call x1, Pallas kernels, project_back(): pl.pallas_call(functools.partial(project_back_kernel, slot=slot, sorted_b...  21 us
    pallas_call x1, Pallas kernels, attend(): pl.pallas_call(functools.partial(attend_kernel, slot=slot), grid=(grid,),...  12.4 us
    pallas_call x1, Pallas kernels, project(): pl.pallas_call(functools.partial(project_kernel, slot=slot), grid=(grid,)...  10.8 us
    unnamed x60, local copies, waits for them, and re-layouts  8.09 us
  transfers between devices with their start and end apart: 25, of which 12 were waited for; matrix products, arithmetic and copies ran while one was open for 0% of the time, Pallas kernels for 32%

profile of v6, /device:TPU:0, one launch (start us, length us, event | category | flops | bytes accessed | tf_op | source)
XLA Modules:
  0.0 252.4 jit_solution(2983194161443000026)
XLA Ops:
  9.7 3.1 %collective-permute-start = (bf16[1,16,1792]{2,1,0:T(8,128)(2,1)S(1)}, bf16[1,16,1792]{2,1,0:T(8,128)(2,1)S(1)}, u32[]{:S(2)}, u32[]{:S(2)}) collective-permute-start(bf16[1,16,1792]{2,1,0:T(8,128)(2,1)S(1)} %bitcast.80), channel_id=1, source_target_pairs={{0,8},{1,9},{2,10},{3,11},{4,12},{5,13},{6,14},{7,15},{8,0},{9,1},... | collective-permute-start | bytes 172040 | tf_op jit(solution)/shard_map/ppermute | solution.py:966
  12.8 2.6 %collective-permute-start.1 = (bf16[1,16,1792]{2,1,0:T(8,128)(2,1)S(1)}, bf16[1,16,1792]{2,1,0:T(8,128)(2,1)S(1)}, u32[]{:S(2)}, u32[]{:S(2)}) collective-permute-start(bf16[1,16,1792]{2,1,0:T(8,128)(2,1)S(1)} %bitcast.81), channel_id=1, source_target_pairs={{0,16},{1,17},{2,18},{3,19},{4,20},{5,21},{6,22},{7,23},{8,24},{9,... | collective-permute-start | bytes 172040 | tf_op jit(solution)/shard_map/ppermute | solution.py:966
  15.3 3.6 %collective-permute-done.1 = bf16[1,16,1792]{2,1,0:T(8,128)(2,1)S(1)} collective-permute-done((bf16[1,16,1792]{2,1,0:T(8,128)(2,1)S(1)}, bf16[1,16,1792]{2,1,0:T(8,128)(2,1)S(1)}, u32[]{:S(2)}, u32[]{:S(2)}) %collective-permute-start.1) | collective-permute-done | bytes 57376 | tf_op jit(solution)/shard_map/ppermute | solution.py:966
  18.9 2.4 collective-permute-done.2
  22.9 5.4 %collective-permute-done.3 = bf16[4,16,1792]{2,1,0:T(8,128)(2,1)S(1)} collective-permute-done((bf16[4,16,1792]{2,1,0:T(8,128)(2,1)S(1)}, bf16[4,16,1792]{2,1,0:T(8,128)(2,1)S(1)}, u32[]{:S(2)}, u32[]{:S(2)}) %collective-permute-start.3) | collective-permute-done | bytes 229408 | tf_op jit(solution)/shard_map/ppermute | solution.py:966
  30.0 8.1 %collective-permute-done.4 = bf16[8,16,1792]{2,1,0:T(8,128)(2,1)S(1)} collective-permute-done((bf16[8,16,1792]{2,1,0:T(8,128)(2,1)S(1)}, bf16[8,16,1792]{2,1,0:T(8,128)(2,1)S(1)}, u32[]{:S(2)}, u32[]{:S(2)}) %collective-permute-start.4) | collective-permute-done | bytes 458784 | tf_op jit(solution)/shard_map/ppermute | solution.py:966
  38.4 2.5 collective-permute-done.5.far_ref
  41.8 10.8 %project.1 = (bf16[4096,512]{1,0:T(8,128)(2,1)S(1)}, bf16[4096,512]{1,0:T(8,128)(2,1)S(1)}, bf16[4096,512]{1,0:T(8,128)(2,1)S(1)}, f32[128,512]{1,0:T(8,128)S(1)...) custom-call(s32[1]{0:T(128)} %bitcast.place, s32[1,4]{1,0:T(1,128)S(1)} %copy-done.20, bf16[4096,512]{1,0:T(8,128)(2,1)} %x_ref.5, ...), custom_call_target="tpu_custom_call" | custom-call | flops 6442450944 | bytes 16777216 | tf_op jit(solution)/shard_map/project/pallas_call | solution.py:147
  52.6 3.4 %sort_net.1 = (f32[1,128]{1,0:T(1,128)S(1)}, f32[16,128,128]{2,1,0:T(8,128)S(1)}) custom-call(s32[1,4]{1,0:T(1,128)S(1)} %copy-done.20, f32[128,512]{1,0:T(8,128)S(1)} %get-tuple-element.182.u_ref, bf16[512,1792]{1,0:T(8,128)(2,1)S(1)} %get-tuple-element.129.ws_ref.w_ref, s32[1,128]{1,0:T(1,128)S(1)} %copy-done.19), custom_call_target="tpu_custom_call" | custom-call | flops 100000000 | bytes 10000000 | tf_op jit(solution)/shard_map/sort_net/pallas_call | solution.py:232
  56.1 12.4 %attend.1 = (bf16[512,4096]{1,0:T(8,128)(2,1)}, bf16[4,2048,256]{2,1,0:T(8,128)(2,1)}) custom-call(s32[1,4]{1,0:T(1,128)S(1)} %copy-done.20, s32[1,128]{1,0:T(1,128)S(1)} %copy-done.19, f32[1,128]{1,0:T(1,128)S(1)} %get-tuple-element.130.bias, bf16[4096,512]{1,0:T(8,128)(2,1)S(1)} %get-tuple-element.166.q_ref, ...), custom_call_target="tpu_custom_call" | custom-call | flops 20000000000 | bytes 20971520 | tf_op jit(solution)/shard_map/attend/pallas_call | solution.py:419
  68.4 2.1 copy-done.21
  70.5 2.0 copy-done.22
  72.5 2.0 copy-done.23
  74.5 2.7 %all-gather.3.cloned.1.call-done = bf16[4608,512]{1,0:T(8,128)(2,1)} async-done(((bf16[144,512]{1,0:T(8,128)(2,1)}), bf16[4608,512]{1,0:T(8,128)(2,1)}) %all-gather.3.cloned.1.call-update) | async-done | bytes 4718608 | tf_op jit(solution)/shard_map/all_gather | solution.py:1039
  77.2 73.9 %ffn.1 = (bf16[4096,512]{1,0:T(8,128)(2,1)}, bf16[4096,512]{1,0:T(8,128)(2,1)}, bf16[4096,512]{1,0:T(8,128)(2,1)}, bf16[16,80,512]{2,1,0:T(8,128)(2,1)}, bf16[16...) custom-call(s32[1]{0:T(128)} %bitcast.place, ...), custom_call_target="tpu_custom_call" | custom-call | flops 57982058496 | bytes 29360128 | tf_op jit(solution)/shard_map/ffn/pallas_call | solution.py:687
  151.7 7.7 %attend_back.4 = (bf16[4096,128]{1,0:T(8,128)(2,1)S(1)}, bf16[4096,128]{1,0:T(8,128)(2,1)S(1)}, bf16[4096,128]{1,0:T(8,128)(2,1)S(1)}, f32[1,128]{1,0:T(1,128)S(1)}) custom-call(s32[1,128]{1,0:T(1,128)S(1)} %copy-done.19, bf16[4096,512]{1,0:T(8,128)(2,1)} %copy-done.21, bf16[4096,512]{1,0:T(8,128)(2,1)} %get-tuple-element.167.do_ref, ...), custom_call_target="tpu_custom_call" | custom-call | flops 10000000000 | bytes 8388608 | tf_op jit(solution)/shard_map/attend_back/pallas_call | solution.py:525
  165.3 7.5 %attend_back.6 = (bf16[4096,128]{1,0:T(8,128)(2,1)S(1)}, bf16[4096,128]{1,0:T(8,128)(2,1)S(1)}, bf16[4096,128]{1,0:T(8,128)(2,1)S(1)}, f32[1,128]{1,0:T(1,128)S(1)}) custom-call(s32[1,128]{1,0:T(1,128)S(1)} %copy-done.19, bf16[4096,512]{1,0:T(8,128)(2,1)} %copy-done.21, bf16[4096,512]{1,0:T(8,128)(2,1)} %get-tuple-element.167.do_ref, ...), custom_call_target="tpu_custom_call" | custom-call | flops 10000000000 | bytes 8388608 | tf_op jit(solution)/shard_map/attend_back/pallas_call | solution.py:525
  172.9 7.6 %attend_back.5 = (bf16[4096,128]{1,0:T(8,128)(2,1)S(1)}, bf16[4096,128]{1,0:T(8,128)(2,1)S(1)}, bf16[4096,128]{1,0:T(8,128)(2,1)S(1)}, f32[1,128]{1,0:T(1,128)S(1)}) custom-call(s32[1,128]{1,0:T(1,128)S(1)} %copy-done.19, bf16[4096,512]{1,0:T(8,128)(2,1)} %copy-done.21, bf16[4096,512]{1,0:T(8,128)(2,1)} %get-tuple-element.167.do_ref, ...), custom_call_target="tpu_custom_call" | custom-call | flops 10000000000 | bytes 8388608 | tf_op jit(solution)/shard_map/attend_back/pallas_call | solution.py:525
  183.0 7.5 %attend_back.7 = (bf16[4096,128]{1,0:T(8,128)(2,1)S(1)}, bf16[4096,128]{1,0:T(8,128)(2,1)S(1)}, bf16[4096,128]{1,0:T(8,128)(2,1)S(1)}, f32[1,128]{1,0:T(1,128)S(1)}) custom-call(s32[1,128]{1,0:T(1,128)S(1)} %copy-done.19, bf16[4096,512]{1,0:T(8,128)(2,1)} %copy-done.21, bf16[4096,512]{1,0:T(8,128)(2,1)} %get-tuple-element.167.do_ref, ...), custom_call_target="tpu_custom_call" | custom-call | flops 10000000000 | bytes 8388608 | tf_op jit(solution)/shard_map/attend_back/pallas_call | solution.py:525
  195.3 2.6 %sort_back.1 = (f32[128,512]{1,0:T(8,128)S(1)}, f32[512,128]{1,0:T(8,128)S(1)}) custom-call(s32[1,4]{1,0:T(1,128)S(1)} %copy-done.20, f32[128,512]{1,0:T(8,128)S(1)} %get-tuple-element.182.u_ref, bf16[512,1792]{1,0:T(8,128)(2,1)S(1)} %get-tuple-element.129.ws_ref.w_ref, s32[1,128]{1,0:T(1,128)S(1)} %copy-done.19, ...), custom_call_target="tpu_custom_call" | custom-call | flops 100000000 | bytes 10000000 | tf_op jit(solution)/shard_map/sort_back/pallas_call | solution.py:272
  197.9 21.0 %project_back.1 = (f32[4096,512]{1,0:T(8,128)}, bf16[16,16,896]{2,1,0:T(8,128)(2,1)S(1)}, bf16[16,16,896]{2,1,0:T(8,128)(2,1)S(1)}, f32[16,16,896]{2,1,0:T(8,128)S(1)}, f32[16,16,896]{2,1,0:T(8,128)S(1)}) custom-call(s32[1]{0:T(128)} %bitcast.place, s32[1,4]{1,0:T(1,128)S(1)} %copy-done.20, bf16[4096,512]{1,0:T(8,128)(2,1)} %x_ref.5, ...), custom_call_target="tpu_custom_call" | custom-call | flops 12884901888 | bytes 37748736 | tf_op jit(solution)/shard_map/project_back/pallas_call | solution.py:817
  223.1 5.5 %collective-permute-done.16 = bf16[8,16,896]{2,1,0:T(8,128)(2,1)S(1)} collective-permute-done((bf16[8,16,896]{2,1,0:T(8,128)(2,1)S(1)}, bf16[8,16,896]{2,1,0:T(8,128)(2,1)S(1)}, u32[]{:S(2)}, u32[]{:S(2)}) %collective-permute-start.16) | collective-permute-done | bytes 229408 | tf_op jit(solution)/shard_map/ppermute | solution.py:966
  231.1 2.7 %collective-permute-done.19 = bf16[4,16,896]{2,1,0:T(8,128)(2,1)S(1)} collective-permute-done((bf16[4,16,896]{2,1,0:T(8,128)(2,1)S(1)}, bf16[4,16,896]{2,1,0:T(8,128)(2,1)S(1)}, u32[]{:S(2)}, u32[]{:S(2)}) %collective-permute-start.19) | collective-permute-done | bytes 114720 | tf_op jit(solution)/shard_map/ppermute | solution.py:966
  239.9 2.3 collective-permute-done.22
  (116 shorter events, 36.4 us)
Async XLA Ops:
  7.2 70.0 %all-gather.3.cloned.1.call-start = ((), (), s32[]{:S(2)}) async-start(), calls=%async_computation | async-start | bytes 4866048 | tf_op jit(solution)/shard_map/all_gather | solution.py:1039
  9.7 5.7 %collective-permute-start = (bf16[1,16,1792]{2,1,0:T(8,128)(2,1)S(1)}, bf16[1,16,1792]{2,1,0:T(8,128)(2,1)S(1)}, u32[]{:S(2)}, u32[]{:S(2)}) collective-permute-start(bf16[1,16,1792]{2,1,0:T(8,128)(2,1)S(1)} %bitcast.80), channel_id=1, source_target_pairs={{0,8},{1,9},{2,10},{3,11},{4,12},{5,13},{6,14},{7,15},{8,0},{9,1},... | collective-permute-start | bytes 172040 | tf_op jit(solution)/shard_map/ppermute | solution.py:966
  12.8 6.2 %collective-permute-start.1 = (bf16[1,16,1792]{2,1,0:T(8,128)(2,1)S(1)}, bf16[1,16,1792]{2,1,0:T(8,128)(2,1)S(1)}, u32[]{:S(2)}, u32[]{:S(2)}) collective-permute-start(bf16[1,16,1792]{2,1,0:T(8,128)(2,1)S(1)} %bitcast.81), channel_id=1, source_target_pairs={{0,16},{1,17},{2,18},{3,19},{4,20},{5,21},{6,22},{7,23},{8,24},{9,... | collective-permute-start | bytes 172040 | tf_op jit(solution)/shard_map/ppermute | solution.py:966
  15.3 6.0 %collective-permute-start.2 = (bf16[1,16,1792]{2,1,0:T(8,128)(2,1)S(1)}, bf16[1,16,1792]{2,1,0:T(8,128)(2,1)S(1)}, u32[]{:S(2)}, u32[]{:S(2)}) collective-permute-start(bf16[1,16,1792]{2,1,0:T(8,128)(2,1)S(1)} %bitcast.82), channel_id=1, source_target_pairs={{0,24},{1,25},{2,26},{3,27},{4,28},{5,29},{6,30},{7,31},{8,16},{9,... | collective-permute-start | bytes 172040 | tf_op jit(solution)/shard_map/ppermute | solution.py:966
  21.4 7.0 %collective-permute-start.3 = (bf16[4,16,1792]{2,1,0:T(8,128)(2,1)S(1)}, bf16[4,16,1792]{2,1,0:T(8,128)(2,1)S(1)}, u32[]{:S(2)}, u32[]{:S(2)}) collective-permute-start(bf16[4,16,1792]{2,1,0:T(8,128)(2,1)S(1)} %get-tuple-element.259), channel_id=1, source_target_pairs={{0,4},{1,5},{2,6},{3,7},{4,0},{5,1},{6,2},{7,3},{8,12},{9,13},{10,... | collective-permute-start | bytes 688136 | tf_op jit(solution)/shard_map/ppermute | solution.py:966
  28.5 9.7 %collective-permute-start.4 = (bf16[8,16,1792]{2,1,0:T(8,128)(2,1)S(1)}, bf16[8,16,1792]{2,1,0:T(8,128)(2,1)S(1)}, u32[]{:S(2)}, u32[]{:S(2)}) collective-permute-start(bf16[8,16,1792]{2,1,0:T(8,128)(2,1)S(1)} %bitcast.94), channel_id=1, source_target_pairs={{0,2},{1,3},{2,0},{3,1},{4,6},{5,7},{6,4},{7,5},{8,10},{9,11},{10,... | collective-permute-start | bytes 1376264 | tf_op jit(solution)/shard_map/ppermute | solution.py:966
  38.4 2.5 %collective-permute-start.5 = (bf16[16,16,1792]{2,1,0:T(8,128)(2,1)S(1)}, bf16[16,16,1792]{2,1,0:T(8,128)(2,1)S(1)}, u32[]{:S(2)}, u32[]{:S(2)}) collective-permute-start(bf16[16,16,1792]{2,1,0:T(8,128)(2,1)S(1)} %bitcast.96), channel_id=1, source_target_pairs={{0,1},{1,0},{2,3},{3,2},{4,5},{5,4},{6,7},{7,6},{8,9},{9,8},{10,11... | collective-permute-start | bytes 2752520 | tf_op jit(solution)/shard_map/ppermute | solution.py:966
  151.2 8.3 %collective-permute-start.6 = (bf16[16,80,512]{2,1,0:T(8,128)(2,1)}, bf16[16,80,512]{2,1,0:T(8,128)(2,1)}, u32[]{:S(2)}, u32[]{:S(2)}) collective-permute-start(bf16[16,80,512]{2,1,0:T(8,128)(2,1)} %get-tuple-element.139), channel_id=1, source_target_pairs={{0,1},{1,0},{2,3},{3,2},{4,5},{5,4},{6,7},{7,6},{8,9},{9,8},{10,11... | collective-permute-start | bytes 3932168 | tf_op jit(solution)/shard_map/ppermute | solution.py:966
  151.4 8.0 %collective-permute-start.7 = (bf16[16,64,512]{2,1,0:T(8,128)(2,1)}, bf16[16,64,512]{2,1,0:T(8,128)(2,1)}, u32[]{:S(2)}, u32[]{:S(2)}) collective-permute-start(bf16[16,64,512]{2,1,0:T(8,128)(2,1)} %get-tuple-element.140), channel_id=1, source_target_pairs={{0,1},{1,0},{2,3},{3,2},{4,5},{5,4},{6,7},{7,6},{8,9},{9,8},{10,11... | collective-permute-start | bytes 3145736 | tf_op jit(solution)/shard_map/ppermute | solution.py:966
  163.3 17.2 %collective-permute-start.8 = (bf16[8,80,512]{2,1,0:T(8,128)(2,1)S(1)}, bf16[8,80,512]{2,1,0:T(8,128)(2,1)S(1)}, u32[]{:S(2)}, u32[]{:S(2)}) collective-permute-start(bf16[8,80,512]{2,1,0:T(8,128)(2,1)S(1)} %get-tuple-element.150), channel_id=1, source_target_pairs={{0,2},{1,3},{2,0},{3,1},{4,6},{5,7},{6,4},{7,5},{8,10},{9,11},{10,... | collective-permute-start | bytes 1966088 | tf_op jit(solution)/shard_map/ppermute | solution.py:966
  164.7 15.7 %collective-permute-start.9 = (bf16[8,64,512]{2,1,0:T(8,128)(2,1)S(1)}, bf16[8,64,512]{2,1,0:T(8,128)(2,1)S(1)}, u32[]{:S(2)}, u32[]{:S(2)}) collective-permute-start(bf16[8,64,512]{2,1,0:T(8,128)(2,1)S(1)} %get-tuple-element.151), channel_id=1, source_target_pairs={{0,4},{1,5},{2,6},{3,7},{4,0},{5,1},{6,2},{7,3},{8,12},{9,13},{10,... | collective-permute-start | bytes 1572872 | tf_op jit(solution)/shard_map/ppermute | solution.py:966
  180.9 9.7 %collective-permute-start.10 = (bf16[4,80,512]{2,1,0:T(8,128)(2,1)S(1)}, bf16[4,80,512]{2,1,0:T(8,128)(2,1)S(1)}, u32[]{:S(2)}, u32[]{:S(2)}) collective-permute-start(bf16[4,80,512]{2,1,0:T(8,128)(2,1)S(1)} %get-tuple-element.164), channel_id=1, source_target_pairs={{0,4},{1,5},{2,6},{3,7},{4,0},{5,1},{6,2},{7,3},{8,12},{9,13},{10,... | collective-permute-start | bytes 983048 | tf_op jit(solution)/shard_map/ppermute | solution.py:966
  182.4 8.2 %collective-permute-start.11 = (bf16[4,64,512]{2,1,0:T(8,128)(2,1)S(1)}, bf16[4,64,512]{2,1,0:T(8,128)(2,1)S(1)}, u32[]{:S(2)}, u32[]{:S(2)}) collective-permute-start(bf16[4,64,512]{2,1,0:T(8,128)(2,1)S(1)} %get-tuple-element.165), channel_id=1, source_target_pairs={{0,2},{1,3},{2,0},{3,1},{4,6},{5,7},{6,4},{7,5},{8,10},{9,11},{10,... | collective-permute-start | bytes 786440 | tf_op jit(solution)/shard_map/ppermute | solution.py:966
  190.9 28.1 %collective-permute-start.12 = (bf16[1,144,512]{2,1,0:T(8,128)(2,1)S(1)}, bf16[1,144,512]{2,1,0:T(8,128)(2,1)S(1)}, u32[]{:S(2)}, u32[]{:S(2)}) collective-permute-start(bf16[1,144,512]{2,1,0:T(8,128)(2,1)S(1)} %get-tuple-element.178), channel_id=1, source_target_pairs={{0,8},{1,9},{2,10},{3,11},{4,12},{5,13},{6,14},{7,15},{8,0},{9,1},... | collective-permute-start | bytes 442376 | tf_op jit(solution)/shard_map/ppermute | solution.py:966
  192.7 26.2 %collective-permute-start.13 = (bf16[1,144,512]{2,1,0:T(8,128)(2,1)S(1)}, bf16[1,144,512]{2,1,0:T(8,128)(2,1)S(1)}, u32[]{:S(2)}, u32[]{:S(2)}) collective-permute-start(bf16[1,144,512]{2,1,0:T(8,128)(2,1)S(1)} %get-tuple-element.179), channel_id=1, source_target_pairs={{0,16},{1,17},{2,18},{3,19},{4,20},{5,21},{6,22},{7,23},{8,24},{9,... | collective-permute-start | bytes 442376 | tf_op jit(solution)/shard_map/ppermute | solution.py:966
  193.6 25.3 %collective-permute-start.14 = (bf16[1,144,512]{2,1,0:T(8,128)(2,1)S(1)}, bf16[1,144,512]{2,1,0:T(8,128)(2,1)S(1)}, u32[]{:S(2)}, u32[]{:S(2)}) collective-permute-start(bf16[1,144,512]{2,1,0:T(8,128)(2,1)S(1)} %get-tuple-element.180), channel_id=1, source_target_pairs={{0,24},{1,25},{2,26},{3,27},{4,28},{5,29},{6,30},{7,31},{8,16},{9,... | collective-permute-start | bytes 442376 | tf_op jit(solution)/shard_map/ppermute | solution.py:966
  219.0 3.3 %collective-permute-start.17 = (bf16[16,16,896]{2,1,0:T(8,128)(2,1)S(1)}, bf16[16,16,896]{2,1,0:T(8,128)(2,1)S(1)}, u32[]{:S(2)}, u32[]{:S(2)}) collective-permute-start(bf16[16,16,896]{2,1,0:T(8,128)(2,1)S(1)} %get-tuple-element.212), channel_id=1, source_target_pairs={{0,1},{1,0},{2,3},{3,2},{4,5},{5,4},{6,7},{7,6},{8,9},{9,8},{10,11... | collective-permute-start | bytes 1376264 | tf_op jit(solution)/shard_map/ppermute | solution.py:966
  220.9 7.7 %collective-permute-start.16 = (bf16[8,16,896]{2,1,0:T(8,128)(2,1)S(1)}, bf16[8,16,896]{2,1,0:T(8,128)(2,1)S(1)}, u32[]{:S(2)}, u32[]{:S(2)}) collective-permute-start(bf16[8,16,896]{2,1,0:T(8,128)(2,1)S(1)} %get-tuple-element.248), channel_id=1, source_target_pairs={{0,2},{1,3},{2,0},{3,1},{4,6},{5,7},{6,4},{7,5},{8,10},{9,11},{10,... | collective-permute-start | bytes 688136 | tf_op jit(solution)/shard_map/ppermute | solution.py:966
  222.4 8.0 %collective-permute-start.18 = (bf16[8,16,896]{2,1,0:T(8,128)(2,1)S(1)}, bf16[8,16,896]{2,1,0:T(8,128)(2,1)S(1)}, u32[]{:S(2)}, u32[]{:S(2)}) collective-permute-start(bf16[8,16,896]{2,1,0:T(8,128)(2,1)S(1)} %get-tuple-element.246), channel_id=1, source_target_pairs={{0,4},{1,5},{2,6},{3,7},{4,0},{5,1},{6,2},{7,3},{8,12},{9,13},{10,... | collective-permute-start | bytes 688136 | tf_op jit(solution)/shard_map/ppermute | solution.py:966
  228.9 4.9 %collective-permute-start.19 = (bf16[4,16,896]{2,1,0:T(8,128)(2,1)S(1)}, bf16[4,16,896]{2,1,0:T(8,128)(2,1)S(1)}, u32[]{:S(2)}, u32[]{:S(2)}) collective-permute-start(bf16[4,16,896]{2,1,0:T(8,128)(2,1)S(1)} %get-tuple-element.256), channel_id=1, source_target_pairs={{0,4},{1,5},{2,6},{3,7},{4,0},{5,1},{6,2},{7,3},{8,12},{9,13},{10,... | collective-permute-start | bytes 344072 | tf_op jit(solution)/shard_map/ppermute | solution.py:966
  230.5 4.9 %collective-permute-start.20 = (bf16[4,16,896]{2,1,0:T(8,128)(2,1)S(1)}, bf16[4,16,896]{2,1,0:T(8,128)(2,1)S(1)}, u32[]{:S(2)}, u32[]{:S(2)}) collective-permute-start(bf16[4,16,896]{2,1,0:T(8,128)(2,1)S(1)} %get-tuple-element.254), channel_id=1, source_target_pairs={{0,2},{1,3},{2,0},{3,1},{4,6},{5,7},{6,4},{7,5},{8,10},{9,11},{10,... | collective-permute-start | bytes 344072 | tf_op jit(solution)/shard_map/ppermute | solution.py:966
  235.5 4.5 %collective-permute-start.21 = (bf16[1,16,1792]{2,1,0:T(8,128)(2,1)S(1)}, bf16[1,16,1792]{2,1,0:T(8,128)(2,1)S(1)}, u32[]{:S(2)}, u32[]{:S(2)}) collective-permute-start(bf16[1,16,1792]{2,1,0:T(8,128)(2,1)S(1)} %get-tuple-element.252), channel_id=1, source_target_pairs={{0,8},{1,9},{2,10},{3,11},{4,12},{5,13},{6,14},{7,15},{8,0},{9,1},... | collective-permute-start | bytes 172040 | tf_op jit(solution)/shard_map/ppermute | solution.py:966
  236.5 5.7 %collective-permute-start.22 = (bf16[1,16,1792]{2,1,0:T(8,128)(2,1)S(1)}, bf16[1,16,1792]{2,1,0:T(8,128)(2,1)S(1)}, u32[]{:S(2)}, u32[]{:S(2)}) collective-permute-start(bf16[1,16,1792]{2,1,0:T(8,128)(2,1)S(1)} %get-tuple-element.253), channel_id=1, source_target_pairs={{0,16},{1,17},{2,18},{3,19},{4,20},{5,21},{6,22},{7,23},{8,24},{9,... | collective-permute-start | bytes 172040 | tf_op jit(solution)/shard_map/ppermute | solution.py:966
  238.2 6.0 %collective-permute-start.23 = (bf16[1,16,1792]{2,1,0:T(8,128)(2,1)S(1)}, bf16[1,16,1792]{2,1,0:T(8,128)(2,1)S(1)}, u32[]{:S(2)}, u32[]{:S(2)}) collective-permute-start(bf16[1,16,1792]{2,1,0:T(8,128)(2,1)S(1)} %get-tuple-element.250), channel_id=1, source_target_pairs={{0,24},{1,25},{2,26},{3,27},{4,28},{5,29},{6,30},{7,31},{8,16},{9,... | collective-permute-start | bytes 172040 | tf_op jit(solution)/shard_map/ppermute | solution.py:966
  (30 other events, 316.8 us)
Sparse Core Ops, SparseCore 0:
  10.9 66.2 all-gather.2
